TPU v7x, 128 devices: a whole 4x4x4 slice. The times are simulated.
128 devices in a mesh: dp: 4 (over y), mp: 32 (over z, x, core).
Axes of the slice: x: 4, y: 4, z: 4, core: 2. Of those that a mesh axis runs over, the one named last changes fastest.
Arguments:
- queries: bfloat16 [32, 48, 2048], P('dp'), may hold values from -3 to 3
- new_keys: bfloat16 [32, 48, 2048], P('dp'), may hold values from -3 to 3
- new_values: bfloat16 [32, 48, 2048], P('dp'), may hold values from -6 to 6
- cache_keys: bfloat16 [32, 4096, 2048], P('dp', 'mp'), may hold values from -3 to 3
- cache_values: bfloat16 [32, 4096, 2048], P('dp', 'mp'), may hold values from -6 to 6
- lengths: int32 [32], P('dp'), may hold values from 64 to 4096, as said below
- parents: int32 [32, 48], P('dp'), may hold values from 0 to 46, as said below
- tree_tokens: int32 [32, 48], P('dp'), may hold values from 0 to 77823
- residual: bfloat16 [32, 48, 2048], P('dp'), may hold values from -6 to 6
- out_weight: bfloat16 [2048, 2048], P(('dp', 'mp')), may hold values from -0.125 to 0.125
- norm_gain: float32 [2048], replicated, may hold values from 0.25 to 1.75
- vocab_weight: bfloat16 [2048, 77824], P(None, 'mp'), may hold values from -0.375 to 0.375
Outputs:
- hidden: bfloat16 [32, 48, 2048], P('dp')
- node_logprob: float32 [32, 48], P('dp')
Inputs may be any that keep to these rules, and one draw needn't show every extreme that they name: `lengths`: A request's cache length is 4096 or lies between 64 and 512; some request has length 4096 in every draw. parents[r, 0] is 0; for j > 0, parents[r, j] is j - 2 or j - 1 (0 for j = 1); some request's last node has parent 48 - 2 in every draw.
All inputs are finite; a program needn't handle non-finite values.
Results may differ from a plain program's by a relative error of at most 0.007.
Values may be sent and summed in bfloat16 or wider, within the bound.
No kernel may reach another device: no remote copies, remote signals or barrier semaphores. Data moves between devices by JAX's collectives and lax.ppermute only.
A program may use at most 128 MiB of HBM per device.

v0:
```python
import jax
import jax.numpy as jnp
from jax import lax
from jax.sharding import PartitionSpec as P

HEADS = 16
SINK = 4


def ancestor_mask(parents):
    tree = parents.shape[-1]
    idx = jnp.arange(tree, dtype=jnp.int32)
    links = (
        (idx[None, :, None] == idx[None, None, :]) | (parents[:, :, None] == idx[None, None, :])
    ).astype(jnp.float32)
    for _ in range((tree - 1).bit_length()):
        links = jnp.minimum(
            jnp.einsum("rij,rjk->rik", links, links, precision=lax.Precision.HIGHEST), 1.0
        )
    return links > 0.5


def local(
    queries,
    new_keys,
    new_values,
    cache_keys,
    cache_values,
    lengths,
    parents,
    tree_tokens,
    residual,
    out_weight,
    norm_gain,
    vocab_weight,
):
    reqs, tree, width = queries.shape
    slots = cache_keys.shape[1]
    head_dim = width // HEADS
    scale = head_dim ** (-0.5)
    shard = lax.axis_index("mp")
    shards = lax.axis_size("mp")
    tokens = reqs * tree
    window = slots * shards // 2
    positions = shard * slots + jnp.arange(slots, dtype=jnp.int32)
    visible = (positions[None, :] < lengths[:, None]) & (
        (positions[None, :] < SINK) | (positions[None, :] >= lengths[:, None] - window)
    )
    q4 = queries.reshape(reqs, tree, HEADS, head_dim)
    k4 = cache_keys.reshape(reqs, slots, HEADS, head_dim)
    v4 = cache_values.reshape(reqs, slots, HEADS, head_dim)
    cache_e = jnp.where(
        visible[:, None, None, :],
        jnp.exp(jnp.einsum("rihd,rshd->rhis", q4, k4, preferred_element_type=jnp.float32) * scale),
        0.0,
    )
    cache_den = jnp.sum(cache_e, -1)
    cache_num = jnp.einsum(
        "rhis,rshd->rihd", cache_e.astype(jnp.bfloat16), v4, preferred_element_type=jnp.float32
    )
    ancestors = ancestor_mask(parents)
    nk4 = new_keys.reshape(reqs, tree, HEADS, head_dim)
    nv4 = new_values.reshape(reqs, tree, HEADS, head_dim)
    tree_e = jnp.where(
        ancestors[:, None],
        jnp.exp(jnp.einsum("rihd,rjhd->rhij", q4, nk4, preferred_element_type=jnp.float32) * scale),
        0.0,
    )
    tree_den = jnp.sum(tree_e, -1)
    tree_num = jnp.einsum(
        "rhij,rjhd->rihd", tree_e.astype(jnp.bfloat16), nv4, preferred_element_type=jnp.float32
    )
    flat_res = residual.reshape(tokens, width)
    num_all, den_all = lax.psum((cache_num.reshape(tokens, width), cache_den), "mp")
    denom = jnp.transpose(den_all + tree_den, (0, 2, 1))
    numer = num_all.reshape(reqs, tree, HEADS, head_dim) + tree_num
    attended = (numer / denom[..., None]).astype(jnp.bfloat16).reshape(tokens, width)
    projected = jnp.dot(
        attended,
        lax.all_gather(out_weight, ("dp", "mp"), axis=0, tiled=True),
        preferred_element_type=jnp.float32,
    )
    hidden = (flat_res.astype(jnp.float32) + projected).astype(jnp.bfloat16)
    hfloat = hidden.astype(jnp.float32)
    normed = (
        hfloat * lax.rsqrt(jnp.mean(hfloat * hfloat, -1, keepdims=True) + 1e-06) * norm_gain
    ).astype(jnp.bfloat16)
    vocab_dev = vocab_weight.shape[1]
    logits = jnp.dot(normed, vocab_weight, preferred_element_type=jnp.float32)
    exp_sums = jnp.sum(jnp.exp(logits), -1)
    parent_rows = (jnp.arange(reqs, dtype=jnp.int32)[:, None] * tree + parents).reshape(-1)
    column = tree_tokens.reshape(-1) - shard * vocab_dev
    inside = (column >= 0) & (column < vocab_dev)
    picked = jnp.where(inside, logits[parent_rows, jnp.clip(column, 0, vocab_dev - 1)], 0.0)
    parent_sums = exp_sums[parent_rows]
    total_sums, total_picked = lax.psum((parent_sums, picked), "mp")
    node_logprob = (total_picked - jnp.log(total_sums)).reshape(reqs, tree)
    return (hidden.reshape(reqs, tree, width), node_logprob)


def solution(mesh):
    placed = (
        P("dp", None, None),
        P("dp", None, None),
        P("dp", None, None),
        P("dp", "mp", None),
        P("dp", "mp", None),
        P("dp"),
        P("dp", None),
        P("dp", None),
        P("dp", None, None),
        P(("dp", "mp"), None),
        P(),
        P(None, "mp"),
    )
    return jax.shard_map(
        local,
        mesh=mesh,
        in_specs=placed,
        out_specs=(P("dp", None, None), P("dp", None)),
        check_vma=False,
    )
```

profile of v0, /device:TPU:1, one launch (start us, length us, event | category | flops | bytes accessed | tf_op | source)
XLA Modules:
  0.0 258.8 jit_solution(10555622454966664763)
XLA Ops:
  8.0 0.0 all-reduce.3.cloned.1.call-start
  8.1 0.8 broadcast_add_fusion.1
  8.9 0.7 or_and_fusion
  9.6 5.4 %fusion.12 = (f32[8,16,48]{2,1,0:T(8,128)S(1)}, f32[8,16,48,128]{3,2,1,0:T(8,128)S(1)}) fusion(pred[8,128]{1,0:T(8,128)(4,1)S(1)} %or_and_fusion, bf16[8,128,2048]{2,1,0:T(8,128)(2,1)} %param.15, bf16[8,48,2048]{2,1,0:T(8,128)(2,1)S(1)} %copy-done), kind=kOutput, calls=%fused_computation.21 | convolution fusion | flops 203679744 | bytes 8938496 | tf_op jit(solution)/shard_map/rihd,rshd->rhis/dot_general | solution.py:54
  15.1 3.0 %fusion.16 = f32[8,48,16,128]{3,1,2,0:T(8,128)} fusion(f32[8,16,48,128]{3,2,1,0:T(8,128)S(1)} %get-tuple-element.7, pred[8,128]{1,0:T(8,128)(4,1)S(1)} %or_and_fusion, bf16[8,128,2048]{2,1,0:T(8,128)(2,1)S(1)} %copy-done.1), kind=kOutput, calls=%fused_computation.25 | convolution fusion | flops 203685888 | bytes 10486784 | tf_op jit(solution)/shard_map/rhis,rshd->rihd/dot_general | solution.py:58
  18.0 0.0 all-reduce.3.cloned.1.call-update
  18.1 0.0 all-gather.2.cloned.1.call-start
  18.1 0.5 all-gather.2.cloned.1.call-update
  18.7 0.1 copy-done.3
  18.7 0.3 convolution_minimum_fusion.5
  19.0 0.3 convolution_minimum_fusion.4
  19.3 0.3 convolution_minimum_fusion.3
  19.7 0.3 convolution_minimum_fusion.2
  20.0 0.3 convolution_minimum_fusion.1
  20.3 0.3 fusion.42
  20.6 0.1 copy.25
  20.8 0.1 min.36
  20.9 0.1 broadcast_add_fusion
  21.0 0.1 reshape.212
  21.1 0.1 and.16
  21.2 126.5 %psum.29 = f32[8,16,48]{2,1,0:T(8,128)S(1)} all-reduce(f32[8,16,48]{2,1,0:T(8,128)S(1)} %get-tuple-element.6), channel_id=1, replica_groups=mesh['dp'=4,'mp'=32] {'mp'}, use_global_device_ids=true, to_apply=%region_2.3 | all-reduce | flops 6144 | bytes 49152 | tf_op jit(solution)/shard_map/psum | solution.py:74
  147.7 2.7 %fusion.14 = (f32[8,16,48]{2,1,0:T(8,128)S(1)}, f32[8,16,48,48]{2,3,1,0:T(8,128)}) fusion(pred[8,48,48]{1,2,0:T(8,128)(4,1)S(1)} %copy.25, bf16[8,48,2048]{2,1,0:T(8,128)(2,1)S(1)} %copy-done.4, bf16[8,48,2048]{2,1,0:T(8,128)(2,1)S(1)} %copy-done), kind=kOutput, calls=%fused_computation.23 | convolution fusion | flops 76376064 | bytes 4368384 | tf_op jit(solution)/shard_map/rihd,rjhd->rhij/dot_general | solution.py:66
  150.4 0.0 all-reduce.3.cloned.1.call-done
  150.5 4.9 %fusion.11 = bf16[8,48,16,128]{3,1,2,0:T(8,128)(2,1)S(1)} fusion(f32[8,48,16,128]{3,1,2,0:T(8,128)} %all-reduce.3.cloned.1.call-done, f32[8,16,48,48]{2,3,1,0:T(8,128)} %get-tuple-element.9, f32[8,48,16]{1,2,0:T(8,128)S(1)} %add_bitcast_fusion, pred[8,48,48]{1,2,0:T(8,128)(4,1)S(1)} %copy.25, bf16[8,48,2048]{2,1,0:T(8,128)(2,1)} %param.14), kind=kOutput, calls=%fused_computation.18 | convolution fusion | flops 78741504 | bytes 7514112 | tf_op jit(solution)/shard_map/rhij,rjhd->rihd/dot_general | solution.py:70
  155.4 0.4 copy.30
  155.8 0.0 all-gather.2.cloned.1.call-done
  155.9 7.4 %fusion.6 = (f32[384]{0:T(512)S(1)}, bf16[384,2048]{1,0:T(8,128)(2,1)S(1)}) fusion(bf16[2048,2048]{1,0:T(8,128)(2,1)} %all-gather.2.cloned.1.call-done, bf16[48,8,16,128]{3,2,1,0:T(8,128)(2,1)S(1)} %bitcast.82, bf16[384,2048]{1,0:T(8,128)(2,1)} %bitcast.83), kind=kOutput, calls=%fused_computation.11 | convolution fusion | flops 3225943552 | bytes 13108736 | tf_op jit(solution)/shard_map/dot_general | solution.py:78
  163.3 10.5 %exponential_reduce_fusion = (f32[384]{0:T(512)S(1)}, f32[384,2432]{1,0:T(8,128)}) fusion(bf16[2048,2432]{1,0:T(8,128)(2,1)} %param.23, bf16[384,2048]{1,0:T(8,128)(2,1)S(1)} %get-tuple-element.11, f32[2048]{0:T(1024)S(1)} %copy-done.5, f32[384]{0:T(512)S(1)} %add_rsqrt_fusion), kind=kOutput, calls=%fused_computation.10 | convolution fusion | flops 3829284352 | bytes 15281152 | tf_op jit(solution)/shard_map/dot_general | solution.py:89
  173.8 6.4 %gather_fusion = f32[384]{0:T(512)S(1)} fusion(f32[384,2432]{1,0:T(8,128)} %get-tuple-element.13, s32[384]{0:T(512)S(1)} %get-tuple-element.3), kind=kCustom, calls=%fused_computation | custom fusion | bytes 6144 | tf_op jit(solution)/shard_map/gather | solution.py:94
  180.1 2.8 %gather_fusion.1 = f32[384]{0:T(512)S(1)} fusion(f32[384]{0:T(512)S(1)} %get-tuple-element.12, s32[1024]{0:T(1024)S(1)} %pad_clamp_fusion), kind=kCustom, calls=%fused_computation.1 | custom fusion | bytes 4608 | tf_op jit(solution)/shard_map/gather | solution.py:95
  182.9 67.7 %all-reduce = (f32[384]{0:T(512)S(1)}, f32[384]{0:T(512)S(1)}) all-reduce(f32[384]{0:T(512)S(1)} %broadcast_select_fusion, f32[384]{0:T(512)S(1)} %gather_fusion.1), channel_id=1, replica_groups=mesh['dp'=4,'mp'=32] {'mp'}, use_global_device_ids=true, to_apply=%region_5.6 | all-reduce | flops 768 | bytes 6144 | tf_op jit(solution)/shard_map/psum | solution.py:96
  250.7 0.7 reshape.213
  (25 shorter events, 0.1 us)
Async XLA Ops:
  8.0 1.6 copy-start
  8.0 142.4 %all-reduce.3.cloned.1.call-start = ((), (), s32[]{:S(2)}) async-start(), calls=%async_computation | async-start | bytes 6291456 | tf_op jit(solution)/shard_map/psum | solution.py:74
  9.6 5.5 %copy-start.1 = (bf16[8,128,2048]{2,1,0:T(8,128)(2,1)S(1)}, bf16[8,128,2048]{2,1,0:T(8,128)(2,1)}, u32[]{:S(2)}) copy-start(bf16[8,128,2048]{2,1,0:T(8,128)(2,1)} %param.16) | copy-start | bytes 12582916
  18.0 0.7 copy-start.3
  18.0 2.8 %copy-start.2 = (s32[8,48]{1,0:T(8,128)S(1)}, s32[8,48]{1,0:T(8,128)}, u32[]{:S(2)}) copy-start(s32[8,48]{1,0:T(8,128)} %param.19) | copy-start | bytes 4612
  18.0 129.6 %copy-start.4 = (bf16[8,48,2048]{2,1,0:T(8,128)(2,1)S(1)}, bf16[8,48,2048]{2,1,0:T(8,128)(2,1)}, u32[]{:S(2)}) copy-start(bf16[8,48,2048]{2,1,0:T(8,128)(2,1)} %param.13) | copy-start | bytes 4718596
  18.1 137.8 %all-gather.2.cloned.1.call-start = ((), (), s32[]{:S(2)}) async-start(), calls=%async_computation.1 | async-start | bytes 8454144 | tf_op jit(solution)/shard_map/all_gather | solution.py:80
  155.9 7.4 %copy-start.5 = (f32[2048]{0:T(1024)S(1)}, f32[2048]{0:T(1024)}, u32[]{:S(2)}) copy-start(f32[2048]{0:T(1024)} %param.22) | copy-start | bytes 24580
  163.3 10.5 %copy-start.6 = (bf16[384,2048]{1,0:T(8,128)(2,1)}, bf16[384,2048]{1,0:T(8,128)(2,1)S(1)}, u32[]{:S(2)}) copy-start(bf16[384,2048]{1,0:T(8,128)(2,1)S(1)} %get-tuple-element.11) | copy-start | bytes 4718596
Sparse Core Ops, SparseCore 0:
  18.2 114.0 all-reduce.2
Sparse Core Ops, SparseCore 1:
  21.5 74.3 all-gather.1
where the time goes:
time: 259 us
  blocking collectives  194 us (75%)
  matrix products  35.8 us (14%)
  between operations  15.7 us (6%)
  local copies, waits for them, and re-layouts  10.7 us (4%)
    psum x1, blocking collectives, local(): lax.psum((cache_num.reshape(tokens, width), cache_den), 'mp')  126 us
    psum x1, blocking collectives, local(): total_sums, total_picked = lax.psum((parent_sums, picked), 'mp')  67.7 us
    dot_general x1, matrix products, local(): logits = jnp.dot(normed, vocab_weight, preferred_element_type=jnp.float32)  10.5 us
    dot_general x1, matrix products, local(): jnp.dot(attended, lax.all_gather(out_weight, ('dp', 'mp'), axis=0, tiled=...  7.39 us
    gather x1, local copies, waits for them, and re-layouts, local(): logits[parent_rows, jnp.clip(column, 0, vocab_dev - 1)]  6.35 us
    dot_general x1, matrix products, local(): jnp.einsum('rihd,rshd->rhis', q4, k4, preferred_element_type=jnp.float32)  5.44 us
  transfers between devices with their start and end apart: 2, of which 0 were waited for; matrix products, arithmetic and copies ran while one was open for 4% of the time, Pallas kernels for 0%

commit v1 on v0

v1 whole, which is shorter than its diff:
```python
import functools

import jax
import jax.numpy as jnp
from jax import lax
from jax.experimental import pallas as pl
from jax.experimental.pallas import tpu as pltpu
from jax.sharding import Mesh, PartitionSpec as P

HEADS = 16
SINK = 4
BF = jnp.bfloat16
F32 = jnp.float32
NT = (((1,), (1,)), ((), ()))
MB = 1 << 20


def attend_kernel(window, lane_off, info_ref, len_ref, par_ref, q_ref, k_ref, v_ref, nk_ref, nv_ref, out_ref, anc_ref):
    r = pl.program_id(0)
    first = info_ref[1]
    treq = info_ref[2]
    length = len_ref[r]
    tree, width = q_ref.shape[1], q_ref.shape[2]
    slots = k_ref.shape[1]
    heads = width // 128
    scale = 128 ** (-0.5)
    lane = lax.broadcasted_iota(jnp.int32, (tree, 128), 1)
    seen = (first < length) & ((first < SINK) | (first + slots - 1 >= length - window))
    is_tree = r == treq

    def attend(keys_ref, values_ref, mask):
        dens = jnp.zeros((tree, 128), F32)
        for h in range(heads):
            cols = slice(h * 128, (h + 1) * 128)
            s = lax.dot_general(q_ref[0, :, cols], keys_ref[0, :, cols], NT, preferred_element_type=F32)
            e = jnp.where(mask, jnp.exp(s * scale), 0.0)
            den = jnp.sum(e, axis=1, keepdims=True)
            dens = jnp.where((lane == lane_off + h) | (lane == lane_off + heads + h), den, dens)
            o = jnp.dot(e.astype(BF), values_ref[0, :, cols], preferred_element_type=F32)
            out_ref[0, :, cols] = o.astype(BF)
        high = dens.astype(BF).astype(F32)
        part = jnp.where(lane < lane_off + heads, high, dens - high)
        out_ref[0, :, width:] = part.astype(BF)

    @pl.when(jnp.logical_not(seen | is_tree))
    def _():
        out_ref[...] = jnp.zeros_like(out_ref)

    @pl.when(seen)
    def _():
        pos = first + lax.broadcasted_iota(jnp.int32, (tree, slots), 1)
        mask = (pos < length) & ((pos < SINK) | (pos >= length - window))
        attend(k_ref, v_ref, mask)

    @pl.when(is_tree)
    def _():
        node = lax.broadcasted_iota(jnp.int32, (1, tree), 1)
        anc_ref[0:1, :] = jnp.where(node == 0, 1.0, 0.0)

        def body(i, carry):
            up = anc_ref[pl.ds(par_ref[r, i], 1), :]
            anc_ref[pl.ds(i, 1), :] = jnp.where(node == i, 1.0, up)
            return carry

        lax.fori_loop(1, tree, body, 0)
        attend(nk_ref, nv_ref, anc_ref[...] > 0.5)


def attend_half(window, lane_off, info, lengths, parents, q, k, v, nk, nv):
    reqs, tree, width = q.shape
    slots = k.shape[1]
    half = width // 2
    qs = pl.BlockSpec((1, tree, half), lambda r, i, l, p: (r, 0, i[0]))
    ks = pl.BlockSpec((1, slots, half), lambda r, i, l, p: (r, 0, i[0]))
    ns = pl.BlockSpec((1, tree, half), lambda r, i, l, p: (jnp.clip(i[2], 0, reqs - 1), 0, i[0]))
    return pl.pallas_call(
        functools.partial(attend_kernel, window, lane_off),
        out_shape=jax.ShapeDtypeStruct((reqs, tree, half + 128), BF),
        grid_spec=pltpu.PrefetchScalarGridSpec(
            num_scalar_prefetch=3,
            grid=(reqs,),
            in_specs=[qs, ks, ks, ns, ns],
            out_specs=pl.BlockSpec((1, tree, half + 128), lambda r, i, l, p: (r, 0, 0)),
            scratch_shapes=[pltpu.VMEM((tree, tree), F32)],
        ),
        compiler_params=pltpu.CompilerParams(vmem_limit_bytes=48 * MB),
        name="attend",
    )(info, lengths, parents, q, k, v, nk, nv)


def combine_kernel(parts_ref, out_ref):
    width = out_ref.shape[2]
    heads = width // 128
    total = jnp.sum(parts_ref[...].astype(F32), axis=0)
    den = total[:, width:]
    lane = lax.broadcasted_iota(jnp.int32, den.shape, 1)
    for h in range(heads):
        d = jnp.sum(jnp.where((lane % heads == h) & (lane < 4 * heads), den, 0.0), axis=1, keepdims=True)
        cols = slice(h * 128, (h + 1) * 128)
        val = (total[:, cols] / d).astype(BF)
        for c in range(out_ref.shape[0]):
            out_ref[c, :, cols] = val


def combine(parts, copies):
    rows, cols = parts.shape[1], parts.shape[2]
    return pl.pallas_call(
        combine_kernel,
        out_shape=jax.ShapeDtypeStruct((copies, rows, cols - 128), BF),
        compiler_params=pltpu.CompilerParams(vmem_limit_bytes=48 * MB),
        name="combine",
    )(parts)


def project_kernel(info_ref, att_ref, w_ref, res_ref, out_ref):
    nx, nc, rows, half = att_ref.shape
    acc = res_ref[...].astype(F32).reshape(nx * rows, res_ref.shape[2])
    for c in range(nc):
        a = jnp.concatenate([att_ref[x, c] for x in range(nx)], axis=0)
        acc = acc + jnp.dot(a, w_ref[c * half:(c + 1) * half, :], preferred_element_type=F32)
    hid = acc.astype(BF)
    for i in range(out_ref.shape[0]):
        out_ref[i] = hid


def project(info, att, w, residual, copies):
    nx, nc, rows, half = att.shape
    tree = residual.shape[1]
    reqs = nx * rows // tree
    cols = w.shape[1]
    return pl.pallas_call(
        project_kernel,
        out_shape=jax.ShapeDtypeStruct((copies, nx * rows, cols), BF),
        grid_spec=pltpu.PrefetchScalarGridSpec(
            num_scalar_prefetch=1,
            grid=(1,),
            in_specs=[
                pl.BlockSpec(att.shape, lambda g, i: (0, 0, 0, 0)),
                pl.BlockSpec(w.shape, lambda g, i: (0, 0)),
                pl.BlockSpec((reqs, tree, cols), lambda g, i: (i[0], 0, i[1])),
            ],
            out_specs=pl.BlockSpec((copies, nx * rows, cols), lambda g, i: (0, 0, 0)),
        ),
        compiler_params=pltpu.CompilerParams(vmem_limit_bytes=48 * MB),
        name="project",
    )(info, att, w, residual)


def vocab_kernel(tree, chunks, info_ref, mine_ref, theirs_ref, gain_ref, tok_ref, w_ref, hid_ref, stat_ref, x_ref, wbuf_ref, sem):
    copies = []
    for i, (start, size) in enumerate(chunks):
        cp = pltpu.make_async_copy(w_ref.at[:, pl.ds(start, size)], wbuf_ref.at[:, pl.ds(start, size)], sem.at[i])
        cp.start()
        copies.append(cp)
    core = info_ref[0]
    nz, nx, rows, cols = mine_ref.shape
    half = nx * cols
    for z in range(nz):
        rs = slice(z * rows, (z + 1) * rows)
        squares = jnp.zeros((rows, cols), F32)
        for x in range(nx):
            mine, theirs = mine_ref[z, x], theirs_ref[z, x]
            low = jnp.where(core == 0, mine, theirs)
            high = jnp.where(core == 0, theirs, mine)
            hid_ref[rs, x * cols:(x + 1) * cols] = low
            hid_ref[rs, half + x * cols:half + (x + 1) * cols] = high
            squares = squares + low.astype(F32) * low.astype(F32) + high.astype(F32) * high.astype(F32)
        inv = lax.rsqrt(jnp.sum(squares, axis=1, keepdims=True) / (2 * half) + 1e-06)
        for j in range(2 * nx):
            cs = slice(j * cols, (j + 1) * cols)
            x_ref[rs, cs] = (hid_ref[rs, cs].astype(F32) * inv * gain_ref[:, cs]).astype(BF)
    tokens = nz * rows
    reqs = tokens // tree
    sums = jnp.zeros((tokens, 128), F32)
    pick1 = jnp.zeros((tokens, 128), F32)
    pick2 = jnp.zeros((tokens, 128), F32)
    pick0 = [jnp.zeros((8, 128), F32) for _ in range(reqs)]
    lane = lax.broadcasted_iota(jnp.int32, (tokens, 128), 1)
    base = info_ref[1]
    t1 = tok_ref[:, 0:1] - base - lane
    t2 = tok_ref[:, 1:2] - base - lane
    t0 = [tok_ref[r * tree:r * tree + 8, 2:3] - base - lane[:8] for r in range(reqs)]
    for (start, size), cp in zip(chunks, copies):
        cp.wait()
        for at in range(start, start + size, 128):
            step = min(256, start + size - at) if (at - start) % 256 == 0 else 0
            if step == 0:
                continue
            logits = jnp.dot(x_ref[...], wbuf_ref[:, at:at + step], preferred_element_type=F32)
            for o in range(0, step, 128):
                lg = logits[:, o:o + 128]
                sums = sums + jnp.exp(lg)
                pick1 = jnp.where(t1 == at + o, lg, pick1)
                pick2 = jnp.where(t2 == at + o, lg, pick2)
                for r in range(reqs):
                    pick0[r] = jnp.where(t0[r] == at + o, lg[r * tree:r * tree + 8], pick0[r])
    zero = jnp.zeros((tree - 8, 128), F32)
    pick0 = jnp.concatenate([p for r in range(reqs) for p in (pick0[r], zero)], axis=0)
    stats = [jnp.sum(jnp.transpose(a), axis=0, keepdims=True) for a in (sums, pick1, pick2, pick0)]
    stats = jnp.concatenate(stats + [jnp.zeros((4, tokens), F32)], axis=0)
    for i in range(stat_ref.shape[0]):
        stat_ref[i] = stats


def vocab(info, mine, theirs, gain, toks, w, tree, copies):
    nz, nx, rows, cols = mine.shape
    tokens, width, size = nz * rows, 2 * nx * cols, w.shape[1]
    chunks = []
    at = 0
    while at < size:
        step = min(512, size - at)
        chunks.append((at, step))
        at += step
    vm = pl.BlockSpec(memory_space=pltpu.VMEM)
    return pl.pallas_call(
        functools.partial(vocab_kernel, tree, tuple(chunks)),
        out_shape=(
            jax.ShapeDtypeStruct((tokens, width), BF),
            jax.ShapeDtypeStruct((copies, 8, tokens), F32),
        ),
        in_specs=[pl.BlockSpec(memory_space=pltpu.SMEM), vm, vm, vm, vm, pl.BlockSpec(memory_space=pl.ANY)],
        out_specs=(vm, vm),
        scratch_shapes=[
            pltpu.VMEM((tokens, width), BF),
            pltpu.VMEM((width, size), BF),
            pltpu.SemaphoreType.DMA((len(chunks),)),
        ],
        compiler_params=pltpu.CompilerParams(vmem_limit_bytes=56 * MB),
        name="vocab",
    )(info, mine, theirs, gain, toks, w)


def local(
    queries, new_keys, new_values, cache_keys, cache_values, lengths, parents,
    tree_tokens, residual, out_weight, norm_gain, vocab_weight,
):
    reqs, tree, width = queries.shape
    slots = cache_keys.shape[1]
    z, x, core = lax.axis_index("z"), lax.axis_index("x"), lax.axis_index("core")
    nz, nx, nc = lax.axis_size("z"), lax.axis_size("x"), lax.axis_size("core")
    shard = (z * nx + x) * nc + core
    shards = nz * nx * nc
    window = slots * shards // 2
    half = width // nc
    block = half // nx
    tokens = reqs * tree
    swap = [(0, 1), (1, 0)]

    w = out_weight.reshape(-1, nc, nx, block).transpose(2, 1, 0, 3).reshape(nx * nc, -1, block)
    w = lax.all_to_all(w, ("x", "core"), 0, 0).reshape(-1, block)
    w = lax.all_gather(w, ("dp", "z"), axis=0, tiled=True)

    treq = jnp.where(shard < 2 * reqs, shard - reqs, -1)
    args = (lengths, parents, queries, cache_keys, cache_values, new_keys, new_values)
    scal = lambda h: jnp.stack([h, shard * slots, treq]).astype(jnp.int32)
    send = attend_half(window, 0, scal(1 - core), *args)
    got = lax.ppermute(send, "core", swap)
    keep = attend_half(window, 16, scal(core), *args)
    part = keep + got
    part = part.reshape(nz * nx, tokens // (nz * nx), half + 128)
    part = lax.all_to_all(part, ("z", "x"), 0, 0)
    att = combine(part, nx * nc)
    att = lax.all_to_all(att, ("x", "core"), 0, 0).reshape(nx, nc, -1, half)
    info = jnp.stack([z, core * nx + x]).astype(jnp.int32)
    hid = project(info, att, w, residual, nz * nx)
    hid = lax.all_to_all(hid, ("z", "x"), 0, 0).reshape(nz, nx, -1, block)
    other = lax.ppermute(hid, "core", swap)

    base = shard * vocab_weight.shape[1]
    pad = jnp.full((reqs, 2), -1, jnp.int32)
    shifted = jnp.concatenate([tree_tokens, pad], axis=1)
    toks = jnp.stack([shifted[:, 1:tree + 1].reshape(-1), shifted[:, 2:].reshape(-1), jnp.where(jnp.arange(tree) == 0, tree_tokens, -1).reshape(-1)], axis=1)
    info = jnp.stack([core, base]).astype(jnp.int32)
    hidden, stats = vocab(info, hid, other, norm_gain.reshape(1, -1), toks, vocab_weight, tree, shards)
    stats = jnp.sum(lax.all_to_all(stats, ("z", "x", "core"), 0, 0), axis=0)
    total, child1, child2, own = (stats[i].reshape(reqs, tree) for i in range(4))
    logt = jnp.log(total)
    back = lambda a, s: jnp.concatenate([a[:, :s], a[:, :tree - s]], axis=1)
    node = jnp.arange(tree)
    near = parents == node - 1
    first = node == 0
    picked = jnp.where(first, own, jnp.where(near, back(child1, 1), back(child2, 2)))
    logt = jnp.where(first, logt, jnp.where(near, back(logt, 1), back(logt, 2)))
    return hidden.reshape(reqs, tree, width), picked - logt


def solution(mesh):
    sizes = (mesh.shape["dp"], 4, 4, 2)
    grid = Mesh(mesh.devices.reshape(sizes), ("dp", "z", "x", "core"))
    mp = ("z", "x", "core")
    row = P("dp", None, None)
    placed = (
        row, row, row, P("dp", mp, None), P("dp", mp, None), P("dp"), P("dp", None), P("dp", None), row,
        P(("dp",) + mp, None), P(), P(None, mp),
    )
    return jax.shard_map(local, mesh=grid, in_specs=placed, out_specs=(row, P("dp", None)), check_vma=False)
```

time: 259 us -> 139 us (0.54)
  blocking collectives: 194 us -> 40.9 us
  Pallas kernels: 0 us -> 36.7 us
  matrix products: 35.8 us -> 0 us
  waiting for transfers between devices: 0.58 us -> 18.5 us
  starting transfers between devices: 0.08 us -> 13.7 us
    psum x2 -> x0, blocking collectives: 194 us -> none  [the longest x1 126 us: local(): lax.psum((cache_num.reshape(tokens, width), cache_den), 'mp')]
    all_to_all x0 -> x3, blocking collectives: none -> 40.9 us  [the longest x1 16.9 us: local(): part = lax.all_to_all(part, ('z', 'x'), 0, 0)]
    pallas_call x0 -> x5, Pallas kernels: none -> 36.7 us  [the longest x2 25.6 us: attend_half(): pl.pallas_call(functools.partial(attend_kernel, window, lane_off), out_sh...]
    dot_general x12 -> x0, matrix products: 35.8 us -> none  [the longest x1 10.5 us: local(): logits = jnp.dot(normed, vocab_weight, preferred_element_type=jnp.float32)]
    all_to_all x0 -> x2, waiting for transfers between devices: none -> 16.2 us  [the longest x1 10.3 us: local(): stats = jnp.sum(lax.all_to_all(stats, ('z', 'x', 'core'), 0, 0), axis=0)]
    all_to_all x0 -> x2, starting transfers between devices: none -> 9.69 us  [the longest x1 5.79 us: local(): att = lax.all_to_all(att, ('x', 'core'), 0, 0).reshape(nx, nc, -1, half)]
    gather x2 -> x0, local copies, waits for them, and re-layouts: 9.15 us -> none  [the longest x1 6.35 us: local(): logits[parent_rows, jnp.clip(column, 0, vocab_dev - 1)]]
    unnamed x14 -> x32, local copies, waits for them, and re-layouts: 0.09 us -> 9.14 us
  transfers between devices with their start and end apart: 2 -> 5, of which waited for: 0 -> 4; matrix products, arithmetic and copies ran while one was open for 4% -> 2% of each run, Pallas kernels for 0% -> 10%
where the time goes in v1:
time: 139 us; the launch traced here: 138 us
  blocking collectives  40.9 us (29%)
  Pallas kernels  36.7 us (26%)
  waiting for transfers between devices  18.5 us (13%)
  between operations  14.2 us (10%)
  starting transfers between devices  13.7 us (10%)
  local copies, waits for them, and re-layouts  10.6 us (8%)
  other arithmetic  3.02 us (2%)
    pallas_call x2, Pallas kernels, attend_half(): pl.pallas_call(functools.partial(attend_kernel, window, lane_off), out_sh...  25.6 us
    all_to_all x1, blocking collectives, local(): part = lax.all_to_all(part, ('z', 'x'), 0, 0)  16.9 us
    all_to_all x1, blocking collectives, local(): hid = lax.all_to_all(hid, ('z', 'x'), 0, 0).reshape(nz, nx, -1, block)  16.1 us
    all_to_all x1, waiting for transfers between devices, local(): stats = jnp.sum(lax.all_to_all(stats, ('z', 'x', 'core'), 0, 0), axis=0)  10.3 us
    pallas_call x1, Pallas kernels, vocab(): pl.pallas_call(functools.partial(vocab_kernel, tree, tuple(chunks)), out_...  9.29 us
    unnamed x32, local copies, waits for them, and re-layouts  9.14 us
    all_to_all x1, blocking collectives, local(): w = lax.all_to_all(w, ('x', 'core'), 0, 0).reshape(-1, block)  7.91 us
    all_to_all x1, waiting for transfers between devices, local(): att = lax.all_to_all(att, ('x', 'core'), 0, 0).reshape(nx, nc, -1, half)  5.9 us
  transfers between devices with their start and end apart: 5, of which 4 were waited for; matrix products, arithmetic and copies ran while one was open for 2% of the time, Pallas kernels for 10%

profile of v1, /device:TPU:1, one launch (start us, length us, event | category | flops | bytes accessed | tf_op | source)
XLA Modules:
  0.0 137.6 jit_solution(998059182436766027)
XLA Ops:
  7.3 1.4 %copy-done = bf16[8,48,2048]{2,1,0:T(8,128)(2,1)S(1)} copy-done((bf16[8,48,2048]{2,1,0:T(8,128)(2,1)S(1)}, bf16[8,48,2048]{2,1,0:T(8,128)(2,1)}, u32[]{:S(2)}) %copy-start) | copy-done | bytes 1572888
  8.7 1.4 %copy-done.2 = bf16[8,48,2048]{2,1,0:T(8,128)(2,1)S(1)} copy-done((bf16[8,48,2048]{2,1,0:T(8,128)(2,1)S(1)}, bf16[8,48,2048]{2,1,0:T(8,128)(2,1)}, u32[]{:S(2)}) %copy-start.2) | copy-done | bytes 1572888
  10.1 1.4 %copy-done.4 = bf16[8,48,2048]{2,1,0:T(8,128)(2,1)S(1)} copy-done((bf16[8,48,2048]{2,1,0:T(8,128)(2,1)S(1)}, bf16[8,48,2048]{2,1,0:T(8,128)(2,1)}, u32[]{:S(2)}) %copy-start.4) | copy-done | bytes 1572888
  11.5 0.7 copy-done.8
  12.2 0.7 copy-done.10
  12.9 13.4 %attend.3 = bf16[8,48,1152]{2,1,0:T(8,128)(2,1)} custom-call(s32[3]{0:T(128)S(1)} %add_add_fusion.1.info_ref, s32[8]{0:T(128)S(1)} %copy-done.10, s32[8,48]{1,0:T(8,128)S(1)} %copy-done.8, bf16[8,48,2048]{2,1,0:T(8,128)(2,1)S(1)} %copy-done, bf16[8,128,2048]{2,1,0:T(8,128)(2,1)} %k_ref.3, bf16[8,128,2048]{2,1,0:T(8,128)(2,1)} %v_ref.3, ...), custom_call_target="tpu_custom_call" | custom-call | tf_op jit(solution)/shard_map/attend/pallas_call | solution.py:76
  26.3 2.2 %collective-permute-start = (bf16[8,48,1152]{2,1,0:T(8,128)(2,1)}, bf16[8,48,1152]{2,1,0:T(8,128)(2,1)}, u32[]{:S(2)}, u32[]{:S(2)}) collective-permute-start(bf16[8,48,1152]{2,1,0:T(8,128)(2,1)} %attend.3), channel_id=1, source_target_pairs={{0,1},{1,0},{2,3},{3,2},{4,5},{5,4},{6,7},{7,6},{8,9},{9,8},{10,11... | collective-permute-start | bytes 2654216 | tf_op jit(solution)/shard_map/ppermute | solution.py:257
  28.5 7.9 %all_to_all.25 = bf16[8,16,256]{2,1,0:T(8,128)(2,1)} all-to-all(bf16[8,16,256]{2,1,0:T(8,128)(2,1)S(1)} %bitcast.28), channel_id=1, replica_groups=mesh['dp'=4,'z'=4,'x'=4,'core'=2] {'x','core'}, dimensions={0} | all-to-all | bytes 131072 | tf_op jit(solution)/shard_map/all_to_all | solution.py:250
  36.5 0.1 add_add_fusion.info_ref
  36.6 1.4 %copy-done.5 = bf16[8,48,2048]{2,1,0:T(8,128)(2,1)S(1)} copy-done((bf16[8,48,2048]{2,1,0:T(8,128)(2,1)S(1)}, bf16[8,48,2048]{2,1,0:T(8,128)(2,1)}, u32[]{:S(2)}) %copy-start.5) | copy-done | bytes 1572888
  38.0 12.2 %attend.2 = bf16[8,48,1152]{2,1,0:T(8,128)(2,1)S(1)} custom-call(s32[3]{0:T(128)S(1)} %add_add_fusion.info_ref, s32[8]{0:T(128)S(1)} %copy-done.11, s32[8,48]{1,0:T(8,128)S(1)} %copy-done.9, bf16[8,48,2048]{2,1,0:T(8,128)(2,1)S(1)} %copy-done.1, bf16[8,128,2048]{2,1,0:T(8,128)(2,1)} %k_ref.3, bf16[8,128,2048]{2,1,0:T(8,128)(2,1)} %v_ref.3, ...), custom_call_target="tpu_custom_call" | custom-call | tf_op jit(solution)/shard_map/attend/pallas_call | solution.py:76
  50.2 1.4 %add.23 = bf16[8,48,1152]{2,1,0:T(8,128)(2,1)S(1)} add(bf16[8,48,1152]{2,1,0:T(8,128)(2,1)S(1)} %attend.2, bf16[8,48,1152]{2,1,0:T(8,128)(2,1)} %collective-permute-done) | non-fusion elementwise | flops 442368 | bytes 2654208 | tf_op jit(solution)/shard_map/add | solution.py:259
  51.6 16.9 %all_to_all.26.parts_ref = bf16[16,24,1152]{2,1,0:T(8,128)(2,1)S(1)} all-to-all(bf16[16,24,1152]{2,1,0:T(8,128)(2,1)S(1)} %bitcast.24), channel_id=1, replica_groups=mesh['dp'=4,'z'=4,'x'=4,'core'=2] {'z','x'}, dimensions={0} | all-to-all | bytes 1769472 | tf_op jit(solution)/shard_map/all_to_all | solution.py:261
  68.5 0.9 combine.1
  69.4 5.8 %all-to-all-start.1 = ((bf16[8,24,1024]{2,1,0:T(8,128)(2,1)}), bf16[8,24,1024]{2,1,0:T(8,128)(2,1)S(1)}, u32[]{:S(2)}, u32[]{:S(2)}) async-start(bf16[8,24,1024]{2,1,0:T(8,128)(2,1)} %combine.1), calls=%async_computation.1 | async-start | bytes 786432 | tf_op jit(solution)/shard_map/all_to_all | solution.py:263
  75.3 2.1 %all-gather.2.cloned.1.call-done.w_ref = bf16[2048,256]{1,0:T(8,128)(2,1)} async-done(((bf16[128,256]{1,0:T(8,128)(2,1)}), bf16[2048,256]{1,0:T(8,128)(2,1)}) %all-gather.2.cloned.1.call-update) | async-done | bytes 1048592 | tf_op jit(solution)/shard_map/all_gather | solution.py:251
  77.4 5.9 %all-to-all-done.1 = bf16[8,24,1024]{2,1,0:T(8,128)(2,1)S(1)} async-done(((bf16[8,24,1024]{2,1,0:T(8,128)(2,1)}), bf16[8,24,1024]{2,1,0:T(8,128)(2,1)S(1)}, u32[]{:S(2)}, u32[]{:S(2)}) %all-to-all-start.1) | async-done | bytes 393248 | tf_op jit(solution)/shard_map/all_to_all | solution.py:263
  83.3 1.2 copy-done.7
  84.5 0.9 project.1
  85.4 16.1 %all_to_all.27 = bf16[16,96,256]{2,1,0:T(8,128)(2,1)S(1)} all-to-all(bf16[16,96,256]{2,1,0:T(8,128)(2,1)S(1)} %project.1), channel_id=1, replica_groups=mesh['dp'=4,'z'=4,'x'=4,'core'=2] {'z','x'}, dimensions={0} | all-to-all | bytes 1572864 | tf_op jit(solution)/shard_map/all_to_all | solution.py:266
  101.5 1.8 %collective-permute-start.1 = (bf16[4,4,96,256]{3,2,1,0:T(8,128)(2,1)S(1)}, bf16[4,4,96,256]{3,2,1,0:T(8,128)(2,1)S(1)}, u32[]{:S(2)}, u32[]{:S(2)}) collective-permute-start(bf16[4,4,96,256]{3,2,1,0:T(8,128)(2,1)S(1)} %bitcast.25), channel_id=1, source_target_pairs={{0,1},{1,0},{2,3},{3,2},{4,5},{5,4},{6,7},{7,6},{8,9},{9,8},{10,11... | collective-permute-start | bytes 2359304 | tf_op jit(solution)/shard_map/ppermute | solution.py:267
  103.4 0.1 stack_reshape.10
  103.5 0.1 stack_reshape.11
  103.7 0.8 copy.20.tok_ref
  104.5 0.6 pad_add_fusion.1.info_ref
  105.1 0.1 collective-permute-done.1.theirs_ref
  105.2 0.9 copy-done.13
  106.2 9.3 %vocab.1 = (bf16[384,2048]{1,0:T(8,128)(2,1)}, f32[32,8,384]{2,1,0:T(8,128)}) custom-call(s32[2]{0:T(128)} %pad_add_fusion.1.info_ref, bf16[4,4,96,256]{3,2,1,0:T(8,128)(2,1)} %bitcast.26, bf16[4,4,96,256]{3,2,1,0:T(8,128)(2,1)} %copy-done.13, f32[1,2048]{1,0:T(1,128)} %bitcast.38, s32[384,3]{1,0:T(8,128)} %copy.20.tok_ref, bf16[2048,2432]{1,0:T(8,128)(2,1)} %w_ref.1), custom_call_target="tpu_custom_call" | custom-call | tf_op jit(solution)/shard_map/vocab/pallas_call | solution.py:215
  115.5 3.9 %all-to-all-start.4 = ((f32[32,8,384]{2,1,0:T(8,128)}), f32[32,8,384]{2,1,0:T(8,128)S(1)}, u32[]{:S(2)}, u32[]{:S(2)}) async-start(f32[32,8,384]{2,1,0:T(8,128)} %get-tuple-element.5), calls=%async_computation.4 | async-start | bytes 786432 | tf_op jit(solution)/shard_map/all_to_all | solution.py:275
  119.4 10.3 %all-to-all-done.4 = f32[32,8,384]{2,1,0:T(8,128)S(1)} async-done(((f32[32,8,384]{2,1,0:T(8,128)}), f32[32,8,384]{2,1,0:T(8,128)S(1)}, u32[]{:S(2)}, u32[]{:S(2)}) %all-to-all-start.4) | async-done | bytes 393248 | tf_op jit(solution)/shard_map/all_to_all | solution.py:275
  130.0 0.1 reshape_squeeze.10
  130.0 0.7 fusion.1
  (41 shorter events, 0.8 us)
Async XLA Ops:
  7.2 70.2 %all-gather.2.cloned.1.call-start = ((), (), s32[]{:S(2)}) async-start(), calls=%async_computation.5 | async-start | bytes 1114112 | tf_op jit(solution)/shard_map/all_gather | solution.py:251
  7.3 1.4 %copy-start = (bf16[8,48,2048]{2,1,0:T(8,128)(2,1)S(1)}, bf16[8,48,2048]{2,1,0:T(8,128)(2,1)}, u32[]{:S(2)}) copy-start(bf16[8,48,2048]{2,1,0:T(8,128)(2,1)} %q_ref.3) | copy-start | bytes 4718596
  8.7 1.4 %copy-start.2 = (bf16[8,48,2048]{2,1,0:T(8,128)(2,1)S(1)}, bf16[8,48,2048]{2,1,0:T(8,128)(2,1)}, u32[]{:S(2)}) copy-start(bf16[8,48,2048]{2,1,0:T(8,128)(2,1)} %nk_ref.3) | copy-start | bytes 4718596
  10.1 1.4 %copy-start.4 = (bf16[8,48,2048]{2,1,0:T(8,128)(2,1)S(1)}, bf16[8,48,2048]{2,1,0:T(8,128)(2,1)}, u32[]{:S(2)}) copy-start(bf16[8,48,2048]{2,1,0:T(8,128)(2,1)} %nv_ref.3) | copy-start | bytes 4718596
  11.5 0.7 copy-start.8
  12.2 0.7 copy-start.10
  12.9 15.6 %copy-start.14 = (bf16[16,2048]{1,0:T(8,128)(2,1)S(1)}, bf16[16,2048]{1,0:T(8,128)(2,1)}, u32[]{:S(2)}) copy-start(bf16[16,2048]{1,0:T(8,128)(2,1)} %param.21) | copy-start | bytes 196612
  12.9 23.7 %copy-start.1 = (bf16[8,48,2048]{2,1,0:T(8,128)(2,1)S(1)}, bf16[8,48,2048]{2,1,0:T(8,128)(2,1)}, u32[]{:S(2)}) copy-start(bf16[8,48,2048]{2,1,0:T(8,128)(2,1)} %q_ref.3) | copy-start | bytes 4718596
  12.9 23.7 %copy-start.3 = (bf16[8,48,2048]{2,1,0:T(8,128)(2,1)S(1)}, bf16[8,48,2048]{2,1,0:T(8,128)(2,1)}, u32[]{:S(2)}) copy-start(bf16[8,48,2048]{2,1,0:T(8,128)(2,1)} %nk_ref.3) | copy-start | bytes 4718596
  12.9 23.7 %copy-start.9 = (s32[8,48]{1,0:T(8,128)S(1)}, s32[8,48]{1,0:T(8,128)}, u32[]{:S(2)}) copy-start(s32[8,48]{1,0:T(8,128)} %par_ref.3) | copy-start | bytes 4612
  12.9 23.7 %copy-start.11 = (s32[8]{0:T(128)S(1)}, s32[8]{0:T(128)}, u32[]{:S(2)}) copy-start(s32[8]{0:T(128)} %len_ref.3) | copy-start | bytes 100
  26.3 23.9 %collective-permute-start = (bf16[8,48,1152]{2,1,0:T(8,128)(2,1)}, bf16[8,48,1152]{2,1,0:T(8,128)(2,1)}, u32[]{:S(2)}, u32[]{:S(2)}) collective-permute-start(bf16[8,48,1152]{2,1,0:T(8,128)(2,1)} %attend.3), channel_id=1, source_target_pairs={{0,1},{1,0},{2,3},{3,2},{4,5},{5,4},{6,7},{7,6},{8,9},{9,8},{10,11... | collective-permute-start | bytes 2654216 | tf_op jit(solution)/shard_map/ppermute | solution.py:257
  36.6 1.4 %copy-start.5 = (bf16[8,48,2048]{2,1,0:T(8,128)(2,1)S(1)}, bf16[8,48,2048]{2,1,0:T(8,128)(2,1)}, u32[]{:S(2)}) copy-start(bf16[8,48,2048]{2,1,0:T(8,128)(2,1)} %nv_ref.3) | copy-start | bytes 4718596
  51.6 31.7 %copy-start.6 = (bf16[8,48,2048]{2,1,0:T(8,128)(2,1)S(1)}, bf16[8,48,2048]{2,1,0:T(8,128)(2,1)}, u32[]{:S(2)}) copy-start(bf16[8,48,2048]{2,1,0:T(8,128)(2,1)} %res_ref.1) | copy-start | bytes 4718596
  69.4 13.9 %all-to-all-start.1 = ((bf16[8,24,1024]{2,1,0:T(8,128)(2,1)}), bf16[8,24,1024]{2,1,0:T(8,128)(2,1)S(1)}, u32[]{:S(2)}, u32[]{:S(2)}) async-start(bf16[8,24,1024]{2,1,0:T(8,128)(2,1)} %combine.1), calls=%async_computation.1 | async-start | bytes 786432 | tf_op jit(solution)/shard_map/all_to_all | solution.py:263
  83.3 1.2 copy-start.7
  85.4 17.9 %copy-start.15 = (s32[8,48]{1,0:T(8,128)S(1)}, s32[8,48]{1,0:T(8,128)}, u32[]{:S(2)}) copy-start(s32[8,48]{1,0:T(8,128)} %param.19) | copy-start | bytes 4612
  101.5 3.7 %copy-start.12 = (bf16[16,96,256]{2,1,0:T(8,128)(2,1)}, bf16[16,96,256]{2,1,0:T(8,128)(2,1)S(1)}, u32[]{:S(2)}) copy-start(bf16[16,96,256]{2,1,0:T(8,128)(2,1)S(1)} %all_to_all.27) | copy-start | bytes 2359300
  101.5 3.7 %collective-permute-start.1 = (bf16[4,4,96,256]{3,2,1,0:T(8,128)(2,1)S(1)}, bf16[4,4,96,256]{3,2,1,0:T(8,128)(2,1)S(1)}, u32[]{:S(2)}, u32[]{:S(2)}) collective-permute-start(bf16[4,4,96,256]{3,2,1,0:T(8,128)(2,1)S(1)} %bitcast.25), channel_id=1, source_target_pairs={{0,1},{1,0},{2,3},{3,2},{4,5},{5,4},{6,7},{7,6},{8,9},{9,8},{10,11... | collective-permute-start | bytes 2359304 | tf_op jit(solution)/shard_map/ppermute | solution.py:267
  105.2 0.9 copy-start.13
  115.5 14.2 %all-to-all-start.4 = ((f32[32,8,384]{2,1,0:T(8,128)}), f32[32,8,384]{2,1,0:T(8,128)S(1)}, u32[]{:S(2)}, u32[]{:S(2)}) async-start(f32[32,8,384]{2,1,0:T(8,128)} %get-tuple-element.5), calls=%async_computation.4 | async-start | bytes 786432 | tf_op jit(solution)/shard_map/all_to_all | solution.py:275
Sparse Core Ops, SparseCore 0:
  36.6 40.7 all-gather.1

commit v2 on v1

v2 whole, which is shorter than its diff:
```python
import functools

import jax
import jax.numpy as jnp
from jax import lax
from jax.experimental import pallas as pl
from jax.experimental.pallas import tpu as pltpu
from jax.sharding import Mesh, PartitionSpec as P

HEADS = 16
SINK = 4
BF = jnp.bfloat16
F32 = jnp.float32
NT = (((1,), (1,)), ((), ()))
TN = (((0,), (0,)), ((), ()))
CORE, FIRST, TREQ, Z, BLOCK, DP, BASE = range(7)
MB = 1 << 20


def attend_kernel(window, lane_off, info_ref, len_ref, par_ref, q_ref, k_ref, v_ref, nk_ref, nv_ref, out_ref, anc_ref):
    step = pl.program_id(0)
    first = info_ref[FIRST]
    treq = info_ref[TREQ]
    reqs, tree, width = q_ref.shape
    slots = k_ref.shape[1]
    heads = width // 128
    scale = 128 ** (-0.5) * 1.4426950408889634

    def attend(r, keys, values, mask):
        dens = []
        scores = [
            lax.dot_general(keys(h), q_ref[r, :, h * 128:(h + 1) * 128], NT, preferred_element_type=F32)
            for h in range(heads)
        ]
        exps = [jnp.where(mask, jnp.exp2(s * scale), 0.0) for s in scores]
        for h in range(heads):
            dens.append(jnp.sum(exps[h], axis=0, keepdims=True))
            o = lax.dot_general(exps[h].astype(BF), values(h), TN, preferred_element_type=F32)
            out_ref[r, :, h * 128:(h + 1) * 128] = o.astype(BF)
        dens = jnp.concatenate(dens, axis=0)
        high = dens.astype(BF).astype(F32)
        pieces = [high, dens - high, jnp.zeros((128 - lane_off - 2 * heads, tree), F32)]
        if lane_off:
            pieces = [jnp.zeros((lane_off, tree), F32)] + pieces
        out_ref[r, :, width:] = jnp.transpose(jnp.concatenate(pieces, axis=0)).astype(BF)

    @pl.when(treq < 0)
    def _():
        pos = first + lax.broadcasted_iota(jnp.int32, (slots, tree), 0)
        for r in range(reqs):
            length = len_ref[step * reqs + r]
            mask = (pos < length) & ((pos < SINK) | (pos >= length - window))
            attend(
                r, lambda h: k_ref[r, :, h * 128:(h + 1) * 128], lambda h: v_ref[r, :, h * 128:(h + 1) * 128], mask
            )

    @pl.when(treq >= 0)
    def _():
        out_ref[...] = jnp.zeros_like(out_ref)

        @pl.when(treq // reqs == step)
        def _():
            node = lax.broadcasted_iota(jnp.int32, (1, 128), 1)
            anc_ref[...] = jnp.zeros_like(anc_ref)
            anc_ref[0:1, :] = jnp.where(node == 0, 1.0, 0.0)

            def body(i, carry):
                up = anc_ref[pl.ds(par_ref[treq, i], 1), :]
                anc_ref[pl.ds(i, 1), :] = jnp.where(node == i, 1.0, up)
                return carry

            lax.fori_loop(1, tree, body, 0)
            mask = jnp.transpose(anc_ref[...])[:tree, :tree] > 0.5
            attend(
                lax.rem(treq, reqs), lambda h: nk_ref[0, :, h * 128:(h + 1) * 128],
                lambda h: nv_ref[0, :, h * 128:(h + 1) * 128], mask,
            )


def attend_half(window, mine, info, lengths, parents, q, k, v, nk, nv):
    reqs, tree, width = q.shape
    slots = k.shape[1]
    half = width // 2
    group = reqs // 2
    hidx = (lambda i: i[CORE]) if mine else (lambda i: 1 - i[CORE])
    qs = pl.BlockSpec((group, tree, half), lambda r, i, l, p: (r, 0, hidx(i)))
    ks = pl.BlockSpec((group, slots, half), lambda r, i, l, p: (r, 0, hidx(i)))
    ns = pl.BlockSpec((1, tree, half), lambda r, i, l, p: (jnp.clip(i[TREQ], 0, reqs - 1), 0, hidx(i)))
    q, k, v, nk, nv = (pltpu.with_memory_space_constraint(a, pltpu.HBM) for a in (q, k, v, nk, nv))
    return pl.pallas_call(
        functools.partial(attend_kernel, window, 16 if mine else 0),
        out_shape=jax.ShapeDtypeStruct((reqs, tree, half + 128), BF),
        grid_spec=pltpu.PrefetchScalarGridSpec(
            num_scalar_prefetch=3,
            grid=(reqs // group,),
            in_specs=[qs, ks, ks, ns, ns],
            out_specs=pl.BlockSpec((group, tree, half + 128), lambda r, i, l, p: (r, 0, 0)),
            scratch_shapes=[pltpu.VMEM((128, 128), F32)],
        ),
        compiler_params=pltpu.CompilerParams(vmem_limit_bytes=48 * MB),
        name="attend_mine" if mine else "attend_theirs",
    )(info, lengths, parents, q, k, v, nk, nv)


def combine_kernel(parts_ref, out_ref):
    heads = out_ref.shape[1]
    width = heads * 128
    total = jnp.sum(parts_ref[...].astype(F32), axis=0)
    den = total[:, width:]
    lane = lax.broadcasted_iota(jnp.int32, den.shape, 1)
    for h in range(heads):
        d = jnp.sum(jnp.where((lane % heads == h) & (lane < 4 * heads), den, 0.0), axis=1, keepdims=True)
        val = (total[:, h * 128:(h + 1) * 128] / d).astype(BF)
        for c in range(out_ref.shape[0]):
            out_ref[c, h] = val


def combine(parts, copies):
    rows, cols = parts.shape[1], parts.shape[2]
    return pl.pallas_call(
        combine_kernel,
        out_shape=jax.ShapeDtypeStruct((copies, cols // 128 - 1, rows, 128), BF),
        compiler_params=pltpu.CompilerParams(vmem_limit_bytes=48 * MB),
        name="combine",
    )(parts)


def project_kernel(info_ref, att_ref, *refs):
    w_refs, res_ref, out_ref = refs[:-2], refs[-2], refs[-1]
    nx, heads, rows, _ = att_ref.shape
    ny, nz = len(w_refs), w_refs[0].shape[0]
    y, z = info_ref[DP], info_ref[Z]
    acc = res_ref[...].astype(F32).reshape(nx * rows, res_ref.shape[2])
    for i in range(ny):
        for j in range(nz):
            h = lax.rem(y + ny - i, ny) * nz + lax.rem(z + nz - j, nz)
            a = jnp.concatenate([att_ref[x, h] for x in range(nx)], axis=0)
            acc = acc + jnp.dot(a, w_refs[i][j], preferred_element_type=F32)
    hid = acc.astype(BF)
    for i in range(out_ref.shape[0]):
        out_ref[i] = hid


def project(info, att, ws, residual, copies):
    nx, heads, rows, _ = att.shape
    tree = residual.shape[1]
    reqs = nx * rows // tree
    cols = ws[0].shape[2]
    return pl.pallas_call(
        project_kernel,
        out_shape=jax.ShapeDtypeStruct((copies, nx * rows, cols), BF),
        grid_spec=pltpu.PrefetchScalarGridSpec(
            num_scalar_prefetch=1,
            grid=(1,),
            in_specs=[pl.BlockSpec(att.shape, lambda g, i: (0, 0, 0, 0))]
            + [pl.BlockSpec(w.shape, lambda g, i: (0, 0, 0)) for w in ws]
            + [pl.BlockSpec((reqs, tree, cols), lambda g, i: (i[Z], 0, i[BLOCK]))],
            out_specs=pl.BlockSpec((copies, nx * rows, cols), lambda g, i: (0, 0, 0)),
        ),
        compiler_params=pltpu.CompilerParams(vmem_limit_bytes=48 * MB),
        name="project",
    )(info, att, *ws, pltpu.with_memory_space_constraint(residual, pltpu.HBM))


def shift_lanes(a, n):
    return jnp.concatenate([a[:, -n:], a[:, :-n]], axis=1)


def vocab_kernel(tree, chunks, info_ref, mine_ref, theirs_ref, gain_ref, tok_ref, par_ref, w_ref, hid_ref, stat_ref, x_ref, wbuf_ref, sem):
    copies = []
    for i, (start, size) in enumerate(chunks):
        cp = pltpu.make_async_copy(w_ref.at[:, pl.ds(start, size)], wbuf_ref.at[:, pl.ds(start, size)], sem.at[i])
        cp.start()
        copies.append(cp)
    core = info_ref[CORE]
    nz, nx, rows, cols = mine_ref.shape
    half = nx * cols
    for z in range(nz):
        rs = slice(z * rows, (z + 1) * rows)
        squares = jnp.zeros((rows, cols), F32)
        for x in range(nx):
            mine, theirs = mine_ref[z, x], theirs_ref[z, x]
            low = jnp.where(core == 0, mine, theirs)
            high = jnp.where(core == 0, theirs, mine)
            hid_ref[rs, x * cols:(x + 1) * cols] = low
            hid_ref[rs, half + x * cols:half + (x + 1) * cols] = high
            squares = squares + low.astype(F32) * low.astype(F32) + high.astype(F32) * high.astype(F32)
        inv = lax.rsqrt(jnp.sum(squares, axis=1, keepdims=True) / (2 * half) + 1e-06)
        for j in range(2 * nx):
            cs = slice(j * cols, (j + 1) * cols)
            x_ref[rs, cs] = (hid_ref[rs, cs].astype(F32) * inv * gain_ref[:, cs]).astype(BF)
    tokens = nz * rows
    reqs = tokens // tree
    sums = jnp.zeros((tokens, 128), F32)
    pick1 = jnp.zeros((tokens, 128), F32)
    pick2 = jnp.zeros((tokens, 128), F32)
    pick0 = [jnp.zeros((8, 128), F32) for _ in range(reqs)]
    lane = lax.broadcasted_iota(jnp.int32, (tokens, 128), 1)
    base = info_ref[BASE]
    tok = jnp.concatenate([tok_ref[...].astype(F32), jnp.full((reqs, 128 - tree), -1.0, F32)], axis=1)
    tok = jnp.transpose(tok)
    column = lambda n: jnp.concatenate([tok[n:n + tree, r:r + 1] for r in range(reqs)], axis=0).astype(jnp.int32)
    t1 = column(1) - base - lane
    t2 = column(2) - base - lane
    node = lax.broadcasted_iota(jnp.int32, (8, 128), 0)
    t0 = [jnp.where(node == 0, tok[0:8, r:r + 1].astype(jnp.int32) - base - lane[:8], -1) for r in range(reqs)]
    for (start, size), cp in zip(chunks, copies):
        cp.wait()
        for at in range(start, start + size, 256):
            step = min(256, start + size - at)
            logits = jnp.dot(x_ref[...], wbuf_ref[:, at:at + step], preferred_element_type=F32)
            for o in range(0, step, 128):
                lg = logits[:, o:o + 128]
                sums = sums + jnp.exp(lg)
                pick1 = jnp.where(t1 == at + o, lg, pick1)
                pick2 = jnp.where(t2 == at + o, lg, pick2)
                for r in range(reqs):
                    pick0[r] = jnp.where(t0[r] == at + o, lg[r * tree:r * tree + 8], pick0[r])
    zero = jnp.zeros((tree - 8, 128), F32)
    pick0 = jnp.concatenate([p for r in range(reqs) for p in (pick0[r], zero)], axis=0)
    total, pick1, pick2, pick0 = (
        jnp.sum(jnp.transpose(a), axis=0, keepdims=True) for a in (sums, pick1, pick2, pick0)
    )
    at_node = lax.broadcasted_iota(jnp.int32, (1, tokens), 1) % tree
    near = par_ref[...] == at_node - 1
    root = at_node == 0
    pick = jnp.where(root, pick0, jnp.where(near, shift_lanes(pick1, 1), shift_lanes(pick2, 2)))
    total = jnp.where(root, total, jnp.where(near, shift_lanes(total, 1), shift_lanes(total, 2)))
    groups = tokens // 128
    stats = [a[:, g * 128:(g + 1) * 128] for a in (total, pick) for g in range(groups)]
    stats = jnp.concatenate(stats + [jnp.zeros((8 - 2 * groups, 128), F32)], axis=0)
    for i in range(stat_ref.shape[0]):
        stat_ref[i] = stats


def vocab(info, mine, theirs, gain, toks, parents, w, copies):
    tree = toks.shape[1]
    nz, nx, rows, cols = mine.shape
    tokens, width, size = nz * rows, 2 * nx * cols, w.shape[1]
    chunks = []
    at = 0
    while at < size:
        step = min(512, size - at)
        chunks.append((at, step))
        at += step
    vm = pl.BlockSpec(memory_space=pltpu.VMEM)
    return pl.pallas_call(
        functools.partial(vocab_kernel, tree, tuple(chunks)),
        out_shape=(
            jax.ShapeDtypeStruct((tokens, width), BF),
            jax.ShapeDtypeStruct((copies, 8, 128), F32),
        ),
        in_specs=[pl.BlockSpec(memory_space=pltpu.SMEM), vm, vm, vm, vm, vm, pl.BlockSpec(memory_space=pl.ANY)],
        out_specs=(vm, vm),
        scratch_shapes=[
            pltpu.VMEM((tokens, width), BF),
            pltpu.VMEM((width, size), BF),
            pltpu.SemaphoreType.DMA((len(chunks),)),
        ],
        compiler_params=pltpu.CompilerParams(vmem_limit_bytes=56 * MB),
        name="vocab",
    )(info, mine, theirs, gain, toks, parents.reshape(1, -1), w)


def shifted(a, axis, step):
    n = lax.axis_size(axis)
    return lax.ppermute(a, axis, [(i, (i + step) % n) for i in range(n)])


def local(
    queries, new_keys, new_values, cache_keys, cache_values, lengths, parents,
    tree_tokens, residual, out_weight, norm_gain, vocab_weight,
):
    reqs, tree, width = queries.shape
    slots = cache_keys.shape[1]
    y, z, x, core = (lax.axis_index(a) for a in ("dp", "z", "x", "core"))
    ny, nz, nx, nc = (lax.axis_size(a) for a in ("dp", "z", "x", "core"))
    shard = (z * nx + x) * nc + core
    shards = nz * nx * nc
    window = slots * shards // 2
    half = width // nc
    block = half // nx
    tokens = reqs * tree
    swap = [(0, 1), (1, 0)]
    treq = jnp.where((shard >= reqs) & (shard < 2 * reqs), shard - reqs, -1)
    info = jnp.stack([core, shard * slots, treq, z, core * nx + x, y, shard * vocab_weight.shape[1]]).astype(jnp.int32)

    w = out_weight.reshape(-1, nc, nx, block).transpose(2, 1, 0, 3).reshape(nx * nc, -1, block)
    w = lax.all_to_all(w, ("x", "core"), 0, 0).reshape(-1, block)
    w = jnp.stack([w] + [shifted(w, "z", s) for s in range(1, nz)])
    ws = [w] + [shifted(w, "dp", s) for s in range(1, ny)]

    args = (lengths, parents, queries, cache_keys, cache_values, new_keys, new_values)
    send = attend_half(window, False, info, *args)
    got = lax.ppermute(send, "core", swap)
    keep = attend_half(window, True, info, *args)
    part = (keep + got).reshape(nz * nx, tokens // (nz * nx), half + 128)
    part = lax.all_to_all(part, ("z", "x"), 0, 0)
    att = combine(part, nx * nc)
    att = lax.all_to_all(att, ("x", "core"), 0, 0).reshape(nx, HEADS, -1, 128)
    hid = project(info, att, ws, residual, nz * nx)
    hid = lax.all_to_all(hid, ("z", "x"), 0, 0).reshape(nz, nx, -1, block)
    other = lax.ppermute(hid, "core", swap)
    hidden, stats = vocab(info, hid, other, norm_gain.reshape(1, -1), tree_tokens, parents, vocab_weight, shards)
    stats = jnp.sum(lax.all_to_all(stats, ("z", "x", "core"), 0, 0), axis=0)
    rows = tokens // 128
    logprob = stats[rows:2 * rows] - jnp.log(stats[:rows])
    return hidden.reshape(reqs, tree, width), logprob.reshape(reqs, tree)


def solution(mesh):
    sizes = (mesh.shape["dp"], 4, 4, 2)
    grid = Mesh(mesh.devices.reshape(sizes), ("dp", "z", "x", "core"))
    mp = ("z", "x", "core")
    row = P("dp", None, None)
    placed = (
        row, row, row, P("dp", mp, None), P("dp", mp, None), P("dp"), P("dp", None), P("dp", None), row,
        P(("dp",) + mp, None), P(), P(None, mp),
    )
    return jax.shard_map(local, mesh=grid, in_specs=placed, out_specs=(row, P("dp", None)), check_vma=False)
```

time: 139 us -> 111 us (0.80)
  starting transfers between devices: 13.7 us -> 31.8 us
  Pallas kernels: 36.7 us -> 22.7 us
  between operations: 14.2 us -> 0.75 us
  blocking collectives: 40.9 us -> 28.2 us
  local copies, waits for them, and re-layouts: 10.6 us -> 4.34 us
  waiting for transfers between devices: 18.5 us -> 21.8 us
  other arithmetic: 3.02 us -> 1.23 us
    pallas_call x3, Pallas kernels: 26.5 us -> 11.7 us  [the longest x2 10.8 us: attend_half(): pl.pallas_call(functools.partial(attend_kernel, window, 16 if mine else 0...]
    all_to_all x2 -> x1, blocking collectives: 24.8 us -> 11.6 us  [local(): stats = jnp.sum(lax.all_to_all(stats, ('z', 'x', 'core'), 0, 0), axis=0)]
    ppermute x0 -> x6, waiting for transfers between devices: none -> 10.9 us  [shifted(): return lax.ppermute(a, axis, [(i, (i + step) % n) for i in range(n)])]
    ppermute x0 -> x6, starting transfers between devices: none -> 10 us  [shifted(): return lax.ppermute(a, axis, [(i, (i + step) % n) for i in range(n)])]
    all_to_all x2 -> x3, starting transfers between devices: 9.69 us -> 17.7 us  [the longest x1 7.74 us: local(): part = lax.all_to_all(part, ('z', 'x'), 0, 0)]
    unnamed x32 -> x16, local copies, waits for them, and re-layouts: 9.14 us -> 2.28 us
    all_to_all x2 -> x3, waiting for transfers between devices: 16.2 us -> 9.65 us  [the longest x1 9.65 us: local(): part = lax.all_to_all(part, ('z', 'x'), 0, 0)]
    all_gather x1 -> x0, waiting for transfers between devices: 2.12 us -> none  [local(): w = lax.all_gather(w, ('dp', 'z'), axis=0, tiled=True)]
  transfers between devices with their start and end apart: 5 -> 11, of which waited for: 4 -> 4; matrix products, arithmetic and copies ran while one was open for 2% -> 2% of each run, Pallas kernels for 10% -> 6%
where the time goes in v2:
time: 111 us
  starting transfers between devices  31.8 us (29%)
  blocking collectives  28.2 us (25%)
  Pallas kernels  22.7 us (20%)
  waiting for transfers between devices  21.8 us (20%)
  local copies, waits for them, and re-layouts  4.34 us (4%)
  other arithmetic  1.23 us (1%)
    all_to_all x1, blocking collectives, local(): hid = lax.all_to_all(hid, ('z', 'x'), 0, 0).reshape(nz, nx, -1, block)  16.6 us
    all_to_all x1, blocking collectives, local(): stats = jnp.sum(lax.all_to_all(stats, ('z', 'x', 'core'), 0, 0), axis=0)  11.6 us
    ppermute x6, waiting for transfers between devices, shifted(): return lax.ppermute(a, axis, [(i, (i + step) % n) for i in range(n)])  10.9 us
    pallas_call x2, Pallas kernels, attend_half(): pl.pallas_call(functools.partial(attend_kernel, window, 16 if mine else 0...  10.8 us
    ppermute x6, starting transfers between devices, shifted(): return lax.ppermute(a, axis, [(i, (i + step) % n) for i in range(n)])  10 us
    all_to_all x1, waiting for transfers between devices, local(): part = lax.all_to_all(part, ('z', 'x'), 0, 0)  9.65 us
    pallas_call x1, Pallas kernels, vocab(): pl.pallas_call(functools.partial(vocab_kernel, tree, tuple(chunks)), out_...  9.26 us
    all_to_all x1, starting transfers between devices, local(): part = lax.all_to_all(part, ('z', 'x'), 0, 0)  7.74 us
  transfers between devices with their start and end apart: 11, of which 4 were waited for; matrix products, arithmetic and copies ran while one was open for 2% of the time, Pallas kernels for 6%

profile of v2, /device:TPU:1, one launch (start us, length us, event | category | flops | bytes accessed | tf_op | source)
XLA Modules:
  0.0 110.9 jit_solution(634063193962602333)
XLA Ops:
  0.6 0.1 stack.43.info_ref
  0.7 0.7 copy-done
  1.4 0.7 copy-done.3
  2.1 5.4 %attend_theirs.1 = bf16[8,48,1152]{2,1,0:T(8,128)(2,1)S(1)} custom-call(s32[7]{0:T(128)S(1)} %stack.43.info_ref, s32[8]{0:T(128)S(1)} %copy-done.3, s32[8,48]{1,0:T(8,128)S(1)} %copy-done, bf16[8,48,2048]{2,1,0:T(8,128)(2,1)} %q_ref.3, bf16[8,128,2048]{2,1,0:T(8,128)(2,1)} %k_ref.3, bf16[8,128,2048]{2,1,0:T(8,128)(2,1)} %v_ref.3, ...), custom_call_target="tpu_custom_call" | custom-call | tf_op jit(solution)/shard_map/attend_theirs/pallas_call | solution.py:90
  7.5 1.5 %collective-permute-start = (bf16[8,48,1152]{2,1,0:T(8,128)(2,1)S(1)}, bf16[8,48,1152]{2,1,0:T(8,128)(2,1)S(1)}, u32[]{:S(2)}, u32[]{:S(2)}) collective-permute-start(bf16[8,48,1152]{2,1,0:T(8,128)(2,1)S(1)} %attend_theirs.1), channel_id=1, source_target_pairs={{0,1},{1,0},{2,3},{3,2},{4,5},{5,4},{6,7},{7,6},{8,9},{9,8},{10,11... | collective-permute-start | bytes 2654216 | tf_op jit(solution)/shard_map/ppermute | solution.py:295
  9.0 0.6 copy.14
  9.7 4.5 %all-to-all-start.2 = ((bf16[8,16,256]{2,1,0:T(8,128)(2,1)}), bf16[8,16,256]{2,1,0:T(8,128)(2,1)S(1)}, u32[]{:S(2)}, u32[]{:S(2)}) async-start(bf16[8,16,256]{2,1,0:T(8,128)(2,1)} %bitcast.10), calls=%async_computation.2 | async-start | bytes 131072 | tf_op jit(solution)/shard_map/all_to_all | solution.py:289
  14.2 5.4 %attend_mine.1 = bf16[8,48,1152]{2,1,0:T(8,128)(2,1)S(1)} custom-call(s32[7]{0:T(128)S(1)} %stack.43.info_ref, s32[8]{0:T(128)S(1)} %copy-done.4, s32[8,48]{1,0:T(8,128)S(1)} %copy-done.1, bf16[8,48,2048]{2,1,0:T(8,128)(2,1)} %q_ref.3, bf16[8,128,2048]{2,1,0:T(8,128)(2,1)} %k_ref.3, bf16[8,128,2048]{2,1,0:T(8,128)(2,1)} %v_ref.3, ...), custom_call_target="tpu_custom_call" | custom-call | tf_op jit(solution)/shard_map/attend_mine/pallas_call | solution.py:90
  19.6 1.1 %add.16 = bf16[8,48,1152]{2,1,0:T(8,128)(2,1)} add(bf16[8,48,1152]{2,1,0:T(8,128)(2,1)S(1)} %attend_mine.1, bf16[8,48,1152]{2,1,0:T(8,128)(2,1)S(1)} %collective-permute-done) | non-fusion elementwise | flops 442368 | bytes 2654208 | tf_op jit(solution)/shard_map/add | solution.py:297
  20.7 0.0 all-to-all-done.2
  20.7 7.7 %all-to-all-start = ((bf16[16,24,1152]{2,1,0:T(8,128)(2,1)}), bf16[16,24,1152]{2,1,0:T(8,128)(2,1)S(1)}, u32[]{:S(2)}, u32[]{:S(2)}) async-start(bf16[16,24,1152]{2,1,0:T(8,128)(2,1)} %bitcast.7), calls=%async_computation | async-start | bytes 1769472 | tf_op jit(solution)/shard_map/all_to_all | solution.py:298
  28.5 1.4 %collective-permute-start.1 = (bf16[128,256]{1,0:T(8,128)(2,1)S(1)}, bf16[128,256]{1,0:T(8,128)(2,1)S(1)}, u32[]{:S(2)}, u32[]{:S(2)}) collective-permute-start(bf16[128,256]{1,0:T(8,128)(2,1)S(1)} %bitcast.23), channel_id=1, source_target_pairs={{0,8},{8,16},{16,24},{24,0},{1,9},{9,17},{17,25},{25,1},{2,10},{10... | collective-permute-start | bytes 196616 | tf_op jit(solution)/shard_map/ppermute | solution.py:267
  29.8 2.4 %collective-permute-start.2 = (bf16[128,256]{1,0:T(8,128)(2,1)S(1)}, bf16[128,256]{1,0:T(8,128)(2,1)S(1)}, u32[]{:S(2)}, u32[]{:S(2)}) collective-permute-start(bf16[128,256]{1,0:T(8,128)(2,1)S(1)} %bitcast.24), channel_id=1, source_target_pairs={{0,16},{8,24},{16,0},{24,8},{1,17},{9,25},{17,1},{25,9},{2,18},{10... | collective-permute-start | bytes 196616 | tf_op jit(solution)/shard_map/ppermute | solution.py:267
  32.2 1.2 %collective-permute-start.3 = (bf16[128,256]{1,0:T(8,128)(2,1)S(1)}, bf16[128,256]{1,0:T(8,128)(2,1)S(1)}, u32[]{:S(2)}, u32[]{:S(2)}) collective-permute-start(bf16[128,256]{1,0:T(8,128)(2,1)S(1)} %bitcast.25), channel_id=1, source_target_pairs={{0,24},{8,0},{16,8},{24,16},{1,25},{9,1},{17,9},{25,17},{2,26},{10... | collective-permute-start | bytes 196616 | tf_op jit(solution)/shard_map/ppermute | solution.py:267
  33.4 9.6 %all-to-all-done.parts_ref = bf16[16,24,1152]{2,1,0:T(8,128)(2,1)S(1)} async-done(((bf16[16,24,1152]{2,1,0:T(8,128)(2,1)}), bf16[16,24,1152]{2,1,0:T(8,128)(2,1)S(1)}, u32[]{:S(2)}, u32[]{:S(2)}) %all-to-all-start) | async-done | bytes 884768 | tf_op jit(solution)/shard_map/all_to_all | solution.py:298
  43.1 0.9 combine.1
  44.0 5.5 %all-to-all-start.1 = ((bf16[8,8,24,128]{3,2,1,0:T(8,128)(2,1)}), bf16[8,8,24,128]{3,2,1,0:T(8,128)(2,1)S(1)}, u32[]{:S(2)}, u32[]{:S(2)}) async-start(bf16[8,8,24,128]{3,2,1,0:T(8,128)(2,1)} %combine.1), calls=%async_computation.1 | async-start | bytes 786432 | tf_op jit(solution)/shard_map/all_to_all | solution.py:300
  49.5 0.0 collective-permute-done.2
  49.5 1.4 %collective-permute-start.4 = (bf16[4,128,256]{2,1,0:T(8,128)(2,1)S(1)}, bf16[4,128,256]{2,1,0:T(8,128)(2,1)S(1)}, u32[]{:S(2)}, u32[]{:S(2)}) collective-permute-start(bf16[4,128,256]{2,1,0:T(8,128)(2,1)S(1)} %pad_maximum_fusion.refs_0_), channel_id=1, source_target_pairs={{0,32},{32,64},{64,96},{96,0},{1,33},{33,65},{65,97},{97,1},{2,34}... | collective-permute-start | bytes 786440 | tf_op jit(solution)/shard_map/ppermute | solution.py:267
  50.9 2.6 %collective-permute-start.5 = (bf16[4,128,256]{2,1,0:T(8,128)(2,1)S(1)}, bf16[4,128,256]{2,1,0:T(8,128)(2,1)S(1)}, u32[]{:S(2)}, u32[]{:S(2)}) collective-permute-start(bf16[4,128,256]{2,1,0:T(8,128)(2,1)S(1)} %pad_maximum_fusion.refs_0_), channel_id=1, source_target_pairs={{0,64},{32,96},{64,0},{96,32},{1,65},{33,97},{65,1},{97,33},{2,66}... | collective-permute-start | bytes 786440 | tf_op jit(solution)/shard_map/ppermute | solution.py:267
  53.5 1.1 collective-permute-start.6
  54.6 4.1 %collective-permute-done.4.refs_1_ = bf16[4,128,256]{2,1,0:T(8,128)(2,1)S(1)} collective-permute-done((bf16[4,128,256]{2,1,0:T(8,128)(2,1)S(1)}, bf16[4,128,256]{2,1,0:T(8,128)(2,1)S(1)}, u32[]{:S(2)}, u32[]{:S(2)}) %collective-permute-start.4) | collective-permute-done | bytes 262176 | tf_op jit(solution)/shard_map/ppermute | solution.py:267
  58.7 6.7 %collective-permute-done.5.refs_2_ = bf16[4,128,256]{2,1,0:T(8,128)(2,1)S(1)} collective-permute-done((bf16[4,128,256]{2,1,0:T(8,128)(2,1)S(1)}, bf16[4,128,256]{2,1,0:T(8,128)(2,1)S(1)}, u32[]{:S(2)}, u32[]{:S(2)}) %collective-permute-start.5) | collective-permute-done | bytes 262176 | tf_op jit(solution)/shard_map/ppermute | solution.py:267
  65.4 1.8 %project.1 = bf16[16,96,256]{2,1,0:T(8,128)(2,1)S(1)} custom-call(s32[7]{0:T(128)S(1)} %stack.43.info_ref, bf16[4,16,24,128]{3,2,1,0:T(8,128)(2,1)S(1)} %bitcast.19, bf16[4,128,256]{2,1,0:T(8,128)(2,1)S(1)} %pad_maximum_fusion.refs_0_, bf16[4,128,256]{2,1,0:T(8,128)(2,1)S(1)} %collective-permute-done.4.refs_1_, ...), custom_call_target="tpu_custom_call" | custom-call | tf_op jit(solution)/shard_map/project/pallas_call | solution.py:149
  67.2 16.6 %all_to_all.25 = bf16[16,96,256]{2,1,0:T(8,128)(2,1)S(1)} all-to-all(bf16[16,96,256]{2,1,0:T(8,128)(2,1)S(1)} %project.1), channel_id=1, replica_groups=mesh['dp'=4,'z'=4,'x'=4,'core'=2] {'z','x'}, dimensions={0} | all-to-all | bytes 1572864 | tf_op jit(solution)/shard_map/all_to_all | solution.py:302
  83.8 2.6 %collective-permute-start.7 = (bf16[4,4,96,256]{3,2,1,0:T(8,128)(2,1)S(1)}, bf16[4,4,96,256]{3,2,1,0:T(8,128)(2,1)S(1)}, u32[]{:S(2)}, u32[]{:S(2)}) collective-permute-start(bf16[4,4,96,256]{3,2,1,0:T(8,128)(2,1)S(1)} %bitcast.20), channel_id=1, source_target_pairs={{0,1},{1,0},{2,3},{3,2},{4,5},{5,4},{6,7},{7,6},{8,9},{9,8},{10,11... | collective-permute-start | bytes 2359304 | tf_op jit(solution)/shard_map/ppermute | solution.py:303
  86.4 0.6 reshape.41.par_ref
  87.1 1.3 %collective-permute-done.7.theirs_ref = bf16[4,4,96,256]{3,2,1,0:T(8,128)(2,1)S(1)} collective-permute-done((bf16[4,4,96,256]{3,2,1,0:T(8,128)(2,1)S(1)}, bf16[4,4,96,256]{3,2,1,0:T(8,128)(2,1)S(1)}, u32[]{:S(2)}, u32[]{:S(2)}) %collective-permute-start.7) | collective-permute-done | bytes 786464 | tf_op jit(solution)/shard_map/ppermute | solution.py:303
  88.3 0.9 copy-done.6
  89.3 9.3 %vocab.1 = (bf16[384,2048]{1,0:T(8,128)(2,1)}, f32[32,8,128]{2,1,0:T(8,128)}) custom-call(s32[7]{0:T(128)} %copy-done.2, bf16[4,4,96,256]{3,2,1,0:T(8,128)(2,1)} %bitcast.21, bf16[4,4,96,256]{3,2,1,0:T(8,128)(2,1)} %copy-done.6, f32[1,2048]{1,0:T(1,128)} %bitcast.30, s32[8,48]{1,0:T(8,128)} %tok_ref.1, s32[1,384]{1,0:T(1,128)} %reshape.41.par_ref, ...), custom_call_target="tpu_custom_call" | custom-call | tf_op jit(solution)/shard_map/vocab/pallas_call | solution.py:247
  98.5 11.6 %all_to_all.26 = f32[32,8,128]{2,1,0:T(8,128)S(1)} all-to-all(f32[32,8,128]{2,1,0:T(8,128)} %get-tuple-element.5), channel_id=1, replica_groups=mesh['dp'=4,'z'=4,'x'=4,'core'=2] {'z','x','core'}, dimensions={0} | all-to-all | bytes 262144 | tf_op jit(solution)/shard_map/all_to_all | solution.py:305
  110.2 0.7 reshape.43
  (22 shorter events, 0.1 us)
Async XLA Ops:
  0.7 0.7 copy-start
  1.4 0.7 copy-start.3
  2.1 63.4 %copy-start.2 = (s32[7]{0:T(128)}, s32[7]{0:T(128)S(1)}, u32[]{:S(2)}) copy-start(s32[7]{0:T(128)S(1)} %stack.43.info_ref) | copy-start | bytes 88
  2.1 6.9 %copy-start.7 = (bf16[16,2048]{1,0:T(8,128)(2,1)S(1)}, bf16[16,2048]{1,0:T(8,128)(2,1)}, u32[]{:S(2)}) copy-start(bf16[16,2048]{1,0:T(8,128)(2,1)} %param.21) | copy-start | bytes 196612
  2.1 12.1 %copy-start.1 = (s32[8,48]{1,0:T(8,128)S(1)}, s32[8,48]{1,0:T(8,128)}, u32[]{:S(2)}) copy-start(s32[8,48]{1,0:T(8,128)} %par_ref.3) | copy-start | bytes 4612
  2.1 12.1 %copy-start.4 = (s32[8]{0:T(128)S(1)}, s32[8]{0:T(128)}, u32[]{:S(2)}) copy-start(s32[8]{0:T(128)} %len_ref.3) | copy-start | bytes 100
  7.5 12.1 %collective-permute-start = (bf16[8,48,1152]{2,1,0:T(8,128)(2,1)S(1)}, bf16[8,48,1152]{2,1,0:T(8,128)(2,1)S(1)}, u32[]{:S(2)}, u32[]{:S(2)}) collective-permute-start(bf16[8,48,1152]{2,1,0:T(8,128)(2,1)S(1)} %attend_theirs.1), channel_id=1, source_target_pairs={{0,1},{1,0},{2,3},{3,2},{4,5},{5,4},{6,7},{7,6},{8,9},{9,8},{10,11... | collective-permute-start | bytes 2654216 | tf_op jit(solution)/shard_map/ppermute | solution.py:295
  9.7 11.1 %all-to-all-start.2 = ((bf16[8,16,256]{2,1,0:T(8,128)(2,1)}), bf16[8,16,256]{2,1,0:T(8,128)(2,1)S(1)}, u32[]{:S(2)}, u32[]{:S(2)}) async-start(bf16[8,16,256]{2,1,0:T(8,128)(2,1)} %bitcast.10), calls=%async_computation.2 | async-start | bytes 131072 | tf_op jit(solution)/shard_map/all_to_all | solution.py:289
  20.7 22.3 %all-to-all-start = ((bf16[16,24,1152]{2,1,0:T(8,128)(2,1)}), bf16[16,24,1152]{2,1,0:T(8,128)(2,1)S(1)}, u32[]{:S(2)}, u32[]{:S(2)}) async-start(bf16[16,24,1152]{2,1,0:T(8,128)(2,1)} %bitcast.7), calls=%async_computation | async-start | bytes 1769472 | tf_op jit(solution)/shard_map/all_to_all | solution.py:298
  28.5 21.0 %collective-permute-start.1 = (bf16[128,256]{1,0:T(8,128)(2,1)S(1)}, bf16[128,256]{1,0:T(8,128)(2,1)S(1)}, u32[]{:S(2)}, u32[]{:S(2)}) collective-permute-start(bf16[128,256]{1,0:T(8,128)(2,1)S(1)} %bitcast.23), channel_id=1, source_target_pairs={{0,8},{8,16},{16,24},{24,0},{1,9},{9,17},{17,25},{25,1},{2,10},{10... | collective-permute-start | bytes 196616 | tf_op jit(solution)/shard_map/ppermute | solution.py:267
  29.8 19.6 %collective-permute-start.2 = (bf16[128,256]{1,0:T(8,128)(2,1)S(1)}, bf16[128,256]{1,0:T(8,128)(2,1)S(1)}, u32[]{:S(2)}, u32[]{:S(2)}) collective-permute-start(bf16[128,256]{1,0:T(8,128)(2,1)S(1)} %bitcast.24), channel_id=1, source_target_pairs={{0,16},{8,24},{16,0},{24,8},{1,17},{9,25},{17,1},{25,9},{2,18},{10... | collective-permute-start | bytes 196616 | tf_op jit(solution)/shard_map/ppermute | solution.py:267
  32.2 17.2 %collective-permute-start.3 = (bf16[128,256]{1,0:T(8,128)(2,1)S(1)}, bf16[128,256]{1,0:T(8,128)(2,1)S(1)}, u32[]{:S(2)}, u32[]{:S(2)}) collective-permute-start(bf16[128,256]{1,0:T(8,128)(2,1)S(1)} %bitcast.25), channel_id=1, source_target_pairs={{0,24},{8,0},{16,8},{24,16},{1,25},{9,1},{17,9},{25,17},{2,26},{10... | collective-permute-start | bytes 196616 | tf_op jit(solution)/shard_map/ppermute | solution.py:267
  44.0 21.5 %all-to-all-start.1 = ((bf16[8,8,24,128]{3,2,1,0:T(8,128)(2,1)}), bf16[8,8,24,128]{3,2,1,0:T(8,128)(2,1)S(1)}, u32[]{:S(2)}, u32[]{:S(2)}) async-start(bf16[8,8,24,128]{3,2,1,0:T(8,128)(2,1)} %combine.1), calls=%async_computation.1 | async-start | bytes 786432 | tf_op jit(solution)/shard_map/all_to_all | solution.py:300
  49.5 9.2 %collective-permute-start.4 = (bf16[4,128,256]{2,1,0:T(8,128)(2,1)S(1)}, bf16[4,128,256]{2,1,0:T(8,128)(2,1)S(1)}, u32[]{:S(2)}, u32[]{:S(2)}) collective-permute-start(bf16[4,128,256]{2,1,0:T(8,128)(2,1)S(1)} %pad_maximum_fusion.refs_0_), channel_id=1, source_target_pairs={{0,32},{32,64},{64,96},{96,0},{1,33},{33,65},{65,97},{97,1},{2,34}... | collective-permute-start | bytes 786440 | tf_op jit(solution)/shard_map/ppermute | solution.py:267
  50.9 14.5 %collective-permute-start.5 = (bf16[4,128,256]{2,1,0:T(8,128)(2,1)S(1)}, bf16[4,128,256]{2,1,0:T(8,128)(2,1)S(1)}, u32[]{:S(2)}, u32[]{:S(2)}) collective-permute-start(bf16[4,128,256]{2,1,0:T(8,128)(2,1)S(1)} %pad_maximum_fusion.refs_0_), channel_id=1, source_target_pairs={{0,64},{32,96},{64,0},{96,32},{1,65},{33,97},{65,1},{97,33},{2,66}... | collective-permute-start | bytes 786440 | tf_op jit(solution)/shard_map/ppermute | solution.py:267
  53.5 11.9 %collective-permute-start.6 = (bf16[4,128,256]{2,1,0:T(8,128)(2,1)S(1)}, bf16[4,128,256]{2,1,0:T(8,128)(2,1)S(1)}, u32[]{:S(2)}, u32[]{:S(2)}) collective-permute-start(bf16[4,128,256]{2,1,0:T(8,128)(2,1)S(1)} %pad_maximum_fusion.refs_0_), channel_id=1, source_target_pairs={{0,96},{32,0},{64,32},{96,64},{1,97},{33,1},{65,33},{97,65},{2,98}... | collective-permute-start | bytes 786440 | tf_op jit(solution)/shard_map/ppermute | solution.py:267
  83.8 4.5 %copy-start.5 = (bf16[16,96,256]{2,1,0:T(8,128)(2,1)}, bf16[16,96,256]{2,1,0:T(8,128)(2,1)S(1)}, u32[]{:S(2)}) copy-start(bf16[16,96,256]{2,1,0:T(8,128)(2,1)S(1)} %all_to_all.25) | copy-start | bytes 2359300
  83.8 4.5 %collective-permute-start.7 = (bf16[4,4,96,256]{3,2,1,0:T(8,128)(2,1)S(1)}, bf16[4,4,96,256]{3,2,1,0:T(8,128)(2,1)S(1)}, u32[]{:S(2)}, u32[]{:S(2)}) collective-permute-start(bf16[4,4,96,256]{3,2,1,0:T(8,128)(2,1)S(1)} %bitcast.20), channel_id=1, source_target_pairs={{0,1},{1,0},{2,3},{3,2},{4,5},{5,4},{6,7},{7,6},{8,9},{9,8},{10,11... | collective-permute-start | bytes 2359304 | tf_op jit(solution)/shard_map/ppermute | solution.py:303
  88.3 0.9 copy-start.6

commit v3 on v2

v3 whole, which is shorter than its diff:
```python
import functools

import jax
import jax.numpy as jnp
from jax import lax
from jax.experimental import pallas as pl
from jax.experimental.pallas import tpu as pltpu
from jax.sharding import Mesh, PartitionSpec as P

HEADS = 16
SINK = 4
BF = jnp.bfloat16
F32 = jnp.float32
NT = (((1,), (1,)), ((), ()))
TN = (((0,), (0,)), ((), ()))
CORE, FIRST, TREQ, Z, X, BLOCK, DP, BASE = range(8)
MB = 1 << 20


def attend_kernel(window, lane_off, info_ref, len_ref, par_ref, q_ref, k_ref, v_ref, nk_ref, nv_ref, *refs):
    step = pl.program_id(0)
    if len(refs) == 4:
        w_ref, out_ref, spread_ref, anc_ref = refs
        nz, nx, nc, _, block = spread_ref.shape

        @pl.when(step == 0)
        def _():
            for c in range(nc):
                for x in range(nx):
                    at = (c * nx + x) * block
                    for z in range(nz):
                        spread_ref[z, x, c] = w_ref[:, at:at + block]
    else:
        out_ref, anc_ref = refs
    first = info_ref[FIRST]
    treq = info_ref[TREQ]
    reqs, tree, width = q_ref.shape
    slots = k_ref.shape[1]
    heads = width // 128
    scale = 128 ** (-0.5) * 1.4426950408889634

    def attend(r, keys, values, mask):
        dens = []
        scores = [
            lax.dot_general(keys(h), q_ref[r, :, h * 128:(h + 1) * 128], NT, preferred_element_type=F32)
            for h in range(heads)
        ]
        exps = [jnp.where(mask, jnp.exp2(s * scale), 0.0) for s in scores]
        for h in range(heads):
            dens.append(jnp.sum(exps[h], axis=0, keepdims=True))
            o = lax.dot_general(exps[h].astype(BF), values(h), TN, preferred_element_type=F32)
            out_ref[r, :, h * 128:(h + 1) * 128] = o.astype(BF)
        dens = jnp.concatenate(dens, axis=0)
        high = dens.astype(BF).astype(F32)
        pieces = [high, dens - high, jnp.zeros((128 - lane_off - 2 * heads, tree), F32)]
        if lane_off:
            pieces = [jnp.zeros((lane_off, tree), F32)] + pieces
        out_ref[r, :, width:] = jnp.transpose(jnp.concatenate(pieces, axis=0)).astype(BF)

    @pl.when(treq < 0)
    def _():
        pos = first + lax.broadcasted_iota(jnp.int32, (slots, tree), 0)
        for r in range(reqs):
            length = len_ref[step * reqs + r]
            mask = (pos < length) & ((pos < SINK) | (pos >= length - window))
            attend(
                r, lambda h: k_ref[r, :, h * 128:(h + 1) * 128], lambda h: v_ref[r, :, h * 128:(h + 1) * 128], mask
            )

    @pl.when(treq >= 0)
    def _():
        out_ref[...] = jnp.zeros_like(out_ref)

        @pl.when(treq // reqs == step)
        def _():
            node = lax.broadcasted_iota(jnp.int32, (1, 128), 1)
            anc_ref[...] = jnp.zeros_like(anc_ref)
            anc_ref[0:1, :] = jnp.where(node == 0, 1.0, 0.0)

            def body(i, carry):
                up = anc_ref[pl.ds(par_ref[treq, i], 1), :]
                anc_ref[pl.ds(i, 1), :] = jnp.where(node == i, 1.0, up)
                return carry

            lax.fori_loop(1, tree, body, 0)
            mask = jnp.transpose(anc_ref[...])[:tree, :tree] > 0.5
            attend(
                lax.rem(treq, reqs), lambda h: nk_ref[0, :, h * 128:(h + 1) * 128],
                lambda h: nv_ref[0, :, h * 128:(h + 1) * 128], mask,
            )


def attend_half(window, mine, info, lengths, parents, q, k, v, nk, nv, w=None, spread=None):
    reqs, tree, width = q.shape
    slots = k.shape[1]
    half = width // 2
    group = reqs // 2
    hidx = (lambda i: i[CORE]) if mine else (lambda i: 1 - i[CORE])
    qs = pl.BlockSpec((group, tree, half), lambda r, i, l, p: (r, 0, hidx(i)))
    ks = pl.BlockSpec((group, slots, half), lambda r, i, l, p: (r, 0, hidx(i)))
    ns = pl.BlockSpec((1, tree, half), lambda r, i, l, p: (jnp.clip(i[TREQ], 0, reqs - 1), 0, hidx(i)))
    lengths, parents, q, k, v, nk, nv = (
        pltpu.with_memory_space_constraint(a, pltpu.HBM) for a in (lengths, parents, q, k, v, nk, nv)
    )
    in_specs = [qs, ks, ks, ns, ns]
    out_specs = [pl.BlockSpec((group, tree, half + 128), lambda r, i, l, p: (r, 0, 0))]
    out_shape = [jax.ShapeDtypeStruct((reqs, tree, half + 128), BF)]
    extra = ()
    if w is not None:
        extra = (pltpu.with_memory_space_constraint(w, pltpu.HBM),)
        in_specs.append(pl.BlockSpec(w.shape, lambda r, i, l, p: (0, 0)))
        out_specs.append(pl.BlockSpec(spread, lambda r, i, l, p: (0, 0, 0, 0, 0)))
        out_shape.append(jax.ShapeDtypeStruct(spread, w.dtype))
    return pl.pallas_call(
        functools.partial(attend_kernel, window, 16 if mine else 0),
        out_shape=out_shape,
        grid_spec=pltpu.PrefetchScalarGridSpec(
            num_scalar_prefetch=3,
            grid=(reqs // group,),
            in_specs=in_specs,
            out_specs=out_specs,
            scratch_shapes=[pltpu.VMEM((128, 128), F32)],
        ),
        compiler_params=pltpu.CompilerParams(vmem_limit_bytes=16 * MB),
        name="attend_mine" if mine else "attend_theirs",
    )(info, lengths, parents, q, k, v, nk, nv, *extra)


def combine_kernel(parts_ref, out_ref):
    width = out_ref.shape[1]
    heads = width // 128
    total = jnp.sum(parts_ref[...].astype(F32), axis=0)
    den = total[:, width:]
    lane = lax.broadcasted_iota(jnp.int32, den.shape, 1)
    for h in range(heads):
        d = jnp.sum(jnp.where((lane % heads == h) & (lane < 4 * heads), den, 0.0), axis=1, keepdims=True)
        cols = slice(h * 128, (h + 1) * 128)
        out_ref[:, cols] = (total[:, cols] / d).astype(BF)


def combine(parts):
    rows, cols = parts.shape[1], parts.shape[2]
    return pl.pallas_call(
        combine_kernel,
        out_shape=jax.ShapeDtypeStruct((rows, cols - 128), BF),
        compiler_params=pltpu.CompilerParams(vmem_limit_bytes=16 * MB),
        name="combine",
    )(parts)


def project_kernel(nx, info_ref, *refs):
    own, other = refs[:nx], refs[nx:2 * nx]
    ws, (res_ref, _, out_ref) = refs[2 * nx:-3], refs[-3:]
    core, x, y = info_ref[CORE], info_ref[X], info_ref[DP]
    rows, half = own[0].shape
    ny, deep = len(ws), ws[0].shape[0]
    mine = jnp.concatenate([own[s][...] for s in range(nx)], axis=0)
    theirs = jnp.concatenate([other[s][...] for s in range(nx)], axis=0)
    acc = None
    for s in range(ny):
        at = lax.rem(y + ny - s, ny)
        a = jnp.where(core == at // 2, mine, theirs)
        a = jnp.where(at % 2 == 0, a[:, :deep], a[:, deep:])
        part = jnp.dot(a, ws[s][...], preferred_element_type=F32)
        acc = part if acc is None else acc + part
    for s in range(nx):
        at = lax.rem(x + nx - s, nx)
        hid = (res_ref[at].astype(F32) + acc[s * rows:(s + 1) * rows]).astype(BF)
        for i in range(out_ref.shape[0]):
            out_ref[i, at] = hid


def project(info, own, other, ws, residual, after, copies):
    nx = len(own)
    rows, half = own[0].shape
    cols = ws[0].shape[1]
    part = pl.BlockSpec((rows, half), lambda g, i: (0, 0))
    residual = pltpu.with_memory_space_constraint(residual.reshape(-1, rows, residual.shape[2]), pltpu.HBM)
    return pl.pallas_call(
        functools.partial(project_kernel, nx),
        out_shape=jax.ShapeDtypeStruct((copies, nx, rows, cols), BF),
        grid_spec=pltpu.PrefetchScalarGridSpec(
            num_scalar_prefetch=1,
            grid=(1,),
            in_specs=[part] * (2 * nx)
            + [pl.BlockSpec(w.shape, lambda g, i: (0, 0)) for w in ws]
            + [pl.BlockSpec((nx, rows, cols), lambda g, i: (i[Z], 0, i[BLOCK]))]
            + [pl.BlockSpec(memory_space=pl.ANY)],
            out_specs=pl.BlockSpec((copies, nx, rows, cols), lambda g, i: (0, 0, 0, 0)),
        ),
        compiler_params=pltpu.CompilerParams(vmem_limit_bytes=16 * MB),
        name="project",
    )(info, *own, *other, *ws, residual, after)


def vocab_kernel(info_ref, mine_ref, theirs_ref, gain_ref, tok_ref, par_ref, w_ref, hid_out, stat_ref, hid_ref, x_ref, sem):
    core = info_ref[CORE]
    nz, nx, rows, cols = mine_ref.shape
    half = nx * cols
    for z in range(nz):
        rs = slice(z * rows, (z + 1) * rows)
        squares = jnp.zeros((rows, cols), F32)
        for x in range(nx):
            mine, theirs = mine_ref[z, x], theirs_ref[z, x]
            low = jnp.where(core == 0, mine, theirs)
            high = jnp.where(core == 0, theirs, mine)
            hid_ref[rs, x * cols:(x + 1) * cols] = low
            hid_ref[rs, half + x * cols:half + (x + 1) * cols] = high
            squares = squares + low.astype(F32) * low.astype(F32) + high.astype(F32) * high.astype(F32)
        inv = lax.rsqrt(jnp.sum(squares, axis=1, keepdims=True) / (2 * half) + 1e-06)
        for j in range(2 * nx):
            cs = slice(j * cols, (j + 1) * cols)
            x_ref[rs, cs] = (hid_ref[rs, cs].astype(F32) * inv * gain_ref[:, cs]).astype(BF)
    copy = pltpu.make_async_copy(hid_ref, hid_out, sem)
    copy.start()
    tokens = nz * rows
    reqs, tree = tok_ref.shape
    size = w_ref.shape[1]
    sums = jnp.zeros((tokens, 128), F32)
    pick1 = jnp.zeros((tokens, 128), F32)
    pick2 = jnp.zeros((tokens, 128), F32)
    pick0 = [jnp.zeros((8, 128), F32) for _ in range(reqs)]
    lane = lax.broadcasted_iota(jnp.int32, (tokens, 128), 1)
    base = info_ref[BASE]
    tok = jnp.concatenate([tok_ref[...].astype(F32), jnp.full((reqs, 128 - tree), -1.0, F32)], axis=1)
    tok = jnp.transpose(tok)
    column = lambda n: jnp.concatenate([tok[n:n + tree, r:r + 1] for r in range(reqs)], axis=0).astype(jnp.int32)
    t1 = column(1) - base - lane
    t2 = column(2) - base - lane
    node = lax.broadcasted_iota(jnp.int32, (8, 128), 0)
    t0 = [jnp.where(node == 0, tok[0:8, r:r + 1].astype(jnp.int32) - base - lane[:8], -1) for r in range(reqs)]
    for at in range(0, size, 256):
        step = min(256, size - at)
        logits = jnp.dot(x_ref[...], w_ref[:, at:at + step], preferred_element_type=F32)
        for o in range(0, step, 128):
            lg = logits[:, o:o + 128]
            sums = sums + jnp.exp(lg)
            pick1 = jnp.where(t1 == at + o, lg, pick1)
            pick2 = jnp.where(t2 == at + o, lg, pick2)
            for r in range(reqs):
                pick0[r] = jnp.where(t0[r] == at + o, lg[r * tree:r * tree + 8], pick0[r])
    zero = jnp.zeros((tree - 8, 128), F32)
    pick0 = jnp.concatenate([p for r in range(reqs) for p in (pick0[r], zero)], axis=0)

    def by_request(a):
        a = jnp.sum(jnp.transpose(a), axis=0, keepdims=True)
        return jnp.concatenate([a[:, r * tree:(r + 1) * tree] for r in range(reqs)], axis=0)

    def later(a, n):
        return jnp.concatenate([a[:, :n], a[:, :tree - n]], axis=1)

    total, pick1, pick2, pick0 = (by_request(a) for a in (sums, pick1, pick2, pick0))
    at_node = lax.broadcasted_iota(jnp.int32, (reqs, tree), 1)
    near = par_ref[...] == at_node - 1
    root = at_node == 0
    pick = jnp.where(root, pick0, jnp.where(near, later(pick1, 1), later(pick2, 2)))
    total = jnp.where(root, total, jnp.where(near, later(total, 1), later(total, 2)))
    gap = jnp.zeros((reqs, 64 - tree), F32)
    stats = jnp.concatenate([total, gap, pick, gap], axis=1)
    for i in range(stat_ref.shape[0]):
        stat_ref[i] = stats
    copy.wait()


def vocab(info, mine, theirs, gain, toks, parents, w, copies):
    nz, nx, rows, cols = mine.shape
    tokens, width = nz * rows, 2 * nx * cols
    vm = pl.BlockSpec(memory_space=pltpu.VMEM)
    return pl.pallas_call(
        vocab_kernel,
        out_shape=(
            jax.ShapeDtypeStruct((tokens, width), BF),
            jax.ShapeDtypeStruct((copies, toks.shape[0], 128), F32),
        ),
        in_specs=[pl.BlockSpec(memory_space=pltpu.SMEM), vm, vm, vm, vm, vm, vm],
        out_specs=(pl.BlockSpec(memory_space=pl.ANY), vm),
        scratch_shapes=[pltpu.VMEM((tokens, width), BF), pltpu.VMEM((tokens, width), BF), pltpu.SemaphoreType.DMA],
        compiler_params=pltpu.CompilerParams(vmem_limit_bytes=24 * MB),
        name="vocab",
    )(info, mine, theirs, gain, toks, parents, w)


def fetch_kernel(w_ref, after_ref, out_ref, sem):
    copy = pltpu.make_async_copy(w_ref, out_ref, sem)
    copy.start()
    copy.wait()


def fetch(w, after):
    hbm = pl.BlockSpec(memory_space=pl.ANY)
    return pl.pallas_call(
        fetch_kernel,
        out_shape=jax.ShapeDtypeStruct(w.shape, w.dtype),
        in_specs=[hbm, hbm],
        out_specs=pl.BlockSpec(memory_space=pltpu.VMEM),
        scratch_shapes=[pltpu.SemaphoreType.DMA],
        compiler_params=pltpu.CompilerParams(vmem_limit_bytes=2 * MB),
        name="fetch",
    )(pltpu.with_memory_space_constraint(w, pltpu.HBM), after)


def shifted(a, axis, step):
    n = lax.axis_size(axis)
    return lax.ppermute(a, axis, [(i, (i + step) % n) for i in range(n)])


def local(
    queries, new_keys, new_values, cache_keys, cache_values, lengths, parents,
    tree_tokens, residual, out_weight, norm_gain, vocab_weight,
):
    reqs, tree, width = queries.shape
    slots = cache_keys.shape[1]
    y, z, x, core = (lax.axis_index(a) for a in ("dp", "z", "x", "core"))
    ny, nz, nx, nc = (lax.axis_size(a) for a in ("dp", "z", "x", "core"))
    shard = (z * nx + x) * nc + core
    shards = nz * nx * nc
    window = slots * shards // 2
    half = width // nc
    block = half // nx
    tokens = reqs * tree
    swap = [(0, 1), (1, 0)]
    treq = jnp.where((shard >= reqs) & (shard < 2 * reqs), shard - reqs, -1)
    info = jnp.stack([core, shard * slots, treq, z, x, core * nx + x, y, shard * vocab_weight.shape[1]]).astype(jnp.int32)

    args = (lengths, parents, queries, cache_keys, cache_values, new_keys, new_values)
    send, w = attend_half(window, False, info, *args, out_weight, (nz, nx, nc, out_weight.shape[0], block))
    got = lax.ppermute(send, "core", swap)
    w = lax.all_to_all(w.reshape(shards, -1, block), ("z", "x", "core"), 0, 0).reshape(-1, block)
    ws = [w] + [shifted(w, "dp", s) for s in range(1, ny)]
    (keep,) = attend_half(window, True, info, *args)
    part = (keep + got).reshape(nz * nx, tokens // (nz * nx), half + 128)
    part = lax.all_to_all(part, ("z", "x"), 0, 0)
    att = combine(part)
    own = [att] + [shifted(att, "x", s) for s in range(1, nx)]
    other = [lax.ppermute(a, "core", swap) for a in own]
    scorer = fetch(vocab_weight, att)
    hid = project(info, own, other, ws, residual, scorer, nz * nx).reshape(nz * nx, -1, block)
    hid = lax.all_to_all(hid, ("z", "x"), 0, 0).reshape(nz, nx, -1, block)
    other = lax.ppermute(hid, "core", swap)
    hidden, stats = vocab(info, hid, other, norm_gain.reshape(1, -1), tree_tokens, parents, scorer, shards)
    stats = jnp.sum(lax.all_to_all(stats, ("z", "x", "core"), 0, 0), axis=0)
    logprob = stats[:, 64:64 + tree] - jnp.log(stats[:, :tree])
    return hidden.reshape(reqs, tree, width), logprob


def solution(mesh):
    sizes = (mesh.shape["dp"], 4, 4, 2)
    grid = Mesh(mesh.devices.reshape(sizes), ("dp", "z", "x", "core"))
    mp = ("z", "x", "core")
    row = P("dp", None, None)
    placed = (
        row, row, row, P("dp", mp, None), P("dp", mp, None), P("dp"), P("dp", None), P("dp", None), row,
        P(("dp",) + mp, None), P(), P(None, mp),
    )
    return jax.shard_map(local, mesh=grid, in_specs=placed, out_specs=(row, P("dp", None)), check_vma=False)
```

time: 111 us -> 99 us (0.89)
  waiting for transfers between devices: 21.8 us -> 14.9 us
  local copies, waits for them, and re-layouts: 4.34 us -> 0.1 us
  starting transfers between devices: 31.8 us -> 28.7 us
  Pallas kernels: 22.7 us -> 24.2 us
    ppermute x6, waiting for transfers between devices: 10.9 us -> 0.02 us  [shifted(): return lax.ppermute(a, axis, [(i, (i + step) % n) for i in range(n)])]
    ppermute x0 -> x4, starting transfers between devices: none -> 7.08 us  [local(): other = [lax.ppermute(a, 'core', swap) for a in own]]
    ppermute x6, starting transfers between devices: 10 us -> 6.57 us  [shifted(): return lax.ppermute(a, axis, [(i, (i + step) % n) for i in range(n)])]
    all_to_all x1, starting transfers between devices: 7.74 us -> 4.48 us  [local(): part = lax.all_to_all(part, ('z', 'x'), 0, 0)]
    unnamed x16 -> x6, local copies, waits for them, and re-layouts: 2.28 us -> 0.02 us
    all_to_all x2 -> x1, waiting for transfers between devices: 0.01 us -> 2.21 us  [local(): lax.all_to_all(w.reshape(shards, -1, block), ('z', 'x', 'core'), 0, 0)]
    all_to_all x2 -> x1, starting transfers between devices: 10 us -> 8.11 us  [local(): lax.all_to_all(w.reshape(shards, -1, block), ('z', 'x', 'core'), 0, 0)]
    ppermute x1, starting transfers between devices: 2.58 us -> 1.08 us  [local(): other = lax.ppermute(hid, 'core', swap)]
  transfers between devices with their start and end apart: 11 -> 14, of which waited for: 4 -> 3; matrix products, arithmetic and copies ran while one was open for 2% -> 1% of each run, Pallas kernels for 6% -> 10%
where the time goes in v3:
time: 99 us; the launch traced here: 98.5 us
  starting transfers between devices  28.7 us (29%)
  blocking collectives  27.9 us (28%)
  Pallas kernels  24.2 us (24%)
  waiting for transfers between devices  14.9 us (15%)
  other arithmetic  1.85 us (2%)
    all_to_all x1, blocking collectives, local(): hid = lax.all_to_all(hid, ('z', 'x'), 0, 0).reshape(nz, nx, -1, block)  17 us
    pallas_call x2, Pallas kernels, attend_half(): pl.pallas_call(functools.partial(attend_kernel, window, 16 if mine else 0...  11.8 us
    all_to_all x1, blocking collectives, local(): stats = jnp.sum(lax.all_to_all(stats, ('z', 'x', 'core'), 0, 0), axis=0)  10.9 us
    all_to_all x1, waiting for transfers between devices, local(): part = lax.all_to_all(part, ('z', 'x'), 0, 0)  10.7 us
    all_to_all x1, starting transfers between devices, local(): lax.all_to_all(w.reshape(shards, -1, block), ('z', 'x', 'core'), 0, 0)  8.11 us
    ppermute x4, starting transfers between devices, local(): other = [lax.ppermute(a, 'core', swap) for a in own]  7.08 us
    pallas_call x1, Pallas kernels, vocab(): pl.pallas_call(vocab_kernel, out_shape=(jax.ShapeDtypeStruct((tokens, wid...  6.71 us
    ppermute x6, starting transfers between devices, shifted(): return lax.ppermute(a, axis, [(i, (i + step) % n) for i in range(n)])  6.57 us
  transfers between devices with their start and end apart: 14, of which 3 were waited for; matrix products, arithmetic and copies ran while one was open for 1% of the time, Pallas kernels for 10%

profile of v3, /device:TPU:1, one launch (start us, length us, event | category | flops | bytes accessed | tf_op | source)
XLA Modules:
  0.0 98.5 jit_solution(2893239289037290260)
XLA Ops:
  0.6 0.1 stack.35.info_ref
  0.7 6.2 %attend_theirs.1 = (bf16[8,48,1152]{2,1,0:T(8,128)(2,1)S(1)}, bf16[4,4,2,16,256]{4,3,2,1,0:T(8,128)(2,1)}) custom-call(s32[8]{0:T(128)S(1)} %stack.35.info_ref, s32[8]{0:T(128)} %len_ref.3, s32[8,48]{1,0:T(8,128)} %par_ref.5, bf16[8,48,2048]{2,1,0:T(8,128)(2,1)} %q_ref.3, bf16[8,128,2048]{2,1,0:T(8,128)(2,1)} %k_ref.3, bf16[8,128,2048]{2,1,0:T(8,128)(2,1)} %v_ref.3, ...), custom_call_target="tpu_custom_call" | custom-call | tf_op jit(solution)/shard_map/attend_theirs/pallas_call | solution.py:114
  7.0 1.4 %collective-permute-start = (bf16[8,48,1152]{2,1,0:T(8,128)(2,1)S(1)}, bf16[8,48,1152]{2,1,0:T(8,128)(2,1)S(1)}, u32[]{:S(2)}, u32[]{:S(2)}) collective-permute-start(bf16[8,48,1152]{2,1,0:T(8,128)(2,1)S(1)} %get-tuple-element.6), channel_id=1, source_target_pairs={{0,1},{1,0},{2,3},{3,2},{4,5},{5,4},{6,7},{7,6},{8,9},{9,8},{10,11... | collective-permute-start | bytes 2654216 | tf_op jit(solution)/shard_map/ppermute | solution.py:327
  8.4 8.1 %all-to-all-start.1 = ((bf16[32,16,256]{2,1,0:T(8,128)(2,1)}), bf16[32,16,256]{2,1,0:T(8,128)(2,1)S(1)}, u32[]{:S(2)}, u32[]{:S(2)}) async-start(bf16[32,16,256]{2,1,0:T(8,128)(2,1)} %bitcast.9), calls=%async_computation.1 | async-start | bytes 524288 | tf_op jit(solution)/shard_map/all_to_all | solution.py:328
  16.5 5.5 %attend_mine.1 = bf16[8,48,1152]{2,1,0:T(8,128)(2,1)S(1)} custom-call(s32[8]{0:T(128)S(1)} %stack.35.info_ref, s32[8]{0:T(128)} %len_ref.3, s32[8,48]{1,0:T(8,128)} %par_ref.5, bf16[8,48,2048]{2,1,0:T(8,128)(2,1)} %q_ref.3, bf16[8,128,2048]{2,1,0:T(8,128)(2,1)} %k_ref.3, bf16[8,128,2048]{2,1,0:T(8,128)(2,1)} %v_ref.3, bf16[8,48,2048]{2,1,0:T(8,128)(2,1)} %nk_ref.3, ...), custom_call_target="tpu_custom_call" | custom-call | tf_op jit(solution)/shard_map/attend_mine/pallas_call | solution.py:114
  22.1 0.0 collective-permute-done
  22.1 1.1 %add.16 = bf16[8,48,1152]{2,1,0:T(8,128)(2,1)} add(bf16[8,48,1152]{2,1,0:T(8,128)(2,1)S(1)} %attend_mine.1, bf16[8,48,1152]{2,1,0:T(8,128)(2,1)S(1)} %collective-permute-done) | non-fusion elementwise | flops 442368 | bytes 2654208 | tf_op jit(solution)/shard_map/add | solution.py:331
  23.2 2.2 %all-to-all-done.1 = bf16[32,16,256]{2,1,0:T(8,128)(2,1)S(1)} async-done(((bf16[32,16,256]{2,1,0:T(8,128)(2,1)}), bf16[32,16,256]{2,1,0:T(8,128)(2,1)S(1)}, u32[]{:S(2)}, u32[]{:S(2)}) %all-to-all-start.1) | async-done | bytes 262176 | tf_op jit(solution)/shard_map/all_to_all | solution.py:328
  25.4 4.5 %all-to-all-start = ((bf16[16,24,1152]{2,1,0:T(8,128)(2,1)}), bf16[16,24,1152]{2,1,0:T(8,128)(2,1)S(1)}, u32[]{:S(2)}, u32[]{:S(2)}) async-start(bf16[16,24,1152]{2,1,0:T(8,128)(2,1)} %bitcast.8), calls=%async_computation | async-start | bytes 1769472 | tf_op jit(solution)/shard_map/all_to_all | solution.py:332
  29.9 2.8 %collective-permute-start.10 = (bf16[512,256]{1,0:T(8,128)(2,1)S(1)}, bf16[512,256]{1,0:T(8,128)(2,1)S(1)}, u32[]{:S(2)}, u32[]{:S(2)}) collective-permute-start(bf16[512,256]{1,0:T(8,128)(2,1)S(1)} %bitcast.19), channel_id=1, source_target_pairs={{0,96},{32,0},{64,32},{96,64},{1,97},{33,1},{65,33},{97,65},{2,98}... | collective-permute-start | bytes 786440 | tf_op jit(solution)/shard_map/ppermute | solution.py:304
  32.7 0.3 collective-permute-start.9
  33.1 0.7 collective-permute-start.8
  33.8 10.7 %all-to-all-done.parts_ref = bf16[16,24,1152]{2,1,0:T(8,128)(2,1)S(1)} async-done(((bf16[16,24,1152]{2,1,0:T(8,128)(2,1)}), bf16[16,24,1152]{2,1,0:T(8,128)(2,1)S(1)}, u32[]{:S(2)}, u32[]{:S(2)}) %all-to-all-start) | async-done | bytes 884768 | tf_op jit(solution)/shard_map/all_to_all | solution.py:332
  44.5 0.1 combine.1.after_ref.refs_0_
  44.6 1.0 collective-permute-start.3
  45.6 1.2 %collective-permute-start.2 = (bf16[24,1024]{1,0:T(8,128)(2,1)S(1)}, bf16[24,1024]{1,0:T(8,128)(2,1)S(1)}, u32[]{:S(2)}, u32[]{:S(2)}) collective-permute-start(bf16[24,1024]{1,0:T(8,128)(2,1)S(1)} %combine.1.after_ref.refs_0_), channel_id=1, source_target_pairs={{0,4},{2,6},{4,0},{6,2},{1,5},{3,7},{5,1},{7,3},{8,12},{10,14},{12... | collective-permute-start | bytes 147464 | tf_op jit(solution)/shard_map/ppermute | solution.py:304
  46.8 0.5 collective-permute-start.1
  47.4 1.9 %collective-permute-start.4 = (bf16[24,1024]{1,0:T(8,128)(2,1)S(1)}, bf16[24,1024]{1,0:T(8,128)(2,1)S(1)}, u32[]{:S(2)}, u32[]{:S(2)}) collective-permute-start(bf16[24,1024]{1,0:T(8,128)(2,1)S(1)} %combine.1.after_ref.refs_0_), channel_id=1, source_target_pairs={{0,1},{1,0},{2,3},{3,2},{4,5},{5,4},{6,7},{7,6},{8,9},{9,8},{10,11... | collective-permute-start | bytes 147464 | tf_op jit(solution)/shard_map/ppermute | solution.py:335
  49.2 1.4 %collective-permute-start.7 = (bf16[24,1024]{1,0:T(8,128)(2,1)S(1)}, bf16[24,1024]{1,0:T(8,128)(2,1)S(1)}, u32[]{:S(2)}, u32[]{:S(2)}) collective-permute-start(bf16[24,1024]{1,0:T(8,128)(2,1)S(1)} %collective-permute-done.3.refs_3_), channel_id=1, source_target_pairs={{0,1},{1,0},{2,3},{3,2},{4,5},{5,4},{6,7},{7,6},{8,9},{9,8},{10,11... | collective-permute-start | bytes 147464 | tf_op jit(solution)/shard_map/ppermute | solution.py:335
  50.7 1.9 %collective-permute-start.6 = (bf16[24,1024]{1,0:T(8,128)(2,1)S(1)}, bf16[24,1024]{1,0:T(8,128)(2,1)S(1)}, u32[]{:S(2)}, u32[]{:S(2)}) collective-permute-start(bf16[24,1024]{1,0:T(8,128)(2,1)S(1)} %collective-permute-done.2.refs_2_), channel_id=1, source_target_pairs={{0,1},{1,0},{2,3},{3,2},{4,5},{5,4},{6,7},{7,6},{8,9},{9,8},{10,11... | collective-permute-start | bytes 147464 | tf_op jit(solution)/shard_map/ppermute | solution.py:335
  52.6 1.9 %collective-permute-start.5 = (bf16[24,1024]{1,0:T(8,128)(2,1)S(1)}, bf16[24,1024]{1,0:T(8,128)(2,1)S(1)}, u32[]{:S(2)}, u32[]{:S(2)}) collective-permute-start(bf16[24,1024]{1,0:T(8,128)(2,1)S(1)} %collective-permute-done.1.refs_1_), channel_id=1, source_target_pairs={{0,1},{1,0},{2,3},{3,2},{4,5},{5,4},{6,7},{7,6},{8,9},{9,8},{10,11... | collective-permute-start | bytes 147464 | tf_op jit(solution)/shard_map/ppermute | solution.py:335
  54.5 3.8 %fetch.1.refs_13_.w_ref = bf16[2048,2432]{1,0:T(8,128)(2,1)S(1)} custom-call(bf16[2048,2432]{1,0:T(8,128)(2,1)} %w_ref.1, bf16[24,1024]{1,0:T(8,128)(2,1)S(1)} %combine.1.after_ref.refs_0_), custom_call_target="tpu_custom_call" | custom-call | tf_op jit(solution)/shard_map/fetch/pallas_call | solution.py:291
  58.4 1.7 %project.1 = bf16[16,4,24,256]{3,2,1,0:T(8,128)(2,1)S(1)} custom-call(s32[8]{0:T(128)S(1)} %stack.35.info_ref, bf16[24,1024]{1,0:T(8,128)(2,1)S(1)} %combine.1.after_ref.refs_0_, bf16[24,1024]{1,0:T(8,128)(2,1)S(1)} %collective-permute-done.1.refs_1_, bf16[24,1024]{1,0:T(8,128)(2,1)S(1)} %collective-permute-done.2.refs_2_, ...), custom_call_target="tpu_custom_call" | custom-call | tf_op jit(solution)/shard_map/project/pallas_call | solution.py:179
  60.1 0.0 copy-start
  60.1 0.0 copy-start.1
  60.1 0.0 copy-start.2
  60.1 17.0 %all_to_all.20 = bf16[16,96,256]{2,1,0:T(8,128)(2,1)S(1)} all-to-all(bf16[16,96,256]{2,1,0:T(8,128)(2,1)S(1)} %bitcast.18), channel_id=1, replica_groups=mesh['dp'=4,'z'=4,'x'=4,'core'=2] {'z','x'}, dimensions={0} | all-to-all | bytes 1572864 | tf_op jit(solution)/shard_map/all_to_all | solution.py:338
  77.1 1.1 %collective-permute-start.11 = (bf16[4,4,96,256]{3,2,1,0:T(8,128)(2,1)S(1)}, bf16[4,4,96,256]{3,2,1,0:T(8,128)(2,1)S(1)}, u32[]{:S(2)}, u32[]{:S(2)}) collective-permute-start(bf16[4,4,96,256]{3,2,1,0:T(8,128)(2,1)S(1)} %bitcast.16), channel_id=1, source_target_pairs={{0,1},{1,0},{2,3},{3,2},{4,5},{5,4},{6,7},{7,6},{8,9},{9,8},{10,11... | collective-permute-start | bytes 2359304 | tf_op jit(solution)/shard_map/ppermute | solution.py:339
  78.2 1.9 %collective-permute-done.11.theirs_ref = bf16[4,4,96,256]{3,2,1,0:T(8,128)(2,1)S(1)} collective-permute-done((bf16[4,4,96,256]{3,2,1,0:T(8,128)(2,1)S(1)}, bf16[4,4,96,256]{3,2,1,0:T(8,128)(2,1)S(1)}, u32[]{:S(2)}, u32[]{:S(2)}) %collective-permute-start.11) | collective-permute-done | bytes 786464 | tf_op jit(solution)/shard_map/ppermute | solution.py:339
  80.1 6.7 %vocab.1 = (bf16[384,2048]{1,0:T(8,128)(2,1)}, f32[32,8,128]{2,1,0:T(8,128)S(1)}) custom-call(s32[8]{0:T(128)S(1)} %stack.35.info_ref, bf16[4,4,96,256]{3,2,1,0:T(8,128)(2,1)S(1)} %bitcast.17, bf16[4,4,96,256]{3,2,1,0:T(8,128)(2,1)S(1)} %collective-permute-done.11.theirs_ref, f32[1,2048]{1,0:T(1,128)S(1)} %bitcast.23, s32[8,48]{1,0:T(8,128)S(1)} %copy-done.2, ...), custom_call_target="tpu_custom_call" | custom-call | tf_op jit(solution)/shard_map/vocab/pallas_call | solution.py:269
  86.8 10.9 %all_to_all.21 = f32[32,8,128]{2,1,0:T(8,128)S(1)} all-to-all(f32[32,8,128]{2,1,0:T(8,128)S(1)} %get-tuple-element.9), channel_id=1, replica_groups=mesh['dp'=4,'z'=4,'x'=4,'core'=2] {'z','x','core'}, dimensions={0} | all-to-all | bytes 262144 | tf_op jit(solution)/shard_map/all_to_all | solution.py:341
  97.8 0.7 log_subtract_fusion
  (14 shorter events, 0.1 us)
Async XLA Ops:
  7.0 15.1 %collective-permute-start = (bf16[8,48,1152]{2,1,0:T(8,128)(2,1)S(1)}, bf16[8,48,1152]{2,1,0:T(8,128)(2,1)S(1)}, u32[]{:S(2)}, u32[]{:S(2)}) collective-permute-start(bf16[8,48,1152]{2,1,0:T(8,128)(2,1)S(1)} %get-tuple-element.6), channel_id=1, source_target_pairs={{0,1},{1,0},{2,3},{3,2},{4,5},{5,4},{6,7},{7,6},{8,9},{9,8},{10,11... | collective-permute-start | bytes 2654216 | tf_op jit(solution)/shard_map/ppermute | solution.py:327
  8.4 17.0 %all-to-all-start.1 = ((bf16[32,16,256]{2,1,0:T(8,128)(2,1)}), bf16[32,16,256]{2,1,0:T(8,128)(2,1)S(1)}, u32[]{:S(2)}, u32[]{:S(2)}) async-start(bf16[32,16,256]{2,1,0:T(8,128)(2,1)} %bitcast.9), calls=%async_computation.1 | async-start | bytes 524288 | tf_op jit(solution)/shard_map/all_to_all | solution.py:328
  25.4 19.1 %all-to-all-start = ((bf16[16,24,1152]{2,1,0:T(8,128)(2,1)}), bf16[16,24,1152]{2,1,0:T(8,128)(2,1)S(1)}, u32[]{:S(2)}, u32[]{:S(2)}) async-start(bf16[16,24,1152]{2,1,0:T(8,128)(2,1)} %bitcast.8), calls=%async_computation | async-start | bytes 1769472 | tf_op jit(solution)/shard_map/all_to_all | solution.py:332
  29.9 16.9 %collective-permute-start.10 = (bf16[512,256]{1,0:T(8,128)(2,1)S(1)}, bf16[512,256]{1,0:T(8,128)(2,1)S(1)}, u32[]{:S(2)}, u32[]{:S(2)}) collective-permute-start(bf16[512,256]{1,0:T(8,128)(2,1)S(1)} %bitcast.19), channel_id=1, source_target_pairs={{0,96},{32,0},{64,32},{96,64},{1,97},{33,1},{65,33},{97,65},{2,98}... | collective-permute-start | bytes 786440 | tf_op jit(solution)/shard_map/ppermute | solution.py:304
  32.7 14.6 %collective-permute-start.9 = (bf16[512,256]{1,0:T(8,128)(2,1)S(1)}, bf16[512,256]{1,0:T(8,128)(2,1)S(1)}, u32[]{:S(2)}, u32[]{:S(2)}) collective-permute-start(bf16[512,256]{1,0:T(8,128)(2,1)S(1)} %bitcast.20), channel_id=1, source_target_pairs={{0,64},{32,96},{64,0},{96,32},{1,65},{33,97},{65,1},{97,33},{2,66}... | collective-permute-start | bytes 786440 | tf_op jit(solution)/shard_map/ppermute | solution.py:304
  33.1 25.2 %collective-permute-start.8 = (bf16[512,256]{1,0:T(8,128)(2,1)S(1)}, bf16[512,256]{1,0:T(8,128)(2,1)S(1)}, u32[]{:S(2)}, u32[]{:S(2)}) collective-permute-start(bf16[512,256]{1,0:T(8,128)(2,1)S(1)} %bitcast.21), channel_id=1, source_target_pairs={{0,32},{32,64},{64,96},{96,0},{1,33},{33,65},{65,97},{97,1},{2,34}... | collective-permute-start | bytes 786440 | tf_op jit(solution)/shard_map/ppermute | solution.py:304
  44.6 4.6 %collective-permute-start.3 = (bf16[24,1024]{1,0:T(8,128)(2,1)S(1)}, bf16[24,1024]{1,0:T(8,128)(2,1)S(1)}, u32[]{:S(2)}, u32[]{:S(2)}) collective-permute-start(bf16[24,1024]{1,0:T(8,128)(2,1)S(1)} %combine.1.after_ref.refs_0_), channel_id=1, source_target_pairs={{0,6},{2,0},{4,2},{6,4},{1,7},{3,1},{5,3},{7,5},{8,14},{10,8},{12,... | collective-permute-start | bytes 147464 | tf_op jit(solution)/shard_map/ppermute | solution.py:304
  45.6 5.1 %collective-permute-start.2 = (bf16[24,1024]{1,0:T(8,128)(2,1)S(1)}, bf16[24,1024]{1,0:T(8,128)(2,1)S(1)}, u32[]{:S(2)}, u32[]{:S(2)}) collective-permute-start(bf16[24,1024]{1,0:T(8,128)(2,1)S(1)} %combine.1.after_ref.refs_0_), channel_id=1, source_target_pairs={{0,4},{2,6},{4,0},{6,2},{1,5},{3,7},{5,1},{7,3},{8,12},{10,14},{12... | collective-permute-start | bytes 147464 | tf_op jit(solution)/shard_map/ppermute | solution.py:304
  46.8 5.8 %collective-permute-start.1 = (bf16[24,1024]{1,0:T(8,128)(2,1)S(1)}, bf16[24,1024]{1,0:T(8,128)(2,1)S(1)}, u32[]{:S(2)}, u32[]{:S(2)}) collective-permute-start(bf16[24,1024]{1,0:T(8,128)(2,1)S(1)} %combine.1.after_ref.refs_0_), channel_id=1, source_target_pairs={{0,2},{2,4},{4,6},{6,0},{1,3},{3,5},{5,7},{7,1},{8,10},{10,12},{12... | collective-permute-start | bytes 147464 | tf_op jit(solution)/shard_map/ppermute | solution.py:304
  47.4 10.9 %collective-permute-start.4 = (bf16[24,1024]{1,0:T(8,128)(2,1)S(1)}, bf16[24,1024]{1,0:T(8,128)(2,1)S(1)}, u32[]{:S(2)}, u32[]{:S(2)}) collective-permute-start(bf16[24,1024]{1,0:T(8,128)(2,1)S(1)} %combine.1.after_ref.refs_0_), channel_id=1, source_target_pairs={{0,1},{1,0},{2,3},{3,2},{4,5},{5,4},{6,7},{7,6},{8,9},{9,8},{10,11... | collective-permute-start | bytes 147464 | tf_op jit(solution)/shard_map/ppermute | solution.py:335
  49.2 9.1 %collective-permute-start.7 = (bf16[24,1024]{1,0:T(8,128)(2,1)S(1)}, bf16[24,1024]{1,0:T(8,128)(2,1)S(1)}, u32[]{:S(2)}, u32[]{:S(2)}) collective-permute-start(bf16[24,1024]{1,0:T(8,128)(2,1)S(1)} %collective-permute-done.3.refs_3_), channel_id=1, source_target_pairs={{0,1},{1,0},{2,3},{3,2},{4,5},{5,4},{6,7},{7,6},{8,9},{9,8},{10,11... | collective-permute-start | bytes 147464 | tf_op jit(solution)/shard_map/ppermute | solution.py:335
  50.7 7.7 %collective-permute-start.6 = (bf16[24,1024]{1,0:T(8,128)(2,1)S(1)}, bf16[24,1024]{1,0:T(8,128)(2,1)S(1)}, u32[]{:S(2)}, u32[]{:S(2)}) collective-permute-start(bf16[24,1024]{1,0:T(8,128)(2,1)S(1)} %collective-permute-done.2.refs_2_), channel_id=1, source_target_pairs={{0,1},{1,0},{2,3},{3,2},{4,5},{5,4},{6,7},{7,6},{8,9},{9,8},{10,11... | collective-permute-start | bytes 147464 | tf_op jit(solution)/shard_map/ppermute | solution.py:335
  52.6 5.8 %collective-permute-start.5 = (bf16[24,1024]{1,0:T(8,128)(2,1)S(1)}, bf16[24,1024]{1,0:T(8,128)(2,1)S(1)}, u32[]{:S(2)}, u32[]{:S(2)}) collective-permute-start(bf16[24,1024]{1,0:T(8,128)(2,1)S(1)} %collective-permute-done.1.refs_1_), channel_id=1, source_target_pairs={{0,1},{1,0},{2,3},{3,2},{4,5},{5,4},{6,7},{7,6},{8,9},{9,8},{10,11... | collective-permute-start | bytes 147464 | tf_op jit(solution)/shard_map/ppermute | solution.py:335
  60.1 20.0 %copy-start = (s32[8,48]{1,0:T(8,128)S(1)}, s32[8,48]{1,0:T(8,128)}, u32[]{:S(2)}) copy-start(s32[8,48]{1,0:T(8,128)} %par_ref.5) | copy-start | bytes 4612
  60.1 20.0 %copy-start.1 = (f32[2048]{0:T(1024)S(1)}, f32[2048]{0:T(1024)}, u32[]{:S(2)}) copy-start(f32[2048]{0:T(1024)} %param.22) | copy-start | bytes 24580
  60.1 20.0 %copy-start.2 = (s32[8,48]{1,0:T(8,128)S(1)}, s32[8,48]{1,0:T(8,128)}, u32[]{:S(2)}) copy-start(s32[8,48]{1,0:T(8,128)} %tok_ref.1) | copy-start | bytes 4612
  77.1 3.0 %collective-permute-start.11 = (bf16[4,4,96,256]{3,2,1,0:T(8,128)(2,1)S(1)}, bf16[4,4,96,256]{3,2,1,0:T(8,128)(2,1)S(1)}, u32[]{:S(2)}, u32[]{:S(2)}) collective-permute-start(bf16[4,4,96,256]{3,2,1,0:T(8,128)(2,1)S(1)} %bitcast.16), channel_id=1, source_target_pairs={{0,1},{1,0},{2,3},{3,2},{4,5},{5,4},{6,7},{7,6},{8,9},{9,8},{10,11... | collective-permute-start | bytes 2359304 | tf_op jit(solution)/shard_map/ppermute | solution.py:339

commit v4 on v3

--- a/solution.py
+++ b/solution.py
@@ -150,7 +150,7 @@
 
 def project_kernel(nx, info_ref, *refs):
     own, other = refs[:nx], refs[nx:2 * nx]
-    ws, (res_ref, _, out_ref) = refs[2 * nx:-3], refs[-3:]
+    ws, (res_ref, out_ref) = refs[2 * nx:-2], refs[-2:]
     core, x, y = info_ref[CORE], info_ref[X], info_ref[DP]
     rows, half = own[0].shape
     ny, deep = len(ws), ws[0].shape[0]
@@ -170,7 +170,7 @@
             out_ref[i, at] = hid
 
 
-def project(info, own, other, ws, residual, after, copies):
+def project(info, own, other, ws, residual, copies):
     nx = len(own)
     rows, half = own[0].shape
     cols = ws[0].shape[1]
@@ -184,16 +184,20 @@
             grid=(1,),
             in_specs=[part] * (2 * nx)
             + [pl.BlockSpec(w.shape, lambda g, i: (0, 0)) for w in ws]
-            + [pl.BlockSpec((nx, rows, cols), lambda g, i: (i[Z], 0, i[BLOCK]))]
-            + [pl.BlockSpec(memory_space=pl.ANY)],
+            + [pl.BlockSpec((nx, rows, cols), lambda g, i: (i[Z], 0, i[BLOCK]))],
             out_specs=pl.BlockSpec((copies, nx, rows, cols), lambda g, i: (0, 0, 0, 0)),
         ),
         compiler_params=pltpu.CompilerParams(vmem_limit_bytes=16 * MB),
         name="project",
-    )(info, *own, *other, *ws, residual, after)
-
-
-def vocab_kernel(info_ref, mine_ref, theirs_ref, gain_ref, tok_ref, par_ref, w_ref, hid_out, stat_ref, hid_ref, x_ref, sem):
+    )(info, *own, *other, *ws, residual)
+
+
+def vocab_kernel(
+    info_ref, mine_ref, theirs_ref, gain_ref, tok_ref, par_ref, w_ref, more_ref, hid_out, stat_ref, hid_ref, x_ref, rest_ref, sem
+):
+    lead, others = w_ref.shape[1], rest_ref.shape[1]
+    load = pltpu.make_async_copy(more_ref.at[:, pl.ds(lead, others)], rest_ref, sem.at[1])
+    load.start()
     core = info_ref[CORE]
     nz, nx, rows, cols = mine_ref.shape
     half = nx * cols
@@ -211,11 +215,10 @@
         for j in range(2 * nx):
             cs = slice(j * cols, (j + 1) * cols)
             x_ref[rs, cs] = (hid_ref[rs, cs].astype(F32) * inv * gain_ref[:, cs]).astype(BF)
-    copy = pltpu.make_async_copy(hid_ref, hid_out, sem)
+    copy = pltpu.make_async_copy(hid_ref, hid_out, sem.at[0])
     copy.start()
     tokens = nz * rows
     reqs, tree = tok_ref.shape
-    size = w_ref.shape[1]
     sums = jnp.zeros((tokens, 128), F32)
     pick1 = jnp.zeros((tokens, 128), F32)
     pick2 = jnp.zeros((tokens, 128), F32)
@@ -229,9 +232,12 @@
     t2 = column(2) - base - lane
     node = lax.broadcasted_iota(jnp.int32, (8, 128), 0)
     t0 = [jnp.where(node == 0, tok[0:8, r:r + 1].astype(jnp.int32) - base - lane[:8], -1) for r in range(reqs)]
-    for at in range(0, size, 256):
-        step = min(256, size - at)
-        logits = jnp.dot(x_ref[...], w_ref[:, at:at + step], preferred_element_type=F32)
+    parts = [(w_ref, at, min(256, lead - at), at) for at in range(0, lead, 256)]
+    parts += [(rest_ref, at, min(256, others - at), lead + at) for at in range(0, others, 256)]
+    for ref, start, step, at in parts:
+        if at == lead:
+            load.wait()
+        logits = jnp.dot(x_ref[...], ref[:, start:start + step], preferred_element_type=F32)
         for o in range(0, step, 128):
             lg = logits[:, o:o + 128]
             sums = sums + jnp.exp(lg)
@@ -262,7 +268,7 @@
     copy.wait()
 
 
-def vocab(info, mine, theirs, gain, toks, parents, w, copies):
+def vocab(info, mine, theirs, gain, toks, parents, lead, w, copies):
     nz, nx, rows, cols = mine.shape
     tokens, width = nz * rows, 2 * nx * cols
     vm = pl.BlockSpec(memory_space=pltpu.VMEM)
@@ -272,25 +278,30 @@
             jax.ShapeDtypeStruct((tokens, width), BF),
             jax.ShapeDtypeStruct((copies, toks.shape[0], 128), F32),
         ),
-        in_specs=[pl.BlockSpec(memory_space=pltpu.SMEM), vm, vm, vm, vm, vm, vm],
+        in_specs=[pl.BlockSpec(memory_space=pltpu.SMEM), vm, vm, vm, vm, vm, vm, pl.BlockSpec(memory_space=pl.ANY)],
         out_specs=(pl.BlockSpec(memory_space=pl.ANY), vm),
-        scratch_shapes=[pltpu.VMEM((tokens, width), BF), pltpu.VMEM((tokens, width), BF), pltpu.SemaphoreType.DMA],
+        scratch_shapes=[
+            pltpu.VMEM((tokens, width), BF),
+            pltpu.VMEM((tokens, width), BF),
+            pltpu.VMEM((width, w.shape[1] - lead.shape[1]), BF),
+            pltpu.SemaphoreType.DMA((2,)),
+        ],
         compiler_params=pltpu.CompilerParams(vmem_limit_bytes=24 * MB),
         name="vocab",
-    )(info, mine, theirs, gain, toks, parents, w)
+    )(info, mine, theirs, gain, toks, parents, lead, pltpu.with_memory_space_constraint(w, pltpu.HBM))
 
 
 def fetch_kernel(w_ref, after_ref, out_ref, sem):
-    copy = pltpu.make_async_copy(w_ref, out_ref, sem)
+    copy = pltpu.make_async_copy(w_ref.at[:, pl.ds(0, out_ref.shape[1])], out_ref, sem)
     copy.start()
     copy.wait()
 
 
-def fetch(w, after):
+def fetch(w, after, cols):
     hbm = pl.BlockSpec(memory_space=pl.ANY)
     return pl.pallas_call(
         fetch_kernel,
-        out_shape=jax.ShapeDtypeStruct(w.shape, w.dtype),
+        out_shape=jax.ShapeDtypeStruct((w.shape[0], cols), w.dtype),
         in_specs=[hbm, hbm],
         out_specs=pl.BlockSpec(memory_space=pltpu.VMEM),
         scratch_shapes=[pltpu.SemaphoreType.DMA],
@@ -333,11 +344,11 @@
     att = combine(part)
     own = [att] + [shifted(att, "x", s) for s in range(1, nx)]
     other = [lax.ppermute(a, "core", swap) for a in own]
-    scorer = fetch(vocab_weight, att)
-    hid = project(info, own, other, ws, residual, scorer, nz * nx).reshape(nz * nx, -1, block)
+    hid = project(info, own, other, ws, residual, nz * nx).reshape(nz * nx, -1, block)
     hid = lax.all_to_all(hid, ("z", "x"), 0, 0).reshape(nz, nx, -1, block)
     other = lax.ppermute(hid, "core", swap)
-    hidden, stats = vocab(info, hid, other, norm_gain.reshape(1, -1), tree_tokens, parents, scorer, shards)
+    scorer = fetch(vocab_weight, hid, 1024)
+    hidden, stats = vocab(info, hid, other, norm_gain.reshape(1, -1), tree_tokens, parents, scorer, vocab_weight, shards)
     stats = jnp.sum(lax.all_to_all(stats, ("z", "x", "core"), 0, 0), axis=0)
     logprob = stats[:, 64:64 + tree] - jnp.log(stats[:, :tree])
     return hidden.reshape(reqs, tree, width), logprob

time: 99 us -> 97.1 us (0.981)
  waiting for transfers between devices: 14.9 us -> 13.9 us
    ppermute x1, waiting for transfers between devices: 1.91 us -> 0.01 us  [local(): other = lax.ppermute(hid, 'core', swap)]
    pallas_call x1, Pallas kernels: 3.84 us -> 2.2 us  [fetch(): pl.pallas_call(fetch_kernel, out_shape=jax.ShapeDtypeStruct((w.shape[0],...]
    pallas_call x1, Pallas kernels: 6.71 us -> 7.89 us  [vocab(): pl.pallas_call(vocab_kernel, out_shape=(jax.ShapeDtypeStruct((tokens, wid...]
  transfers between devices with their start and end apart: 14 -> 14, of which waited for: 3 -> 3; matrix products, arithmetic and copies ran while one was open for 1% -> 1% of each run, Pallas kernels for 10% -> 8%
where the time goes in v4:
time: 97.1 us; the launch traced here: 96.5 us
  starting transfers between devices  28.8 us (30%)
  blocking collectives  27.4 us (28%)
  Pallas kernels  23.7 us (24%)
  waiting for transfers between devices  13.9 us (14%)
  other arithmetic  1.85 us (2%)
    all_to_all x1, blocking collectives, local(): hid = lax.all_to_all(hid, ('z', 'x'), 0, 0).reshape(nz, nx, -1, block)  16.7 us
    pallas_call x2, Pallas kernels, attend_half(): pl.pallas_call(functools.partial(attend_kernel, window, 16 if mine else 0...  11.8 us
    all_to_all x1, waiting for transfers between devices, local(): part = lax.all_to_all(part, ('z', 'x'), 0, 0)  10.8 us
    all_to_all x1, blocking collectives, local(): stats = jnp.sum(lax.all_to_all(stats, ('z', 'x', 'core'), 0, 0), axis=0)  10.7 us
    all_to_all x1, starting transfers between devices, local(): lax.all_to_all(w.reshape(shards, -1, block), ('z', 'x', 'core'), 0, 0)  8.12 us
    pallas_call x1, Pallas kernels, vocab(): pl.pallas_call(vocab_kernel, out_shape=(jax.ShapeDtypeStruct((tokens, wid...  7.89 us
    ppermute x4, starting transfers between devices, local(): other = [lax.ppermute(a, 'core', swap) for a in own]  7.08 us
    ppermute x6, starting transfers between devices, shifted(): return lax.ppermute(a, axis, [(i, (i + step) % n) for i in range(n)])  6.56 us
  transfers between devices with their start and end apart: 14, of which 3 were waited for; matrix products, arithmetic and copies ran while one was open for 1% of the time, Pallas kernels for 8%

profile of v4, /device:TPU:1, one launch (start us, length us, event | category | flops | bytes accessed | tf_op | source)
XLA Modules:
  0.0 96.5 jit_solution(1440674979882880788)
XLA Ops:
  0.6 0.1 stack.35.info_ref
  0.7 6.2 %attend_theirs.1 = (bf16[8,48,1152]{2,1,0:T(8,128)(2,1)S(1)}, bf16[4,4,2,16,256]{4,3,2,1,0:T(8,128)(2,1)}) custom-call(s32[8]{0:T(128)S(1)} %stack.35.info_ref, s32[8]{0:T(128)} %len_ref.3, s32[8,48]{1,0:T(8,128)} %par_ref.5, bf16[8,48,2048]{2,1,0:T(8,128)(2,1)} %q_ref.3, bf16[8,128,2048]{2,1,0:T(8,128)(2,1)} %k_ref.3, bf16[8,128,2048]{2,1,0:T(8,128)(2,1)} %v_ref.3, ...), custom_call_target="tpu_custom_call" | custom-call | tf_op jit(solution)/shard_map/attend_theirs/pallas_call | solution.py:114
  7.0 1.4 %collective-permute-start = (bf16[8,48,1152]{2,1,0:T(8,128)(2,1)S(1)}, bf16[8,48,1152]{2,1,0:T(8,128)(2,1)S(1)}, u32[]{:S(2)}, u32[]{:S(2)}) collective-permute-start(bf16[8,48,1152]{2,1,0:T(8,128)(2,1)S(1)} %get-tuple-element.6), channel_id=1, source_target_pairs={{0,1},{1,0},{2,3},{3,2},{4,5},{5,4},{6,7},{7,6},{8,9},{9,8},{10,11... | collective-permute-start | bytes 2654216 | tf_op jit(solution)/shard_map/ppermute | solution.py:338
  8.4 8.1 %all-to-all-start.1 = ((bf16[32,16,256]{2,1,0:T(8,128)(2,1)}), bf16[32,16,256]{2,1,0:T(8,128)(2,1)S(1)}, u32[]{:S(2)}, u32[]{:S(2)}) async-start(bf16[32,16,256]{2,1,0:T(8,128)(2,1)} %bitcast.9), calls=%async_computation.1 | async-start | bytes 524288 | tf_op jit(solution)/shard_map/all_to_all | solution.py:339
  16.5 5.5 %attend_mine.1 = bf16[8,48,1152]{2,1,0:T(8,128)(2,1)S(1)} custom-call(s32[8]{0:T(128)S(1)} %stack.35.info_ref, s32[8]{0:T(128)} %len_ref.3, s32[8,48]{1,0:T(8,128)} %par_ref.5, bf16[8,48,2048]{2,1,0:T(8,128)(2,1)} %q_ref.3, bf16[8,128,2048]{2,1,0:T(8,128)(2,1)} %k_ref.3, bf16[8,128,2048]{2,1,0:T(8,128)(2,1)} %v_ref.3, bf16[8,48,2048]{2,1,0:T(8,128)(2,1)} %nk_ref.3, ...), custom_call_target="tpu_custom_call" | custom-call | tf_op jit(solution)/shard_map/attend_mine/pallas_call | solution.py:114
  22.1 1.1 %add.16 = bf16[8,48,1152]{2,1,0:T(8,128)(2,1)} add(bf16[8,48,1152]{2,1,0:T(8,128)(2,1)S(1)} %attend_mine.1, bf16[8,48,1152]{2,1,0:T(8,128)(2,1)S(1)} %collective-permute-done) | non-fusion elementwise | flops 442368 | bytes 2654208 | tf_op jit(solution)/shard_map/add | solution.py:342
  23.2 2.2 %all-to-all-done.1 = bf16[32,16,256]{2,1,0:T(8,128)(2,1)S(1)} async-done(((bf16[32,16,256]{2,1,0:T(8,128)(2,1)}), bf16[32,16,256]{2,1,0:T(8,128)(2,1)S(1)}, u32[]{:S(2)}, u32[]{:S(2)}) %all-to-all-start.1) | async-done | bytes 262176 | tf_op jit(solution)/shard_map/all_to_all | solution.py:339
  25.4 4.5 %all-to-all-start = ((bf16[16,24,1152]{2,1,0:T(8,128)(2,1)}), bf16[16,24,1152]{2,1,0:T(8,128)(2,1)S(1)}, u32[]{:S(2)}, u32[]{:S(2)}) async-start(bf16[16,24,1152]{2,1,0:T(8,128)(2,1)} %bitcast.8), calls=%async_computation | async-start | bytes 1769472 | tf_op jit(solution)/shard_map/all_to_all | solution.py:343
  29.9 2.8 %collective-permute-start.10 = (bf16[512,256]{1,0:T(8,128)(2,1)S(1)}, bf16[512,256]{1,0:T(8,128)(2,1)S(1)}, u32[]{:S(2)}, u32[]{:S(2)}) collective-permute-start(bf16[512,256]{1,0:T(8,128)(2,1)S(1)} %bitcast.20), channel_id=1, source_target_pairs={{0,96},{32,0},{64,32},{96,64},{1,97},{33,1},{65,33},{97,65},{2,98}... | collective-permute-start | bytes 786440 | tf_op jit(solution)/shard_map/ppermute | solution.py:315
  32.7 0.4 collective-permute-start.9
  33.1 0.7 collective-permute-start.8
  33.8 10.8 %all-to-all-done.parts_ref = bf16[16,24,1152]{2,1,0:T(8,128)(2,1)S(1)} async-done(((bf16[16,24,1152]{2,1,0:T(8,128)(2,1)}), bf16[16,24,1152]{2,1,0:T(8,128)(2,1)S(1)}, u32[]{:S(2)}, u32[]{:S(2)}) %all-to-all-start) | async-done | bytes 884768 | tf_op jit(solution)/shard_map/all_to_all | solution.py:343
  44.5 0.1 combine.1.refs_0_
  44.6 1.0 collective-permute-start.3
  45.6 1.2 %collective-permute-start.2 = (bf16[24,1024]{1,0:T(8,128)(2,1)S(1)}, bf16[24,1024]{1,0:T(8,128)(2,1)S(1)}, u32[]{:S(2)}, u32[]{:S(2)}) collective-permute-start(bf16[24,1024]{1,0:T(8,128)(2,1)S(1)} %combine.1.refs_0_), channel_id=1, source_target_pairs={{0,4},{2,6},{4,0},{6,2},{1,5},{3,7},{5,1},{7,3},{8,12},{10,14},{12... | collective-permute-start | bytes 147464 | tf_op jit(solution)/shard_map/ppermute | solution.py:315
  46.8 0.0 collective-permute-done.10.refs_11_
  46.8 0.5 collective-permute-start.1
  47.4 1.9 %collective-permute-start.4 = (bf16[24,1024]{1,0:T(8,128)(2,1)S(1)}, bf16[24,1024]{1,0:T(8,128)(2,1)S(1)}, u32[]{:S(2)}, u32[]{:S(2)}) collective-permute-start(bf16[24,1024]{1,0:T(8,128)(2,1)S(1)} %combine.1.refs_0_), channel_id=1, source_target_pairs={{0,1},{1,0},{2,3},{3,2},{4,5},{5,4},{6,7},{7,6},{8,9},{9,8},{10,11... | collective-permute-start | bytes 147464 | tf_op jit(solution)/shard_map/ppermute | solution.py:346
  49.3 0.0 collective-permute-done.3.refs_3_
  49.3 1.4 %collective-permute-start.7 = (bf16[24,1024]{1,0:T(8,128)(2,1)S(1)}, bf16[24,1024]{1,0:T(8,128)(2,1)S(1)}, u32[]{:S(2)}, u32[]{:S(2)}) collective-permute-start(bf16[24,1024]{1,0:T(8,128)(2,1)S(1)} %collective-permute-done.3.refs_3_), channel_id=1, source_target_pairs={{0,1},{1,0},{2,3},{3,2},{4,5},{5,4},{6,7},{7,6},{8,9},{9,8},{10,11... | collective-permute-start | bytes 147464 | tf_op jit(solution)/shard_map/ppermute | solution.py:346
  50.7 0.0 collective-permute-done.2.refs_2_
  50.7 1.9 %collective-permute-start.6 = (bf16[24,1024]{1,0:T(8,128)(2,1)S(1)}, bf16[24,1024]{1,0:T(8,128)(2,1)S(1)}, u32[]{:S(2)}, u32[]{:S(2)}) collective-permute-start(bf16[24,1024]{1,0:T(8,128)(2,1)S(1)} %collective-permute-done.2.refs_2_), channel_id=1, source_target_pairs={{0,1},{1,0},{2,3},{3,2},{4,5},{5,4},{6,7},{7,6},{8,9},{9,8},{10,11... | collective-permute-start | bytes 147464 | tf_op jit(solution)/shard_map/ppermute | solution.py:346
  52.6 1.9 %collective-permute-start.5 = (bf16[24,1024]{1,0:T(8,128)(2,1)S(1)}, bf16[24,1024]{1,0:T(8,128)(2,1)S(1)}, u32[]{:S(2)}, u32[]{:S(2)}) collective-permute-start(bf16[24,1024]{1,0:T(8,128)(2,1)S(1)} %collective-permute-done.1.refs_1_), channel_id=1, source_target_pairs={{0,1},{1,0},{2,3},{3,2},{4,5},{5,4},{6,7},{7,6},{8,9},{9,8},{10,11... | collective-permute-start | bytes 147464 | tf_op jit(solution)/shard_map/ppermute | solution.py:346
  54.5 0.0 collective-permute-done.8.refs_9_
  54.5 0.9 collective-permute-done.5.refs_5_
  55.3 1.7 %project.1 = bf16[16,4,24,256]{3,2,1,0:T(8,128)(2,1)S(1)} custom-call(s32[8]{0:T(128)S(1)} %stack.35.info_ref, bf16[24,1024]{1,0:T(8,128)(2,1)S(1)} %combine.1.refs_0_, bf16[24,1024]{1,0:T(8,128)(2,1)S(1)} %collective-permute-done.1.refs_1_, bf16[24,1024]{1,0:T(8,128)(2,1)S(1)} %collective-permute-done.2.refs_2_, ...), custom_call_target="tpu_custom_call" | custom-call | tf_op jit(solution)/shard_map/project/pallas_call | solution.py:179
  57.1 16.7 %all_to_all.20 = bf16[16,96,256]{2,1,0:T(8,128)(2,1)S(1)} all-to-all(bf16[16,96,256]{2,1,0:T(8,128)(2,1)S(1)} %bitcast.19), channel_id=1, replica_groups=mesh['dp'=4,'z'=4,'x'=4,'core'=2] {'z','x'}, dimensions={0} | all-to-all | bytes 1572864 | tf_op jit(solution)/shard_map/all_to_all | solution.py:348
  73.8 1.2 %collective-permute-start.11 = (bf16[4,4,96,256]{3,2,1,0:T(8,128)(2,1)S(1)}, bf16[4,4,96,256]{3,2,1,0:T(8,128)(2,1)S(1)}, u32[]{:S(2)}, u32[]{:S(2)}) collective-permute-start(bf16[4,4,96,256]{3,2,1,0:T(8,128)(2,1)S(1)} %bitcast.16), channel_id=1, source_target_pairs={{0,1},{1,0},{2,3},{3,2},{4,5},{5,4},{6,7},{7,6},{8,9},{9,8},{10,11... | collective-permute-start | bytes 2359304 | tf_op jit(solution)/shard_map/ppermute | solution.py:349
  75.0 2.2 %fetch.1.w_ref = bf16[2048,1024]{1,0:T(8,128)(2,1)S(1)} custom-call(bf16[2048,2432]{1,0:T(8,128)(2,1)} %more_ref.1, bf16[4,4,96,256]{3,2,1,0:T(8,128)(2,1)S(1)} %bitcast.17), custom_call_target="tpu_custom_call" | custom-call | tf_op jit(solution)/shard_map/fetch/pallas_call | solution.py:302
  77.2 7.9 %vocab.1 = (bf16[384,2048]{1,0:T(8,128)(2,1)}, f32[32,8,128]{2,1,0:T(8,128)S(1)}) custom-call(s32[8]{0:T(128)S(1)} %stack.35.info_ref, bf16[4,4,96,256]{3,2,1,0:T(8,128)(2,1)S(1)} %bitcast.18, bf16[4,4,96,256]{3,2,1,0:T(8,128)(2,1)S(1)} %collective-permute-done.11.theirs_ref, f32[1,2048]{1,0:T(1,128)S(1)} %bitcast.24, s32[8,48]{1,0:T(8,128)S(1)} %copy-done.2, ...), custom_call_target="tpu_custom_call" | custom-call | tf_op jit(solution)/shard_map/vocab/pallas_call | solution.py:275
  85.1 10.7 %all_to_all.21 = f32[32,8,128]{2,1,0:T(8,128)S(1)} all-to-all(f32[32,8,128]{2,1,0:T(8,128)S(1)} %get-tuple-element.9), channel_id=1, replica_groups=mesh['dp'=4,'z'=4,'x'=4,'core'=2] {'z','x','core'}, dimensions={0} | all-to-all | bytes 262144 | tf_op jit(solution)/shard_map/all_to_all | solution.py:352
  95.9 0.7 log_subtract_fusion
  (14 shorter events, 0.1 us)
Async XLA Ops:
  7.0 15.1 %collective-permute-start = (bf16[8,48,1152]{2,1,0:T(8,128)(2,1)S(1)}, bf16[8,48,1152]{2,1,0:T(8,128)(2,1)S(1)}, u32[]{:S(2)}, u32[]{:S(2)}) collective-permute-start(bf16[8,48,1152]{2,1,0:T(8,128)(2,1)S(1)} %get-tuple-element.6), channel_id=1, source_target_pairs={{0,1},{1,0},{2,3},{3,2},{4,5},{5,4},{6,7},{7,6},{8,9},{9,8},{10,11... | collective-permute-start | bytes 2654216 | tf_op jit(solution)/shard_map/ppermute | solution.py:338
  8.4 17.0 %all-to-all-start.1 = ((bf16[32,16,256]{2,1,0:T(8,128)(2,1)}), bf16[32,16,256]{2,1,0:T(8,128)(2,1)S(1)}, u32[]{:S(2)}, u32[]{:S(2)}) async-start(bf16[32,16,256]{2,1,0:T(8,128)(2,1)} %bitcast.9), calls=%async_computation.1 | async-start | bytes 524288 | tf_op jit(solution)/shard_map/all_to_all | solution.py:339
  25.4 19.1 %all-to-all-start = ((bf16[16,24,1152]{2,1,0:T(8,128)(2,1)}), bf16[16,24,1152]{2,1,0:T(8,128)(2,1)S(1)}, u32[]{:S(2)}, u32[]{:S(2)}) async-start(bf16[16,24,1152]{2,1,0:T(8,128)(2,1)} %bitcast.8), calls=%async_computation | async-start | bytes 1769472 | tf_op jit(solution)/shard_map/all_to_all | solution.py:343
  29.9 16.9 %collective-permute-start.10 = (bf16[512,256]{1,0:T(8,128)(2,1)S(1)}, bf16[512,256]{1,0:T(8,128)(2,1)S(1)}, u32[]{:S(2)}, u32[]{:S(2)}) collective-permute-start(bf16[512,256]{1,0:T(8,128)(2,1)S(1)} %bitcast.20), channel_id=1, source_target_pairs={{0,96},{32,0},{64,32},{96,64},{1,97},{33,1},{65,33},{97,65},{2,98}... | collective-permute-start | bytes 786440 | tf_op jit(solution)/shard_map/ppermute | solution.py:315
  32.7 14.7 %collective-permute-start.9 = (bf16[512,256]{1,0:T(8,128)(2,1)S(1)}, bf16[512,256]{1,0:T(8,128)(2,1)S(1)}, u32[]{:S(2)}, u32[]{:S(2)}) collective-permute-start(bf16[512,256]{1,0:T(8,128)(2,1)S(1)} %bitcast.21), channel_id=1, source_target_pairs={{0,64},{32,96},{64,0},{96,32},{1,65},{33,97},{65,1},{97,33},{2,66}... | collective-permute-start | bytes 786440 | tf_op jit(solution)/shard_map/ppermute | solution.py:315
  33.1 21.4 %collective-permute-start.8 = (bf16[512,256]{1,0:T(8,128)(2,1)S(1)}, bf16[512,256]{1,0:T(8,128)(2,1)S(1)}, u32[]{:S(2)}, u32[]{:S(2)}) collective-permute-start(bf16[512,256]{1,0:T(8,128)(2,1)S(1)} %bitcast.22), channel_id=1, source_target_pairs={{0,32},{32,64},{64,96},{96,0},{1,33},{33,65},{65,97},{97,1},{2,34}... | collective-permute-start | bytes 786440 | tf_op jit(solution)/shard_map/ppermute | solution.py:315
  44.6 4.6 %collective-permute-start.3 = (bf16[24,1024]{1,0:T(8,128)(2,1)S(1)}, bf16[24,1024]{1,0:T(8,128)(2,1)S(1)}, u32[]{:S(2)}, u32[]{:S(2)}) collective-permute-start(bf16[24,1024]{1,0:T(8,128)(2,1)S(1)} %combine.1.refs_0_), channel_id=1, source_target_pairs={{0,6},{2,0},{4,2},{6,4},{1,7},{3,1},{5,3},{7,5},{8,14},{10,8},{12,... | collective-permute-start | bytes 147464 | tf_op jit(solution)/shard_map/ppermute | solution.py:315
  45.6 5.1 %collective-permute-start.2 = (bf16[24,1024]{1,0:T(8,128)(2,1)S(1)}, bf16[24,1024]{1,0:T(8,128)(2,1)S(1)}, u32[]{:S(2)}, u32[]{:S(2)}) collective-permute-start(bf16[24,1024]{1,0:T(8,128)(2,1)S(1)} %combine.1.refs_0_), channel_id=1, source_target_pairs={{0,4},{2,6},{4,0},{6,2},{1,5},{3,7},{5,1},{7,3},{8,12},{10,14},{12... | collective-permute-start | bytes 147464 | tf_op jit(solution)/shard_map/ppermute | solution.py:315
  46.8 5.8 %collective-permute-start.1 = (bf16[24,1024]{1,0:T(8,128)(2,1)S(1)}, bf16[24,1024]{1,0:T(8,128)(2,1)S(1)}, u32[]{:S(2)}, u32[]{:S(2)}) collective-permute-start(bf16[24,1024]{1,0:T(8,128)(2,1)S(1)} %combine.1.refs_0_), channel_id=1, source_target_pairs={{0,2},{2,4},{4,6},{6,0},{1,3},{3,5},{5,7},{7,1},{8,10},{10,12},{12... | collective-permute-start | bytes 147464 | tf_op jit(solution)/shard_map/ppermute | solution.py:315
  47.4 7.1 %collective-permute-start.4 = (bf16[24,1024]{1,0:T(8,128)(2,1)S(1)}, bf16[24,1024]{1,0:T(8,128)(2,1)S(1)}, u32[]{:S(2)}, u32[]{:S(2)}) collective-permute-start(bf16[24,1024]{1,0:T(8,128)(2,1)S(1)} %combine.1.refs_0_), channel_id=1, source_target_pairs={{0,1},{1,0},{2,3},{3,2},{4,5},{5,4},{6,7},{7,6},{8,9},{9,8},{10,11... | collective-permute-start | bytes 147464 | tf_op jit(solution)/shard_map/ppermute | solution.py:346
  49.3 5.2 %collective-permute-start.7 = (bf16[24,1024]{1,0:T(8,128)(2,1)S(1)}, bf16[24,1024]{1,0:T(8,128)(2,1)S(1)}, u32[]{:S(2)}, u32[]{:S(2)}) collective-permute-start(bf16[24,1024]{1,0:T(8,128)(2,1)S(1)} %collective-permute-done.3.refs_3_), channel_id=1, source_target_pairs={{0,1},{1,0},{2,3},{3,2},{4,5},{5,4},{6,7},{7,6},{8,9},{9,8},{10,11... | collective-permute-start | bytes 147464 | tf_op jit(solution)/shard_map/ppermute | solution.py:346
  50.7 3.8 %collective-permute-start.6 = (bf16[24,1024]{1,0:T(8,128)(2,1)S(1)}, bf16[24,1024]{1,0:T(8,128)(2,1)S(1)}, u32[]{:S(2)}, u32[]{:S(2)}) collective-permute-start(bf16[24,1024]{1,0:T(8,128)(2,1)S(1)} %collective-permute-done.2.refs_2_), channel_id=1, source_target_pairs={{0,1},{1,0},{2,3},{3,2},{4,5},{5,4},{6,7},{7,6},{8,9},{9,8},{10,11... | collective-permute-start | bytes 147464 | tf_op jit(solution)/shard_map/ppermute | solution.py:346
  52.6 2.8 %collective-permute-start.5 = (bf16[24,1024]{1,0:T(8,128)(2,1)S(1)}, bf16[24,1024]{1,0:T(8,128)(2,1)S(1)}, u32[]{:S(2)}, u32[]{:S(2)}) collective-permute-start(bf16[24,1024]{1,0:T(8,128)(2,1)S(1)} %collective-permute-done.1.refs_1_), channel_id=1, source_target_pairs={{0,1},{1,0},{2,3},{3,2},{4,5},{5,4},{6,7},{7,6},{8,9},{9,8},{10,11... | collective-permute-start | bytes 147464 | tf_op jit(solution)/shard_map/ppermute | solution.py:346
  73.8 3.4 %copy-start = (s32[8,48]{1,0:T(8,128)S(1)}, s32[8,48]{1,0:T(8,128)}, u32[]{:S(2)}) copy-start(s32[8,48]{1,0:T(8,128)} %par_ref.5) | copy-start | bytes 4612
  73.8 3.4 %copy-start.1 = (f32[2048]{0:T(1024)S(1)}, f32[2048]{0:T(1024)}, u32[]{:S(2)}) copy-start(f32[2048]{0:T(1024)} %param.22) | copy-start | bytes 24580
  73.8 3.4 %copy-start.2 = (s32[8,48]{1,0:T(8,128)S(1)}, s32[8,48]{1,0:T(8,128)}, u32[]{:S(2)}) copy-start(s32[8,48]{1,0:T(8,128)} %tok_ref.1) | copy-start | bytes 4612
  73.8 3.4 %collective-permute-start.11 = (bf16[4,4,96,256]{3,2,1,0:T(8,128)(2,1)S(1)}, bf16[4,4,96,256]{3,2,1,0:T(8,128)(2,1)S(1)}, u32[]{:S(2)}, u32[]{:S(2)}) collective-permute-start(bf16[4,4,96,256]{3,2,1,0:T(8,128)(2,1)S(1)} %bitcast.16), channel_id=1, source_target_pairs={{0,1},{1,0},{2,3},{3,2},{4,5},{5,4},{6,7},{7,6},{8,9},{9,8},{10,11... | collective-permute-start | bytes 2359304 | tf_op jit(solution)/shard_map/ppermute | solution.py:349

commit v5 on v4

--- a/solution.py
+++ b/solution.py
@@ -17,9 +17,11 @@
 MB = 1 << 20
 
 
-def attend_kernel(window, lane_off, info_ref, len_ref, par_ref, q_ref, k_ref, v_ref, nk_ref, nv_ref, *refs):
+def attend_kernel(window, add, info_ref, len_ref, par_ref, q_ref, k_ref, v_ref, nk_ref, nv_ref, *refs):
     step = pl.program_id(0)
-    if len(refs) == 4:
+    if add:
+        got_ref, out_ref, anc_ref = refs
+    else:
         w_ref, out_ref, spread_ref, anc_ref = refs
         nz, nx, nc, _, block = spread_ref.shape
 
@@ -30,46 +32,67 @@
                     at = (c * nx + x) * block
                     for z in range(nz):
                         spread_ref[z, x, c] = w_ref[:, at:at + block]
-    else:
-        out_ref, anc_ref = refs
+
     first = info_ref[FIRST]
     treq = info_ref[TREQ]
     reqs, tree, width = q_ref.shape
     slots = k_ref.shape[1]
     heads = width // 128
+    part = tree // 2
     scale = 128 ** (-0.5) * 1.4426950408889634
-
-    def attend(r, keys, values, mask):
-        dens = []
-        scores = [
-            lax.dot_general(keys(h), q_ref[r, :, h * 128:(h + 1) * 128], NT, preferred_element_type=F32)
-            for h in range(heads)
-        ]
+    zero = jnp.zeros((tree, 128), BF)
+    pairs = [slice(p * 256, (p + 1) * 256) for p in range(heads // 2)]
+
+    def score(r, keys):
+        out = []
+        for cols in pairs:
+            q = q_ref[r, :, cols]
+            q = jnp.concatenate(
+                [jnp.concatenate([q[:, :128], zero], axis=1), jnp.concatenate([zero, q[:, 128:]], axis=1)], axis=0
+            )
+            out.append(lax.dot_general(keys(cols), q, NT, preferred_element_type=F32))
+        return out
+
+    def weigh(scores, mask):
         exps = [jnp.where(mask, jnp.exp2(s * scale), 0.0) for s in scores]
-        for h in range(heads):
-            dens.append(jnp.sum(exps[h], axis=0, keepdims=True))
-            o = lax.dot_general(exps[h].astype(BF), values(h), TN, preferred_element_type=F32)
-            out_ref[r, :, h * 128:(h + 1) * 128] = o.astype(BF)
-        dens = jnp.concatenate(dens, axis=0)
-        high = dens.astype(BF).astype(F32)
-        pieces = [high, dens - high, jnp.zeros((128 - lane_off - 2 * heads, tree), F32)]
-        if lane_off:
-            pieces = [jnp.zeros((lane_off, tree), F32)] + pieces
-        out_ref[r, :, width:] = jnp.transpose(jnp.concatenate(pieces, axis=0)).astype(BF)
+        dens = [jnp.sum(e, axis=0, keepdims=True) for e in exps]
+        dens = [d[:, t * tree:(t + 1) * tree] for d in dens for t in range(2)]
+        return [e.astype(BF) for e in exps], jnp.concatenate(dens, axis=0)
+
+    def finish(r, exps, dens, values):
+        for p, cols in enumerate(pairs):
+            o = lax.dot_general(exps[p], values(cols), TN, preferred_element_type=F32)
+            for h, val in ((2 * p, o[:tree, :128]), (2 * p + 1, o[tree:, 128:])):
+                for t in range(2):
+                    rows = slice(h * part, (h + 1) * part)
+                    half = val[t * part:(t + 1) * part]
+                    if add:
+                        half = half + got_ref[2 * r + t, rows].astype(F32)
+                    out_ref[2 * r + t, rows] = half.astype(BF)
+        gap = jnp.zeros((heads, 64 - part), F32)
+        for t in range(2):
+            den = dens[:, t * part:(t + 1) * part]
+            if add:
+                got = got_ref[2 * r + t, heads * part:].astype(F32)
+                den = den + got[:, :part] + got[:, 64:64 + part]
+            high = den.astype(BF).astype(F32)
+            out_ref[2 * r + t, heads * part:] = jnp.concatenate([high, gap, den - high, gap], axis=1).astype(BF)
 
     @pl.when(treq < 0)
     def _():
-        pos = first + lax.broadcasted_iota(jnp.int32, (slots, tree), 0)
+        pos = first + lax.broadcasted_iota(jnp.int32, (slots, 2 * tree), 0)
+        scores = [score(r, lambda cols: k_ref[r, :, cols]) for r in range(reqs)]
+        weights = []
         for r in range(reqs):
             length = len_ref[step * reqs + r]
             mask = (pos < length) & ((pos < SINK) | (pos >= length - window))
-            attend(
-                r, lambda h: k_ref[r, :, h * 128:(h + 1) * 128], lambda h: v_ref[r, :, h * 128:(h + 1) * 128], mask
-            )
+            weights.append(weigh(scores[r], mask))
+        for r in range(reqs):
+            finish(r, *weights[r], lambda cols: v_ref[r, :, cols])
 
     @pl.when(treq >= 0)
     def _():
-        out_ref[...] = jnp.zeros_like(out_ref)
+        out_ref[...] = got_ref[...] if add else jnp.zeros_like(out_ref)
 
         @pl.when(treq // reqs == step)
         def _():
@@ -83,36 +106,41 @@
                 return carry
 
             lax.fori_loop(1, tree, body, 0)
-            mask = jnp.transpose(anc_ref[...])[:tree, :tree] > 0.5
-            attend(
-                lax.rem(treq, reqs), lambda h: nk_ref[0, :, h * 128:(h + 1) * 128],
-                lambda h: nv_ref[0, :, h * 128:(h + 1) * 128], mask,
-            )
-
-
-def attend_half(window, mine, info, lengths, parents, q, k, v, nk, nv, w=None, spread=None):
+            mask = jnp.transpose(anc_ref[...])[:tree, :tree]
+            mask = jnp.concatenate([mask, mask], axis=1) > 0.5
+            r = lax.rem(treq, reqs)
+            weights = weigh(score(r, lambda cols: nk_ref[0, :, cols]), mask)
+            finish(r, *weights, lambda cols: nv_ref[0, :, cols])
+
+
+def attend_half(window, info, lengths, parents, q, k, v, nk, nv, got=None, w=None, spread=None):
     reqs, tree, width = q.shape
     slots = k.shape[1]
     half = width // 2
     group = reqs // 2
-    hidx = (lambda i: i[CORE]) if mine else (lambda i: 1 - i[CORE])
+    add = got is not None
+    hidx = (lambda i: i[CORE]) if add else (lambda i: 1 - i[CORE])
     qs = pl.BlockSpec((group, tree, half), lambda r, i, l, p: (r, 0, hidx(i)))
     ks = pl.BlockSpec((group, slots, half), lambda r, i, l, p: (r, 0, hidx(i)))
     ns = pl.BlockSpec((1, tree, half), lambda r, i, l, p: (jnp.clip(i[TREQ], 0, reqs - 1), 0, hidx(i)))
     lengths, parents, q, k, v, nk, nv = (
         pltpu.with_memory_space_constraint(a, pltpu.HBM) for a in (lengths, parents, q, k, v, nk, nv)
     )
+    rows = half // 128 * (tree // 2) + half // 128
+    sums = pl.BlockSpec((2 * group, rows, 128), lambda r, i, l, p: (r, 0, 0))
     in_specs = [qs, ks, ks, ns, ns]
-    out_specs = [pl.BlockSpec((group, tree, half + 128), lambda r, i, l, p: (r, 0, 0))]
-    out_shape = [jax.ShapeDtypeStruct((reqs, tree, half + 128), BF)]
-    extra = ()
-    if w is not None:
+    out_specs = [sums]
+    out_shape = [jax.ShapeDtypeStruct((2 * reqs, rows, 128), BF)]
+    if add:
+        extra = (got,)
+        in_specs.append(sums)
+    else:
         extra = (pltpu.with_memory_space_constraint(w, pltpu.HBM),)
         in_specs.append(pl.BlockSpec(w.shape, lambda r, i, l, p: (0, 0)))
         out_specs.append(pl.BlockSpec(spread, lambda r, i, l, p: (0, 0, 0, 0, 0)))
         out_shape.append(jax.ShapeDtypeStruct(spread, w.dtype))
     return pl.pallas_call(
-        functools.partial(attend_kernel, window, 16 if mine else 0),
+        functools.partial(attend_kernel, window, add),
         out_shape=out_shape,
         grid_spec=pltpu.PrefetchScalarGridSpec(
             num_scalar_prefetch=3,
@@ -121,28 +149,27 @@
             out_specs=out_specs,
             scratch_shapes=[pltpu.VMEM((128, 128), F32)],
         ),
-        compiler_params=pltpu.CompilerParams(vmem_limit_bytes=16 * MB),
-        name="attend_mine" if mine else "attend_theirs",
+        compiler_params=pltpu.CompilerParams(vmem_limit_bytes=24 * MB),
+        name="attend_mine" if add else "attend_theirs",
     )(info, lengths, parents, q, k, v, nk, nv, *extra)
 
 
 def combine_kernel(parts_ref, out_ref):
-    width = out_ref.shape[1]
+    rows, width = out_ref.shape
     heads = width // 128
     total = jnp.sum(parts_ref[...].astype(F32), axis=0)
-    den = total[:, width:]
-    lane = lax.broadcasted_iota(jnp.int32, den.shape, 1)
+    den = total[heads * rows:]
+    den = jnp.concatenate([den[:, :rows] + den[:, 64:64 + rows], jnp.ones((heads, 128 - rows), F32)], axis=1)
+    den = jnp.transpose(jnp.concatenate([den, jnp.ones((128 - heads, 128), F32)], axis=0))
     for h in range(heads):
-        d = jnp.sum(jnp.where((lane % heads == h) & (lane < 4 * heads), den, 0.0), axis=1, keepdims=True)
-        cols = slice(h * 128, (h + 1) * 128)
-        out_ref[:, cols] = (total[:, cols] / d).astype(BF)
-
-
-def combine(parts):
-    rows, cols = parts.shape[1], parts.shape[2]
+        val = total[h * rows:(h + 1) * rows] / den[:rows, h:h + 1]
+        out_ref[:, h * 128:(h + 1) * 128] = val.astype(BF)
+
+
+def combine(parts, rows, width):
     return pl.pallas_call(
         combine_kernel,
-        out_shape=jax.ShapeDtypeStruct((rows, cols - 128), BF),
+        out_shape=jax.ShapeDtypeStruct((rows, width), BF),
         compiler_params=pltpu.CompilerParams(vmem_limit_bytes=16 * MB),
         name="combine",
     )(parts)
@@ -334,14 +361,14 @@
     info = jnp.stack([core, shard * slots, treq, z, x, core * nx + x, y, shard * vocab_weight.shape[1]]).astype(jnp.int32)
 
     args = (lengths, parents, queries, cache_keys, cache_values, new_keys, new_values)
-    send, w = attend_half(window, False, info, *args, out_weight, (nz, nx, nc, out_weight.shape[0], block))
+    spread = (nz, nx, nc, out_weight.shape[0], block)
+    send, w = attend_half(window, info, *args, w=out_weight, spread=spread)
     got = lax.ppermute(send, "core", swap)
     w = lax.all_to_all(w.reshape(shards, -1, block), ("z", "x", "core"), 0, 0).reshape(-1, block)
     ws = [w] + [shifted(w, "dp", s) for s in range(1, ny)]
-    (keep,) = attend_half(window, True, info, *args)
-    part = (keep + got).reshape(nz * nx, tokens // (nz * nx), half + 128)
+    (part,) = attend_half(window, info, *args, got=got)
     part = lax.all_to_all(part, ("z", "x"), 0, 0)
-    att = combine(part)
+    att = combine(part, tokens // (nz * nx), half)
     own = [att] + [shifted(att, "x", s) for s in range(1, nx)]
     other = [lax.ppermute(a, "core", swap) for a in own]
     hid = project(info, own, other, ws, residual, nz * nx).reshape(nz * nx, -1, block)

time: 97.1 us -> 94.2 us (0.970)
  Pallas kernels: 23.7 us -> 21.8 us
  waiting for transfers between devices: 13.9 us -> 15.4 us
  starting transfers between devices: 28.8 us -> 27.5 us
  other arithmetic: 1.85 us -> 0.7 us
    pallas_call x3, Pallas kernels: 11.9 us -> 10 us  [the longest x2 9.71 us: attend_half(): pl.pallas_call(functools.partial(attend_kernel, window, add), out_shape=o...]
    all_to_all x1, waiting for transfers between devices: 2.21 us -> 4.02 us  [local(): lax.all_to_all(w.reshape(shards, -1, block), ('z', 'x', 'core'), 0, 0)]
    add x1 -> x0, other arithmetic: 1.14 us -> none  [local(): part = (keep + got).reshape(nz * nx, tokens // (nz * nx), half + 128)]
  transfers between devices with their start and end apart: 14 -> 14, of which waited for: 3 -> 3; matrix products, arithmetic and copies ran while one was open for 1% -> 0% of each run, Pallas kernels for 8% -> 8%
where the time goes in v5:
time: 94.2 us; the launch traced here: 93.7 us
  starting transfers between devices  27.5 us (29%)
  blocking collectives  27.4 us (29%)
  Pallas kernels  21.8 us (23%)
  waiting for transfers between devices  15.4 us (16%)
    all_to_all x1, blocking collectives, local(): hid = lax.all_to_all(hid, ('z', 'x'), 0, 0).reshape(nz, nx, -1, block)  16.7 us
    all_to_all x1, blocking collectives, local(): stats = jnp.sum(lax.all_to_all(stats, ('z', 'x', 'core'), 0, 0), axis=0)  10.7 us
    all_to_all x1, waiting for transfers between devices, local(): part = lax.all_to_all(part, ('z', 'x'), 0, 0)  10.5 us
    pallas_call x2, Pallas kernels, attend_half(): pl.pallas_call(functools.partial(attend_kernel, window, add), out_shape=o...  9.71 us
    all_to_all x1, starting transfers between devices, local(): lax.all_to_all(w.reshape(shards, -1, block), ('z', 'x', 'core'), 0, 0)  8.12 us
    pallas_call x1, Pallas kernels, vocab(): pl.pallas_call(vocab_kernel, out_shape=(jax.ShapeDtypeStruct((tokens, wid...  7.91 us
    ppermute x4, starting transfers between devices, local(): other = [lax.ppermute(a, 'core', swap) for a in own]  7.06 us
    ppermute x6, starting transfers between devices, shifted(): return lax.ppermute(a, axis, [(i, (i + step) % n) for i in range(n)])  6.07 us
  transfers between devices with their start and end apart: 14, of which 3 were waited for; matrix products, arithmetic and copies ran while one was open for 0% of the time, Pallas kernels for 8%

profile of v5, /device:TPU:1, one launch (start us, length us, event | category | flops | bytes accessed | tf_op | source)
XLA Modules:
  0.0 93.7 jit_solution(15681133694731973028)
XLA Ops:
  0.6 0.1 stack.35.info_ref
  0.7 4.8 %attend_theirs.1 = (bf16[16,200,128]{2,1,0:T(8,128)(2,1)S(1)}, bf16[4,4,2,16,256]{4,3,2,1,0:T(8,128)(2,1)}) custom-call(s32[8]{0:T(128)S(1)} %stack.35.info_ref, s32[8]{0:T(128)} %len_ref.3, s32[8,48]{1,0:T(8,128)} %par_ref.5, bf16[8,48,2048]{2,1,0:T(8,128)(2,1)} %q_ref.3, bf16[8,128,2048]{2,1,0:T(8,128)(2,1)} %k_ref.3, bf16[8,128,2048]{2,1,0:T(8,128)(2,1)} %v_ref.3, ...), custom_call_target="tpu_custom_call" | custom-call | tf_op jit(solution)/shard_map/attend_theirs/pallas_call | solution.py:142
  5.6 1.4 %collective-permute-start = (bf16[16,200,128]{2,1,0:T(8,128)(2,1)S(1)}, bf16[16,200,128]{2,1,0:T(8,128)(2,1)S(1)}, u32[]{:S(2)}, u32[]{:S(2)}) collective-permute-start(bf16[16,200,128]{2,1,0:T(8,128)(2,1)S(1)} %get-tuple-element.6), channel_id=1, source_target_pairs={{0,1},{1,0},{2,3},{3,2},{4,5},{5,4},{6,7},{7,6},{8,9},{9,8},{10,11... | collective-permute-start | bytes 2457608 | tf_op jit(solution)/shard_map/ppermute | solution.py:366
  7.0 8.1 %all-to-all-start.1 = ((bf16[32,16,256]{2,1,0:T(8,128)(2,1)}), bf16[32,16,256]{2,1,0:T(8,128)(2,1)S(1)}, u32[]{:S(2)}, u32[]{:S(2)}) async-start(bf16[32,16,256]{2,1,0:T(8,128)(2,1)} %bitcast.8), calls=%async_computation.1 | async-start | bytes 524288 | tf_op jit(solution)/shard_map/all_to_all | solution.py:367
  15.1 0.0 collective-permute-done.refs_0_
  15.1 4.9 %attend_mine.1 = bf16[16,200,128]{2,1,0:T(8,128)(2,1)} custom-call(s32[8]{0:T(128)S(1)} %stack.35.info_ref, s32[8]{0:T(128)} %len_ref.3, s32[8,48]{1,0:T(8,128)} %par_ref.5, bf16[8,48,2048]{2,1,0:T(8,128)(2,1)} %q_ref.3, bf16[8,128,2048]{2,1,0:T(8,128)(2,1)} %k_ref.3, bf16[8,128,2048]{2,1,0:T(8,128)(2,1)} %v_ref.3, bf16[8,48,2048]{2,1,0:T(8,128)(2,1)} %nk_ref.3, ...), custom_call_target="tpu_custom_call" | custom-call | tf_op jit(solution)/shard_map/attend_mine/pallas_call | solution.py:142
  20.0 4.0 %all-to-all-done.1 = bf16[32,16,256]{2,1,0:T(8,128)(2,1)S(1)} async-done(((bf16[32,16,256]{2,1,0:T(8,128)(2,1)}), bf16[32,16,256]{2,1,0:T(8,128)(2,1)S(1)}, u32[]{:S(2)}, u32[]{:S(2)}) %all-to-all-start.1) | async-done | bytes 262176 | tf_op jit(solution)/shard_map/all_to_all | solution.py:367
  24.0 3.6 %all-to-all-start = ((bf16[16,200,128]{2,1,0:T(8,128)(2,1)}), bf16[16,200,128]{2,1,0:T(8,128)(2,1)S(1)}, u32[]{:S(2)}, u32[]{:S(2)}) async-start(bf16[16,200,128]{2,1,0:T(8,128)(2,1)} %attend_mine.1), calls=%async_computation | async-start | bytes 1638400 | tf_op jit(solution)/shard_map/all_to_all | solution.py:370
  27.7 2.8 %collective-permute-start.10 = (bf16[512,256]{1,0:T(8,128)(2,1)S(1)}, bf16[512,256]{1,0:T(8,128)(2,1)S(1)}, u32[]{:S(2)}, u32[]{:S(2)}) collective-permute-start(bf16[512,256]{1,0:T(8,128)(2,1)S(1)} %bitcast.19), channel_id=1, source_target_pairs={{0,96},{32,0},{64,32},{96,64},{1,97},{33,1},{65,33},{97,65},{2,98}... | collective-permute-start | bytes 786440 | tf_op jit(solution)/shard_map/ppermute | solution.py:342
  30.5 0.4 collective-permute-start.9
  30.8 0.7 collective-permute-start.8
  31.5 10.5 %all-to-all-done.parts_ref = bf16[16,200,128]{2,1,0:T(8,128)(2,1)S(1)} async-done(((bf16[16,200,128]{2,1,0:T(8,128)(2,1)}), bf16[16,200,128]{2,1,0:T(8,128)(2,1)S(1)}, u32[]{:S(2)}, u32[]{:S(2)}) %all-to-all-start) | async-done | bytes 819232 | tf_op jit(solution)/shard_map/all_to_all | solution.py:370
  42.0 0.3 combine.1.refs_0_
  42.3 0.1 collective-permute-start.3
  42.4 2.0 %collective-permute-start.2 = (bf16[24,1024]{1,0:T(8,128)(2,1)S(1)}, bf16[24,1024]{1,0:T(8,128)(2,1)S(1)}, u32[]{:S(2)}, u32[]{:S(2)}) collective-permute-start(bf16[24,1024]{1,0:T(8,128)(2,1)S(1)} %combine.1.refs_0_), channel_id=1, source_target_pairs={{0,4},{2,6},{4,0},{6,2},{1,5},{3,7},{5,1},{7,3},{8,12},{10,14},{12... | collective-permute-start | bytes 147464 | tf_op jit(solution)/shard_map/ppermute | solution.py:342
  44.4 0.0 collective-permute-done.10.refs_11_
  44.4 0.1 collective-permute-start.1
  44.5 1.9 %collective-permute-start.4 = (bf16[24,1024]{1,0:T(8,128)(2,1)S(1)}, bf16[24,1024]{1,0:T(8,128)(2,1)S(1)}, u32[]{:S(2)}, u32[]{:S(2)}) collective-permute-start(bf16[24,1024]{1,0:T(8,128)(2,1)S(1)} %combine.1.refs_0_), channel_id=1, source_target_pairs={{0,1},{1,0},{2,3},{3,2},{4,5},{5,4},{6,7},{7,6},{8,9},{9,8},{10,11... | collective-permute-start | bytes 147464 | tf_op jit(solution)/shard_map/ppermute | solution.py:373
  46.4 1.5 %collective-permute-start.7 = (bf16[24,1024]{1,0:T(8,128)(2,1)S(1)}, bf16[24,1024]{1,0:T(8,128)(2,1)S(1)}, u32[]{:S(2)}, u32[]{:S(2)}) collective-permute-start(bf16[24,1024]{1,0:T(8,128)(2,1)S(1)} %collective-permute-done.3.refs_3_), channel_id=1, source_target_pairs={{0,1},{1,0},{2,3},{3,2},{4,5},{5,4},{6,7},{7,6},{8,9},{9,8},{10,11... | collective-permute-start | bytes 147464 | tf_op jit(solution)/shard_map/ppermute | solution.py:373
  47.9 0.0 collective-permute-done.2.refs_2_
  47.9 2.2 %collective-permute-start.6 = (bf16[24,1024]{1,0:T(8,128)(2,1)S(1)}, bf16[24,1024]{1,0:T(8,128)(2,1)S(1)}, u32[]{:S(2)}, u32[]{:S(2)}) collective-permute-start(bf16[24,1024]{1,0:T(8,128)(2,1)S(1)} %collective-permute-done.2.refs_2_), channel_id=1, source_target_pairs={{0,1},{1,0},{2,3},{3,2},{4,5},{5,4},{6,7},{7,6},{8,9},{9,8},{10,11... | collective-permute-start | bytes 147464 | tf_op jit(solution)/shard_map/ppermute | solution.py:373
  50.1 0.0 collective-permute-done.1.refs_1_
  50.1 1.5 %collective-permute-start.5 = (bf16[24,1024]{1,0:T(8,128)(2,1)S(1)}, bf16[24,1024]{1,0:T(8,128)(2,1)S(1)}, u32[]{:S(2)}, u32[]{:S(2)}) collective-permute-start(bf16[24,1024]{1,0:T(8,128)(2,1)S(1)} %collective-permute-done.1.refs_1_), channel_id=1, source_target_pairs={{0,1},{1,0},{2,3},{3,2},{4,5},{5,4},{6,7},{7,6},{8,9},{9,8},{10,11... | collective-permute-start | bytes 147464 | tf_op jit(solution)/shard_map/ppermute | solution.py:373
  51.6 0.0 collective-permute-done.4.refs_4_
  51.6 0.9 collective-permute-done.5.refs_5_
  52.5 1.7 %project.1 = bf16[16,4,24,256]{3,2,1,0:T(8,128)(2,1)S(1)} custom-call(s32[8]{0:T(128)S(1)} %stack.35.info_ref, bf16[24,1024]{1,0:T(8,128)(2,1)S(1)} %combine.1.refs_0_, bf16[24,1024]{1,0:T(8,128)(2,1)S(1)} %collective-permute-done.1.refs_1_, bf16[24,1024]{1,0:T(8,128)(2,1)S(1)} %collective-permute-done.2.refs_2_, ...), custom_call_target="tpu_custom_call" | custom-call | tf_op jit(solution)/shard_map/project/pallas_call | solution.py:206
  54.2 16.7 %all_to_all.20 = bf16[16,96,256]{2,1,0:T(8,128)(2,1)S(1)} all-to-all(bf16[16,96,256]{2,1,0:T(8,128)(2,1)S(1)} %bitcast.18), channel_id=1, replica_groups=mesh['dp'=4,'z'=4,'x'=4,'core'=2] {'z','x'}, dimensions={0} | all-to-all | bytes 1572864 | tf_op jit(solution)/shard_map/all_to_all | solution.py:375
  70.9 1.2 %collective-permute-start.11 = (bf16[4,4,96,256]{3,2,1,0:T(8,128)(2,1)S(1)}, bf16[4,4,96,256]{3,2,1,0:T(8,128)(2,1)S(1)}, u32[]{:S(2)}, u32[]{:S(2)}) collective-permute-start(bf16[4,4,96,256]{3,2,1,0:T(8,128)(2,1)S(1)} %bitcast.15), channel_id=1, source_target_pairs={{0,1},{1,0},{2,3},{3,2},{4,5},{5,4},{6,7},{7,6},{8,9},{9,8},{10,11... | collective-permute-start | bytes 2359304 | tf_op jit(solution)/shard_map/ppermute | solution.py:376
  72.1 2.2 %fetch.1.w_ref = bf16[2048,1024]{1,0:T(8,128)(2,1)S(1)} custom-call(bf16[2048,2432]{1,0:T(8,128)(2,1)} %more_ref.1, bf16[4,4,96,256]{3,2,1,0:T(8,128)(2,1)S(1)} %bitcast.16), custom_call_target="tpu_custom_call" | custom-call | tf_op jit(solution)/shard_map/fetch/pallas_call | solution.py:329
  74.3 7.9 %vocab.1 = (bf16[384,2048]{1,0:T(8,128)(2,1)}, f32[32,8,128]{2,1,0:T(8,128)S(1)}) custom-call(s32[8]{0:T(128)S(1)} %stack.35.info_ref, bf16[4,4,96,256]{3,2,1,0:T(8,128)(2,1)S(1)} %bitcast.17, bf16[4,4,96,256]{3,2,1,0:T(8,128)(2,1)S(1)} %collective-permute-done.11.theirs_ref, f32[1,2048]{1,0:T(1,128)S(1)} %bitcast.23, s32[8,48]{1,0:T(8,128)S(1)} %copy-done.2, ...), custom_call_target="tpu_custom_call" | custom-call | tf_op jit(solution)/shard_map/vocab/pallas_call | solution.py:302
  82.3 10.7 %all_to_all.21 = f32[32,8,128]{2,1,0:T(8,128)S(1)} all-to-all(f32[32,8,128]{2,1,0:T(8,128)S(1)} %get-tuple-element.9), channel_id=1, replica_groups=mesh['dp'=4,'z'=4,'x'=4,'core'=2] {'z','x','core'}, dimensions={0} | all-to-all | bytes 262144 | tf_op jit(solution)/shard_map/all_to_all | solution.py:379
  93.0 0.7 log_subtract_fusion
  (13 shorter events, 0.1 us)
Async XLA Ops:
  5.6 9.6 %collective-permute-start = (bf16[16,200,128]{2,1,0:T(8,128)(2,1)S(1)}, bf16[16,200,128]{2,1,0:T(8,128)(2,1)S(1)}, u32[]{:S(2)}, u32[]{:S(2)}) collective-permute-start(bf16[16,200,128]{2,1,0:T(8,128)(2,1)S(1)} %get-tuple-element.6), channel_id=1, source_target_pairs={{0,1},{1,0},{2,3},{3,2},{4,5},{5,4},{6,7},{7,6},{8,9},{9,8},{10,11... | collective-permute-start | bytes 2457608 | tf_op jit(solution)/shard_map/ppermute | solution.py:366
  7.0 17.0 %all-to-all-start.1 = ((bf16[32,16,256]{2,1,0:T(8,128)(2,1)}), bf16[32,16,256]{2,1,0:T(8,128)(2,1)S(1)}, u32[]{:S(2)}, u32[]{:S(2)}) async-start(bf16[32,16,256]{2,1,0:T(8,128)(2,1)} %bitcast.8), calls=%async_computation.1 | async-start | bytes 524288 | tf_op jit(solution)/shard_map/all_to_all | solution.py:367
  24.0 18.0 %all-to-all-start = ((bf16[16,200,128]{2,1,0:T(8,128)(2,1)}), bf16[16,200,128]{2,1,0:T(8,128)(2,1)S(1)}, u32[]{:S(2)}, u32[]{:S(2)}) async-start(bf16[16,200,128]{2,1,0:T(8,128)(2,1)} %attend_mine.1), calls=%async_computation | async-start | bytes 1638400 | tf_op jit(solution)/shard_map/all_to_all | solution.py:370
  27.7 16.7 %collective-permute-start.10 = (bf16[512,256]{1,0:T(8,128)(2,1)S(1)}, bf16[512,256]{1,0:T(8,128)(2,1)S(1)}, u32[]{:S(2)}, u32[]{:S(2)}) collective-permute-start(bf16[512,256]{1,0:T(8,128)(2,1)S(1)} %bitcast.19), channel_id=1, source_target_pairs={{0,96},{32,0},{64,32},{96,64},{1,97},{33,1},{65,33},{97,65},{2,98}... | collective-permute-start | bytes 786440 | tf_op jit(solution)/shard_map/ppermute | solution.py:342
  30.5 14.1 %collective-permute-start.9 = (bf16[512,256]{1,0:T(8,128)(2,1)S(1)}, bf16[512,256]{1,0:T(8,128)(2,1)S(1)}, u32[]{:S(2)}, u32[]{:S(2)}) collective-permute-start(bf16[512,256]{1,0:T(8,128)(2,1)S(1)} %bitcast.20), channel_id=1, source_target_pairs={{0,64},{32,96},{64,0},{96,32},{1,65},{33,97},{65,1},{97,33},{2,66}... | collective-permute-start | bytes 786440 | tf_op jit(solution)/shard_map/ppermute | solution.py:342
  30.8 20.8 %collective-permute-start.8 = (bf16[512,256]{1,0:T(8,128)(2,1)S(1)}, bf16[512,256]{1,0:T(8,128)(2,1)S(1)}, u32[]{:S(2)}, u32[]{:S(2)}) collective-permute-start(bf16[512,256]{1,0:T(8,128)(2,1)S(1)} %bitcast.21), channel_id=1, source_target_pairs={{0,32},{32,64},{64,96},{96,0},{1,33},{33,65},{65,97},{97,1},{2,34}... | collective-permute-start | bytes 786440 | tf_op jit(solution)/shard_map/ppermute | solution.py:342
  42.3 4.1 %collective-permute-start.3 = (bf16[24,1024]{1,0:T(8,128)(2,1)S(1)}, bf16[24,1024]{1,0:T(8,128)(2,1)S(1)}, u32[]{:S(2)}, u32[]{:S(2)}) collective-permute-start(bf16[24,1024]{1,0:T(8,128)(2,1)S(1)} %combine.1.refs_0_), channel_id=1, source_target_pairs={{0,6},{2,0},{4,2},{6,4},{1,7},{3,1},{5,3},{7,5},{8,14},{10,8},{12,... | collective-permute-start | bytes 147464 | tf_op jit(solution)/shard_map/ppermute | solution.py:342
  42.4 5.5 %collective-permute-start.2 = (bf16[24,1024]{1,0:T(8,128)(2,1)S(1)}, bf16[24,1024]{1,0:T(8,128)(2,1)S(1)}, u32[]{:S(2)}, u32[]{:S(2)}) collective-permute-start(bf16[24,1024]{1,0:T(8,128)(2,1)S(1)} %combine.1.refs_0_), channel_id=1, source_target_pairs={{0,4},{2,6},{4,0},{6,2},{1,5},{3,7},{5,1},{7,3},{8,12},{10,14},{12... | collective-permute-start | bytes 147464 | tf_op jit(solution)/shard_map/ppermute | solution.py:342
  44.4 5.7 %collective-permute-start.1 = (bf16[24,1024]{1,0:T(8,128)(2,1)S(1)}, bf16[24,1024]{1,0:T(8,128)(2,1)S(1)}, u32[]{:S(2)}, u32[]{:S(2)}) collective-permute-start(bf16[24,1024]{1,0:T(8,128)(2,1)S(1)} %combine.1.refs_0_), channel_id=1, source_target_pairs={{0,2},{2,4},{4,6},{6,0},{1,3},{3,5},{5,7},{7,1},{8,10},{10,12},{12... | collective-permute-start | bytes 147464 | tf_op jit(solution)/shard_map/ppermute | solution.py:342
  44.5 7.1 %collective-permute-start.4 = (bf16[24,1024]{1,0:T(8,128)(2,1)S(1)}, bf16[24,1024]{1,0:T(8,128)(2,1)S(1)}, u32[]{:S(2)}, u32[]{:S(2)}) collective-permute-start(bf16[24,1024]{1,0:T(8,128)(2,1)S(1)} %combine.1.refs_0_), channel_id=1, source_target_pairs={{0,1},{1,0},{2,3},{3,2},{4,5},{5,4},{6,7},{7,6},{8,9},{9,8},{10,11... | collective-permute-start | bytes 147464 | tf_op jit(solution)/shard_map/ppermute | solution.py:373
  46.4 5.2 %collective-permute-start.7 = (bf16[24,1024]{1,0:T(8,128)(2,1)S(1)}, bf16[24,1024]{1,0:T(8,128)(2,1)S(1)}, u32[]{:S(2)}, u32[]{:S(2)}) collective-permute-start(bf16[24,1024]{1,0:T(8,128)(2,1)S(1)} %collective-permute-done.3.refs_3_), channel_id=1, source_target_pairs={{0,1},{1,0},{2,3},{3,2},{4,5},{5,4},{6,7},{7,6},{8,9},{9,8},{10,11... | collective-permute-start | bytes 147464 | tf_op jit(solution)/shard_map/ppermute | solution.py:373
  47.9 3.7 %collective-permute-start.6 = (bf16[24,1024]{1,0:T(8,128)(2,1)S(1)}, bf16[24,1024]{1,0:T(8,128)(2,1)S(1)}, u32[]{:S(2)}, u32[]{:S(2)}) collective-permute-start(bf16[24,1024]{1,0:T(8,128)(2,1)S(1)} %collective-permute-done.2.refs_2_), channel_id=1, source_target_pairs={{0,1},{1,0},{2,3},{3,2},{4,5},{5,4},{6,7},{7,6},{8,9},{9,8},{10,11... | collective-permute-start | bytes 147464 | tf_op jit(solution)/shard_map/ppermute | solution.py:373
  50.1 2.4 %collective-permute-start.5 = (bf16[24,1024]{1,0:T(8,128)(2,1)S(1)}, bf16[24,1024]{1,0:T(8,128)(2,1)S(1)}, u32[]{:S(2)}, u32[]{:S(2)}) collective-permute-start(bf16[24,1024]{1,0:T(8,128)(2,1)S(1)} %collective-permute-done.1.refs_1_), channel_id=1, source_target_pairs={{0,1},{1,0},{2,3},{3,2},{4,5},{5,4},{6,7},{7,6},{8,9},{9,8},{10,11... | collective-permute-start | bytes 147464 | tf_op jit(solution)/shard_map/ppermute | solution.py:373
  70.9 3.4 %copy-start = (s32[8,48]{1,0:T(8,128)S(1)}, s32[8,48]{1,0:T(8,128)}, u32[]{:S(2)}) copy-start(s32[8,48]{1,0:T(8,128)} %par_ref.5) | copy-start | bytes 4612
  70.9 3.4 %copy-start.1 = (f32[2048]{0:T(1024)S(1)}, f32[2048]{0:T(1024)}, u32[]{:S(2)}) copy-start(f32[2048]{0:T(1024)} %param.22) | copy-start | bytes 24580
  70.9 3.4 %copy-start.2 = (s32[8,48]{1,0:T(8,128)S(1)}, s32[8,48]{1,0:T(8,128)}, u32[]{:S(2)}) copy-start(s32[8,48]{1,0:T(8,128)} %tok_ref.1) | copy-start | bytes 4612
  70.9 3.4 %collective-permute-start.11 = (bf16[4,4,96,256]{3,2,1,0:T(8,128)(2,1)S(1)}, bf16[4,4,96,256]{3,2,1,0:T(8,128)(2,1)S(1)}, u32[]{:S(2)}, u32[]{:S(2)}) collective-permute-start(bf16[4,4,96,256]{3,2,1,0:T(8,128)(2,1)S(1)} %bitcast.15), channel_id=1, source_target_pairs={{0,1},{1,0},{2,3},{3,2},{4,5},{5,4},{6,7},{7,6},{8,9},{9,8},{10,11... | collective-permute-start | bytes 2359304 | tf_op jit(solution)/shard_map/ppermute | solution.py:376

commit v6 on v5

--- a/solution.py
+++ b/solution.py
@@ -23,15 +23,17 @@
         got_ref, out_ref, anc_ref = refs
     else:
         w_ref, out_ref, spread_ref, anc_ref = refs
-        nz, nx, nc, _, block = spread_ref.shape
+        nz, nx, _, _, block = spread_ref.shape
 
         @pl.when(step == 0)
         def _():
-            for c in range(nc):
-                for x in range(nx):
-                    at = (c * nx + x) * block
-                    for z in range(nz):
-                        spread_ref[z, x, c] = w_ref[:, at:at + block]
+            for x in range(nx):
+                a = w_ref[:, x * block:(x + 1) * block]
+                b = w_ref[:, (nx + x) * block:(nx + x + 1) * block]
+                low = info_ref[CORE] == 0
+                for z in range(nz):
+                    spread_ref[z, x, 0] = jnp.where(low, a, b)
+                    spread_ref[z, x, 1] = jnp.where(low, b, a)
 
     first = info_ref[FIRST]
     treq = info_ref[TREQ]
@@ -180,7 +182,9 @@
     ws, (res_ref, out_ref) = refs[2 * nx:-2], refs[-2:]
     core, x, y = info_ref[CORE], info_ref[X], info_ref[DP]
     rows, half = own[0].shape
-    ny, deep = len(ws), ws[0].shape[0]
+    ny, deep = len(ws), 2 * ws[0].shape[1]
+    run = out_ref.shape[0]
+    run = deep // (2 * run)
     mine = jnp.concatenate([own[s][...] for s in range(nx)], axis=0)
     theirs = jnp.concatenate([other[s][...] for s in range(nx)], axis=0)
     acc = None
@@ -188,7 +192,10 @@
         at = lax.rem(y + ny - s, ny)
         a = jnp.where(core == at // 2, mine, theirs)
         a = jnp.where(at % 2 == 0, a[:, :deep], a[:, deep:])
-        part = jnp.dot(a, ws[s][...], preferred_element_type=F32)
+        even = jnp.where(core == 0, ws[s][0], ws[s][1])
+        odd = jnp.where(core == 0, ws[s][1], ws[s][0])
+        w = [b[i:i + run] for i in range(0, deep // 2, run) for b in (even, odd)]
+        part = jnp.dot(a, jnp.concatenate(w, axis=0), preferred_element_type=F32)
         acc = part if acc is None else acc + part
     for s in range(nx):
         at = lax.rem(x + nx - s, nx)
@@ -200,7 +207,7 @@
 def project(info, own, other, ws, residual, copies):
     nx = len(own)
     rows, half = own[0].shape
-    cols = ws[0].shape[1]
+    cols = ws[0].shape[2]
     part = pl.BlockSpec((rows, half), lambda g, i: (0, 0))
     residual = pltpu.with_memory_space_constraint(residual.reshape(-1, rows, residual.shape[2]), pltpu.HBM)
     return pl.pallas_call(
@@ -210,7 +217,7 @@
             num_scalar_prefetch=1,
             grid=(1,),
             in_specs=[part] * (2 * nx)
-            + [pl.BlockSpec(w.shape, lambda g, i: (0, 0)) for w in ws]
+            + [pl.BlockSpec(w.shape, lambda g, i: (0, 0, 0)) for w in ws]
             + [pl.BlockSpec((nx, rows, cols), lambda g, i: (i[Z], 0, i[BLOCK]))],
             out_specs=pl.BlockSpec((copies, nx, rows, cols), lambda g, i: (0, 0, 0, 0)),
         ),
@@ -364,7 +371,8 @@
     spread = (nz, nx, nc, out_weight.shape[0], block)
     send, w = attend_half(window, info, *args, w=out_weight, spread=spread)
     got = lax.ppermute(send, "core", swap)
-    w = lax.all_to_all(w.reshape(shards, -1, block), ("z", "x", "core"), 0, 0).reshape(-1, block)
+    w = lax.all_to_all(w.reshape((nz * nx,) + w.shape[2:]), ("z", "x"), 0, 0)
+    w = jnp.stack([w[:, 0].reshape(-1, block), lax.ppermute(w[:, 1].reshape(-1, block), "core", swap)])
     ws = [w] + [shifted(w, "dp", s) for s in range(1, ny)]
     (part,) = attend_half(window, info, *args, got=got)
     part = lax.all_to_all(part, ("z", "x"), 0, 0)
@@ -374,7 +382,7 @@
     hid = project(info, own, other, ws, residual, nz * nx).reshape(nz * nx, -1, block)
     hid = lax.all_to_all(hid, ("z", "x"), 0, 0).reshape(nz, nx, -1, block)
     other = lax.ppermute(hid, "core", swap)
-    scorer = fetch(vocab_weight, hid, 1024)
+    scorer = fetch(vocab_weight, hid, 1536)
     hidden, stats = vocab(info, hid, other, norm_gain.reshape(1, -1), tree_tokens, parents, scorer, vocab_weight, shards)
     stats = jnp.sum(lax.all_to_all(stats, ("z", "x", "core"), 0, 0), axis=0)
     logprob = stats[:, 64:64 + tree] - jnp.log(stats[:, :tree])

time: 94.2 us -> 93.6 us (level)
  waiting for transfers between devices: 15.4 us -> 12.8 us
  starting transfers between devices: 27.5 us -> 29.4 us
  Pallas kernels: 21.8 us -> 20.7 us
  blocking collectives: 27.4 us -> 28.5 us
    all_to_all x1, waiting for transfers between devices: 10.5 us -> 7.27 us  [local(): part = lax.all_to_all(part, ('z', 'x'), 0, 0)]
    pallas_call x1, Pallas kernels: 7.91 us -> 6.16 us  [vocab(): pl.pallas_call(vocab_kernel, out_shape=(jax.ShapeDtypeStruct((tokens, wid...]
    ppermute x6, starting transfers between devices: 6.07 us -> 7.51 us  [shifted(): return lax.ppermute(a, axis, [(i, (i + step) % n) for i in range(n)])]
    ppermute x0 -> x1, starting transfers between devices: none -> 1.18 us  [local(): lax.ppermute(w[:, 1].reshape(-1, block), 'core', swap)]
    all_to_all x1, blocking collectives: 16.7 us -> 17.9 us  [local(): hid = lax.all_to_all(hid, ('z', 'x'), 0, 0).reshape(nz, nx, -1, block)]
    ppermute x0 -> x1, waiting for transfers between devices: none -> 0.99 us  [local(): lax.ppermute(w[:, 1].reshape(-1, block), 'core', swap)]
  transfers between devices with their start and end apart: 14 -> 15, of which waited for: 3 -> 5; matrix products, arithmetic and copies ran while one was open for 0% -> 0% of each run, Pallas kernels for 8% -> 9%
where the time goes in v6:
time: 93.6 us; the launch traced here: 93.1 us
  starting transfers between devices  29.4 us (31%)
  blocking collectives  28.5 us (30%)
  Pallas kernels  20.7 us (22%)
  waiting for transfers between devices  12.8 us (14%)
    all_to_all x1, blocking collectives, local(): hid = lax.all_to_all(hid, ('z', 'x'), 0, 0).reshape(nz, nx, -1, block)  17.9 us
    all_to_all x1, blocking collectives, local(): stats = jnp.sum(lax.all_to_all(stats, ('z', 'x', 'core'), 0, 0), axis=0)  10.7 us
    pallas_call x2, Pallas kernels, attend_half(): pl.pallas_call(functools.partial(attend_kernel, window, add), out_shape=o...  9.74 us
    all_to_all x1, starting transfers between devices, local(): w = lax.all_to_all(w.reshape((nz * nx,) + w.shape[2:]), ('z', 'x'), 0, 0)  7.68 us
    ppermute x6, starting transfers between devices, shifted(): return lax.ppermute(a, axis, [(i, (i + step) % n) for i in range(n)])  7.51 us
    all_to_all x1, waiting for transfers between devices, local(): part = lax.all_to_all(part, ('z', 'x'), 0, 0)  7.27 us
    ppermute x4, starting transfers between devices, local(): other = [lax.ppermute(a, 'core', swap) for a in own]  6.55 us
    pallas_call x1, Pallas kernels, vocab(): pl.pallas_call(vocab_kernel, out_shape=(jax.ShapeDtypeStruct((tokens, wid...  6.16 us
  transfers between devices with their start and end apart: 15, of which 5 were waited for; matrix products, arithmetic and copies ran while one was open for 0% of the time, Pallas kernels for 9%

profile of v6, /device:TPU:1, one launch (start us, length us, event | category | flops | bytes accessed | tf_op | source)
XLA Modules:
  0.0 93.1 jit_solution(2629580487999641860)
XLA Ops:
  0.6 0.1 stack.41.info_ref
  0.7 4.8 %attend_theirs.1 = (bf16[16,200,128]{2,1,0:T(8,128)(2,1)S(1)}, bf16[4,4,2,16,256]{4,3,2,1,0:T(8,128)(2,1)}) custom-call(s32[8]{0:T(128)S(1)} %stack.41.info_ref, s32[8]{0:T(128)} %len_ref.3, s32[8,48]{1,0:T(8,128)} %par_ref.5, bf16[8,48,2048]{2,1,0:T(8,128)(2,1)} %q_ref.3, bf16[8,128,2048]{2,1,0:T(8,128)(2,1)} %k_ref.3, bf16[8,128,2048]{2,1,0:T(8,128)(2,1)} %v_ref.3, ...), custom_call_target="tpu_custom_call" | custom-call | tf_op jit(solution)/shard_map/attend_theirs/pallas_call | solution.py:144
  5.6 1.4 %collective-permute-start = (bf16[16,200,128]{2,1,0:T(8,128)(2,1)S(1)}, bf16[16,200,128]{2,1,0:T(8,128)(2,1)S(1)}, u32[]{:S(2)}, u32[]{:S(2)}) collective-permute-start(bf16[16,200,128]{2,1,0:T(8,128)(2,1)S(1)} %get-tuple-element.6), channel_id=1, source_target_pairs={{0,1},{1,0},{2,3},{3,2},{4,5},{5,4},{6,7},{7,6},{8,9},{9,8},{10,11... | collective-permute-start | bytes 2457608 | tf_op jit(solution)/shard_map/ppermute | solution.py:373
  7.0 7.7 %all-to-all-start.1 = ((bf16[16,2,16,256]{3,2,1,0:T(8,128)(2,1)}), bf16[16,2,16,256]{3,2,1,0:T(8,128)(2,1)S(1)}, u32[]{:S(2)}, u32[]{:S(2)}) async-start(bf16[16,2,16,256]{3,2,1,0:T(8,128)(2,1)} %bitcast.8), calls=%async_computation.1 | async-start | bytes 524288 | tf_op jit(solution)/shard_map/all_to_all | solution.py:374
  14.7 0.0 collective-permute-done.refs_0_
  14.7 4.9 %attend_mine.1 = bf16[16,200,128]{2,1,0:T(8,128)(2,1)} custom-call(s32[8]{0:T(128)S(1)} %stack.41.info_ref, s32[8]{0:T(128)} %len_ref.3, s32[8,48]{1,0:T(8,128)} %par_ref.5, bf16[8,48,2048]{2,1,0:T(8,128)(2,1)} %q_ref.3, bf16[8,128,2048]{2,1,0:T(8,128)(2,1)} %k_ref.3, bf16[8,128,2048]{2,1,0:T(8,128)(2,1)} %v_ref.3, bf16[8,48,2048]{2,1,0:T(8,128)(2,1)} %nk_ref.3, ...), custom_call_target="tpu_custom_call" | custom-call | tf_op jit(solution)/shard_map/attend_mine/pallas_call | solution.py:144
  19.6 3.6 %all-to-all-done.1 = bf16[16,2,16,256]{3,2,1,0:T(8,128)(2,1)S(1)} async-done(((bf16[16,2,16,256]{3,2,1,0:T(8,128)(2,1)}), bf16[16,2,16,256]{3,2,1,0:T(8,128)(2,1)S(1)}, u32[]{:S(2)}, u32[]{:S(2)}) %all-to-all-start.1) | async-done | bytes 262176 | tf_op jit(solution)/shard_map/all_to_all | solution.py:374
  23.2 3.6 %all-to-all-start = ((bf16[16,200,128]{2,1,0:T(8,128)(2,1)}), bf16[16,200,128]{2,1,0:T(8,128)(2,1)S(1)}, u32[]{:S(2)}, u32[]{:S(2)}) async-start(bf16[16,200,128]{2,1,0:T(8,128)(2,1)} %attend_mine.1), calls=%async_computation | async-start | bytes 1638400 | tf_op jit(solution)/shard_map/all_to_all | solution.py:378
  26.9 1.2 %collective-permute-start.8 = (bf16[256,256]{1,0:T(8,128)(2,1)S(1)}, bf16[256,256]{1,0:T(8,128)(2,1)S(1)}, u32[]{:S(2)}, u32[]{:S(2)}) collective-permute-start(bf16[256,256]{1,0:T(8,128)(2,1)S(1)} %bitcast.24), channel_id=1, source_target_pairs={{0,1},{1,0},{2,3},{3,2},{4,5},{5,4},{6,7},{7,6},{8,9},{9,8},{10,11... | collective-permute-start | bytes 393224 | tf_op jit(solution)/shard_map/ppermute | solution.py:375
  28.1 1.0 %collective-permute-done.8 = bf16[256,256]{1,0:T(8,128)(2,1)S(1)} collective-permute-done((bf16[256,256]{1,0:T(8,128)(2,1)S(1)}, bf16[256,256]{1,0:T(8,128)(2,1)S(1)}, u32[]{:S(2)}, u32[]{:S(2)}) %collective-permute-start.8) | collective-permute-done | bytes 131104 | tf_op jit(solution)/shard_map/ppermute | solution.py:375
  29.1 2.8 %collective-permute-start.11 = (bf16[2,256,256]{2,1,0:T(8,128)(2,1)S(1)}, bf16[2,256,256]{2,1,0:T(8,128)(2,1)S(1)}, u32[]{:S(2)}, u32[]{:S(2)}) collective-permute-start(bf16[2,256,256]{2,1,0:T(8,128)(2,1)S(1)} %pad_maximum_fusion.refs_8_), channel_id=1, source_target_pairs={{0,96},{32,0},{64,32},{96,64},{1,97},{33,1},{65,33},{97,65},{2,98}... | collective-permute-start | bytes 786440 | tf_op jit(solution)/shard_map/ppermute | solution.py:349
  31.9 0.4 collective-permute-start.10
  32.2 0.7 collective-permute-start.9
  32.9 7.3 %all-to-all-done.parts_ref = bf16[16,200,128]{2,1,0:T(8,128)(2,1)S(1)} async-done(((bf16[16,200,128]{2,1,0:T(8,128)(2,1)}), bf16[16,200,128]{2,1,0:T(8,128)(2,1)S(1)}, u32[]{:S(2)}, u32[]{:S(2)}) %all-to-all-start) | async-done | bytes 819232 | tf_op jit(solution)/shard_map/all_to_all | solution.py:378
  40.2 0.3 combine.1.refs_0_
  40.5 1.5 %collective-permute-start.3 = (bf16[24,1024]{1,0:T(8,128)(2,1)S(1)}, bf16[24,1024]{1,0:T(8,128)(2,1)S(1)}, u32[]{:S(2)}, u32[]{:S(2)}) collective-permute-start(bf16[24,1024]{1,0:T(8,128)(2,1)S(1)} %combine.1.refs_0_), channel_id=1, source_target_pairs={{0,6},{2,0},{4,2},{6,4},{1,7},{3,1},{5,3},{7,5},{8,14},{10,8},{12,... | collective-permute-start | bytes 147464 | tf_op jit(solution)/shard_map/ppermute | solution.py:349
  42.0 0.7 collective-permute-start.2
  42.6 0.1 collective-permute-done.11.refs_11_
  42.7 1.5 %collective-permute-start.1 = (bf16[24,1024]{1,0:T(8,128)(2,1)S(1)}, bf16[24,1024]{1,0:T(8,128)(2,1)S(1)}, u32[]{:S(2)}, u32[]{:S(2)}) collective-permute-start(bf16[24,1024]{1,0:T(8,128)(2,1)S(1)} %combine.1.refs_0_), channel_id=1, source_target_pairs={{0,2},{2,4},{4,6},{6,0},{1,3},{3,5},{5,7},{7,1},{8,10},{10,12},{12... | collective-permute-start | bytes 147464 | tf_op jit(solution)/shard_map/ppermute | solution.py:349
  44.2 1.6 %collective-permute-start.4 = (bf16[24,1024]{1,0:T(8,128)(2,1)S(1)}, bf16[24,1024]{1,0:T(8,128)(2,1)S(1)}, u32[]{:S(2)}, u32[]{:S(2)}) collective-permute-start(bf16[24,1024]{1,0:T(8,128)(2,1)S(1)} %combine.1.refs_0_), channel_id=1, source_target_pairs={{0,1},{1,0},{2,3},{3,2},{4,5},{5,4},{6,7},{7,6},{8,9},{9,8},{10,11... | collective-permute-start | bytes 147464 | tf_op jit(solution)/shard_map/ppermute | solution.py:381
  45.8 1.2 %collective-permute-start.7 = (bf16[24,1024]{1,0:T(8,128)(2,1)S(1)}, bf16[24,1024]{1,0:T(8,128)(2,1)S(1)}, u32[]{:S(2)}, u32[]{:S(2)}) collective-permute-start(bf16[24,1024]{1,0:T(8,128)(2,1)S(1)} %collective-permute-done.3.refs_3_), channel_id=1, source_target_pairs={{0,1},{1,0},{2,3},{3,2},{4,5},{5,4},{6,7},{7,6},{8,9},{9,8},{10,11... | collective-permute-start | bytes 147464 | tf_op jit(solution)/shard_map/ppermute | solution.py:381
  47.1 0.0 collective-permute-done.2.refs_2_
  47.1 2.2 %collective-permute-start.6 = (bf16[24,1024]{1,0:T(8,128)(2,1)S(1)}, bf16[24,1024]{1,0:T(8,128)(2,1)S(1)}, u32[]{:S(2)}, u32[]{:S(2)}) collective-permute-start(bf16[24,1024]{1,0:T(8,128)(2,1)S(1)} %collective-permute-done.2.refs_2_), channel_id=1, source_target_pairs={{0,1},{1,0},{2,3},{3,2},{4,5},{5,4},{6,7},{7,6},{8,9},{9,8},{10,11... | collective-permute-start | bytes 147464 | tf_op jit(solution)/shard_map/ppermute | solution.py:381
  49.3 1.5 %collective-permute-start.5 = (bf16[24,1024]{1,0:T(8,128)(2,1)S(1)}, bf16[24,1024]{1,0:T(8,128)(2,1)S(1)}, u32[]{:S(2)}, u32[]{:S(2)}) collective-permute-start(bf16[24,1024]{1,0:T(8,128)(2,1)S(1)} %collective-permute-done.1.refs_1_), channel_id=1, source_target_pairs={{0,1},{1,0},{2,3},{3,2},{4,5},{5,4},{6,7},{7,6},{8,9},{9,8},{10,11... | collective-permute-start | bytes 147464 | tf_op jit(solution)/shard_map/ppermute | solution.py:381
  50.8 0.9 collective-permute-done.5.refs_5_
  51.6 1.7 %project.1 = bf16[16,4,24,256]{3,2,1,0:T(8,128)(2,1)S(1)} custom-call(s32[8]{0:T(128)S(1)} %stack.41.info_ref, bf16[24,1024]{1,0:T(8,128)(2,1)S(1)} %combine.1.refs_0_, bf16[24,1024]{1,0:T(8,128)(2,1)S(1)} %collective-permute-done.1.refs_1_, bf16[24,1024]{1,0:T(8,128)(2,1)S(1)} %collective-permute-done.2.refs_2_, ...), custom_call_target="tpu_custom_call" | custom-call | tf_op jit(solution)/shard_map/project/pallas_call | solution.py:213
  53.4 17.9 %all_to_all.20 = bf16[16,96,256]{2,1,0:T(8,128)(2,1)S(1)} all-to-all(bf16[16,96,256]{2,1,0:T(8,128)(2,1)S(1)} %bitcast.20), channel_id=1, replica_groups=mesh['dp'=4,'z'=4,'x'=4,'core'=2] {'z','x'}, dimensions={0} | all-to-all | bytes 1572864 | tf_op jit(solution)/shard_map/all_to_all | solution.py:383
  71.2 1.5 %collective-permute-start.12 = (bf16[4,4,96,256]{3,2,1,0:T(8,128)(2,1)S(1)}, bf16[4,4,96,256]{3,2,1,0:T(8,128)(2,1)S(1)}, u32[]{:S(2)}, u32[]{:S(2)}) collective-permute-start(bf16[4,4,96,256]{3,2,1,0:T(8,128)(2,1)S(1)} %bitcast.17), channel_id=1, source_target_pairs={{0,1},{1,0},{2,3},{3,2},{4,5},{5,4},{6,7},{7,6},{8,9},{9,8},{10,11... | collective-permute-start | bytes 2359304 | tf_op jit(solution)/shard_map/ppermute | solution.py:384
  72.7 2.8 %fetch.1.w_ref = bf16[2048,1536]{1,0:T(8,128)(2,1)S(1)} custom-call(bf16[2048,2432]{1,0:T(8,128)(2,1)} %more_ref.1, bf16[4,4,96,256]{3,2,1,0:T(8,128)(2,1)S(1)} %bitcast.18), custom_call_target="tpu_custom_call" | custom-call | tf_op jit(solution)/shard_map/fetch/pallas_call | solution.py:336
  75.5 6.2 %vocab.1 = (bf16[384,2048]{1,0:T(8,128)(2,1)}, f32[32,8,128]{2,1,0:T(8,128)S(1)}) custom-call(s32[8]{0:T(128)S(1)} %stack.41.info_ref, bf16[4,4,96,256]{3,2,1,0:T(8,128)(2,1)S(1)} %bitcast.19, bf16[4,4,96,256]{3,2,1,0:T(8,128)(2,1)S(1)} %collective-permute-done.12.theirs_ref, f32[1,2048]{1,0:T(1,128)S(1)} %bitcast.21, s32[8,48]{1,0:T(8,128)S(1)} %copy-done.2, ...), custom_call_target="tpu_custom_call" | custom-call | tf_op jit(solution)/shard_map/vocab/pallas_call | solution.py:309
  81.7 10.7 %all_to_all.21 = f32[32,8,128]{2,1,0:T(8,128)S(1)} all-to-all(f32[32,8,128]{2,1,0:T(8,128)S(1)} %get-tuple-element.9), channel_id=1, replica_groups=mesh['dp'=4,'z'=4,'x'=4,'core'=2] {'z','x','core'}, dimensions={0} | all-to-all | bytes 262144 | tf_op jit(solution)/shard_map/all_to_all | solution.py:387
  92.4 0.7 log_subtract_fusion
  (17 shorter events, 0.1 us)
Async XLA Ops:
  5.6 9.1 %collective-permute-start = (bf16[16,200,128]{2,1,0:T(8,128)(2,1)S(1)}, bf16[16,200,128]{2,1,0:T(8,128)(2,1)S(1)}, u32[]{:S(2)}, u32[]{:S(2)}) collective-permute-start(bf16[16,200,128]{2,1,0:T(8,128)(2,1)S(1)} %get-tuple-element.6), channel_id=1, source_target_pairs={{0,1},{1,0},{2,3},{3,2},{4,5},{5,4},{6,7},{7,6},{8,9},{9,8},{10,11... | collective-permute-start | bytes 2457608 | tf_op jit(solution)/shard_map/ppermute | solution.py:373
  7.0 16.2 %all-to-all-start.1 = ((bf16[16,2,16,256]{3,2,1,0:T(8,128)(2,1)}), bf16[16,2,16,256]{3,2,1,0:T(8,128)(2,1)S(1)}, u32[]{:S(2)}, u32[]{:S(2)}) async-start(bf16[16,2,16,256]{3,2,1,0:T(8,128)(2,1)} %bitcast.8), calls=%async_computation.1 | async-start | bytes 524288 | tf_op jit(solution)/shard_map/all_to_all | solution.py:374
  23.2 17.0 %all-to-all-start = ((bf16[16,200,128]{2,1,0:T(8,128)(2,1)}), bf16[16,200,128]{2,1,0:T(8,128)(2,1)S(1)}, u32[]{:S(2)}, u32[]{:S(2)}) async-start(bf16[16,200,128]{2,1,0:T(8,128)(2,1)} %attend_mine.1), calls=%async_computation | async-start | bytes 1638400 | tf_op jit(solution)/shard_map/all_to_all | solution.py:378
  26.9 2.2 %collective-permute-start.8 = (bf16[256,256]{1,0:T(8,128)(2,1)S(1)}, bf16[256,256]{1,0:T(8,128)(2,1)S(1)}, u32[]{:S(2)}, u32[]{:S(2)}) collective-permute-start(bf16[256,256]{1,0:T(8,128)(2,1)S(1)} %bitcast.24), channel_id=1, source_target_pairs={{0,1},{1,0},{2,3},{3,2},{4,5},{5,4},{6,7},{7,6},{8,9},{9,8},{10,11... | collective-permute-start | bytes 393224 | tf_op jit(solution)/shard_map/ppermute | solution.py:375
  29.1 13.6 %collective-permute-start.11 = (bf16[2,256,256]{2,1,0:T(8,128)(2,1)S(1)}, bf16[2,256,256]{2,1,0:T(8,128)(2,1)S(1)}, u32[]{:S(2)}, u32[]{:S(2)}) collective-permute-start(bf16[2,256,256]{2,1,0:T(8,128)(2,1)S(1)} %pad_maximum_fusion.refs_8_), channel_id=1, source_target_pairs={{0,96},{32,0},{64,32},{96,64},{1,97},{33,1},{65,33},{97,65},{2,98}... | collective-permute-start | bytes 786440 | tf_op jit(solution)/shard_map/ppermute | solution.py:349
  31.9 12.3 %collective-permute-start.10 = (bf16[2,256,256]{2,1,0:T(8,128)(2,1)S(1)}, bf16[2,256,256]{2,1,0:T(8,128)(2,1)S(1)}, u32[]{:S(2)}, u32[]{:S(2)}) collective-permute-start(bf16[2,256,256]{2,1,0:T(8,128)(2,1)S(1)} %pad_maximum_fusion.refs_8_), channel_id=1, source_target_pairs={{0,64},{32,96},{64,0},{96,32},{1,65},{33,97},{65,1},{97,33},{2,66}... | collective-permute-start | bytes 786440 | tf_op jit(solution)/shard_map/ppermute | solution.py:349
  32.2 18.5 %collective-permute-start.9 = (bf16[2,256,256]{2,1,0:T(8,128)(2,1)S(1)}, bf16[2,256,256]{2,1,0:T(8,128)(2,1)S(1)}, u32[]{:S(2)}, u32[]{:S(2)}) collective-permute-start(bf16[2,256,256]{2,1,0:T(8,128)(2,1)S(1)} %pad_maximum_fusion.refs_8_), channel_id=1, source_target_pairs={{0,32},{32,64},{64,96},{96,0},{1,33},{33,65},{65,97},{97,1},{2,34}... | collective-permute-start | bytes 786440 | tf_op jit(solution)/shard_map/ppermute | solution.py:349
  40.5 5.3 %collective-permute-start.3 = (bf16[24,1024]{1,0:T(8,128)(2,1)S(1)}, bf16[24,1024]{1,0:T(8,128)(2,1)S(1)}, u32[]{:S(2)}, u32[]{:S(2)}) collective-permute-start(bf16[24,1024]{1,0:T(8,128)(2,1)S(1)} %combine.1.refs_0_), channel_id=1, source_target_pairs={{0,6},{2,0},{4,2},{6,4},{1,7},{3,1},{5,3},{7,5},{8,14},{10,8},{12,... | collective-permute-start | bytes 147464 | tf_op jit(solution)/shard_map/ppermute | solution.py:349
  42.0 5.1 %collective-permute-start.2 = (bf16[24,1024]{1,0:T(8,128)(2,1)S(1)}, bf16[24,1024]{1,0:T(8,128)(2,1)S(1)}, u32[]{:S(2)}, u32[]{:S(2)}) collective-permute-start(bf16[24,1024]{1,0:T(8,128)(2,1)S(1)} %combine.1.refs_0_), channel_id=1, source_target_pairs={{0,4},{2,6},{4,0},{6,2},{1,5},{3,7},{5,1},{7,3},{8,12},{10,14},{12... | collective-permute-start | bytes 147464 | tf_op jit(solution)/shard_map/ppermute | solution.py:349
  42.7 6.6 %collective-permute-start.1 = (bf16[24,1024]{1,0:T(8,128)(2,1)S(1)}, bf16[24,1024]{1,0:T(8,128)(2,1)S(1)}, u32[]{:S(2)}, u32[]{:S(2)}) collective-permute-start(bf16[24,1024]{1,0:T(8,128)(2,1)S(1)} %combine.1.refs_0_), channel_id=1, source_target_pairs={{0,2},{2,4},{4,6},{6,0},{1,3},{3,5},{5,7},{7,1},{8,10},{10,12},{12... | collective-permute-start | bytes 147464 | tf_op jit(solution)/shard_map/ppermute | solution.py:349
  44.2 6.6 %collective-permute-start.4 = (bf16[24,1024]{1,0:T(8,128)(2,1)S(1)}, bf16[24,1024]{1,0:T(8,128)(2,1)S(1)}, u32[]{:S(2)}, u32[]{:S(2)}) collective-permute-start(bf16[24,1024]{1,0:T(8,128)(2,1)S(1)} %combine.1.refs_0_), channel_id=1, source_target_pairs={{0,1},{1,0},{2,3},{3,2},{4,5},{5,4},{6,7},{7,6},{8,9},{9,8},{10,11... | collective-permute-start | bytes 147464 | tf_op jit(solution)/shard_map/ppermute | solution.py:381
  45.8 5.0 %collective-permute-start.7 = (bf16[24,1024]{1,0:T(8,128)(2,1)S(1)}, bf16[24,1024]{1,0:T(8,128)(2,1)S(1)}, u32[]{:S(2)}, u32[]{:S(2)}) collective-permute-start(bf16[24,1024]{1,0:T(8,128)(2,1)S(1)} %collective-permute-done.3.refs_3_), channel_id=1, source_target_pairs={{0,1},{1,0},{2,3},{3,2},{4,5},{5,4},{6,7},{7,6},{8,9},{9,8},{10,11... | collective-permute-start | bytes 147464 | tf_op jit(solution)/shard_map/ppermute | solution.py:381
  47.1 3.7 %collective-permute-start.6 = (bf16[24,1024]{1,0:T(8,128)(2,1)S(1)}, bf16[24,1024]{1,0:T(8,128)(2,1)S(1)}, u32[]{:S(2)}, u32[]{:S(2)}) collective-permute-start(bf16[24,1024]{1,0:T(8,128)(2,1)S(1)} %collective-permute-done.2.refs_2_), channel_id=1, source_target_pairs={{0,1},{1,0},{2,3},{3,2},{4,5},{5,4},{6,7},{7,6},{8,9},{9,8},{10,11... | collective-permute-start | bytes 147464 | tf_op jit(solution)/shard_map/ppermute | solution.py:381
  49.3 2.3 %collective-permute-start.5 = (bf16[24,1024]{1,0:T(8,128)(2,1)S(1)}, bf16[24,1024]{1,0:T(8,128)(2,1)S(1)}, u32[]{:S(2)}, u32[]{:S(2)}) collective-permute-start(bf16[24,1024]{1,0:T(8,128)(2,1)S(1)} %collective-permute-done.1.refs_1_), channel_id=1, source_target_pairs={{0,1},{1,0},{2,3},{3,2},{4,5},{5,4},{6,7},{7,6},{8,9},{9,8},{10,11... | collective-permute-start | bytes 147464 | tf_op jit(solution)/shard_map/ppermute | solution.py:381
  71.2 4.3 %copy-start = (s32[8,48]{1,0:T(8,128)S(1)}, s32[8,48]{1,0:T(8,128)}, u32[]{:S(2)}) copy-start(s32[8,48]{1,0:T(8,128)} %par_ref.5) | copy-start | bytes 4612
  71.2 4.3 %copy-start.1 = (f32[2048]{0:T(1024)S(1)}, f32[2048]{0:T(1024)}, u32[]{:S(2)}) copy-start(f32[2048]{0:T(1024)} %param.22) | copy-start | bytes 24580
  71.2 4.3 %copy-start.2 = (s32[8,48]{1,0:T(8,128)S(1)}, s32[8,48]{1,0:T(8,128)}, u32[]{:S(2)}) copy-start(s32[8,48]{1,0:T(8,128)} %tok_ref.1) | copy-start | bytes 4612
  71.2 4.3 %collective-permute-start.12 = (bf16[4,4,96,256]{3,2,1,0:T(8,128)(2,1)S(1)}, bf16[4,4,96,256]{3,2,1,0:T(8,128)(2,1)S(1)}, u32[]{:S(2)}, u32[]{:S(2)}) collective-permute-start(bf16[4,4,96,256]{3,2,1,0:T(8,128)(2,1)S(1)} %bitcast.17), channel_id=1, source_target_pairs={{0,1},{1,0},{2,3},{3,2},{4,5},{5,4},{6,7},{7,6},{8,9},{9,8},{10,11... | collective-permute-start | bytes 2359304 | tf_op jit(solution)/shard_map/ppermute | solution.py:384

commit v7 on v6

--- a/solution.py
+++ b/solution.py
@@ -177,16 +177,33 @@
     )(parts)
 
 
-def project_kernel(nx, info_ref, *refs):
-    own, other = refs[:nx], refs[nx:2 * nx]
-    ws, (res_ref, out_ref) = refs[2 * nx:-2], refs[-2:]
+def pile_kernel(n, *refs):
+    for i in range(n):
+        refs[-1][i] = refs[i][...]
+
+
+def pile(arrays, after):
+    shape = (len(arrays),) + arrays[0].shape
+    vm = pl.BlockSpec(memory_space=pltpu.VMEM)
+    return pl.pallas_call(
+        functools.partial(pile_kernel, len(arrays)),
+        out_shape=jax.ShapeDtypeStruct(shape, arrays[0].dtype),
+        in_specs=[vm] * len(arrays) + [pl.BlockSpec(memory_space=pl.ANY)] * len(after),
+        out_specs=vm,
+        compiler_params=pltpu.CompilerParams(vmem_limit_bytes=2 * MB),
+        name="pile",
+    )(*arrays, *after)
+
+
+def project_kernel(info_ref, own, other, *refs):
+    ws, (res_ref, out_ref) = refs[:-2], refs[-2:]
     core, x, y = info_ref[CORE], info_ref[X], info_ref[DP]
-    rows, half = own[0].shape
+    nx, rows, half = own.shape
     ny, deep = len(ws), 2 * ws[0].shape[1]
     run = out_ref.shape[0]
     run = deep // (2 * run)
-    mine = jnp.concatenate([own[s][...] for s in range(nx)], axis=0)
-    theirs = jnp.concatenate([other[s][...] for s in range(nx)], axis=0)
+    mine = jnp.concatenate([own[s] for s in range(nx)], axis=0)
+    theirs = jnp.concatenate([other[s] for s in range(nx)], axis=0)
     acc = None
     for s in range(ny):
         at = lax.rem(y + ny - s, ny)
@@ -205,25 +222,24 @@
 
 
 def project(info, own, other, ws, residual, copies):
-    nx = len(own)
-    rows, half = own[0].shape
+    nx, rows, half = own.shape
     cols = ws[0].shape[2]
-    part = pl.BlockSpec((rows, half), lambda g, i: (0, 0))
+    part = pl.BlockSpec((nx, rows, half), lambda g, i: (0, 0, 0))
     residual = pltpu.with_memory_space_constraint(residual.reshape(-1, rows, residual.shape[2]), pltpu.HBM)
     return pl.pallas_call(
-        functools.partial(project_kernel, nx),
+        project_kernel,
         out_shape=jax.ShapeDtypeStruct((copies, nx, rows, cols), BF),
         grid_spec=pltpu.PrefetchScalarGridSpec(
             num_scalar_prefetch=1,
             grid=(1,),
-            in_specs=[part] * (2 * nx)
+            in_specs=[part, part]
             + [pl.BlockSpec(w.shape, lambda g, i: (0, 0, 0)) for w in ws]
             + [pl.BlockSpec((nx, rows, cols), lambda g, i: (i[Z], 0, i[BLOCK]))],
             out_specs=pl.BlockSpec((copies, nx, rows, cols), lambda g, i: (0, 0, 0, 0)),
         ),
         compiler_params=pltpu.CompilerParams(vmem_limit_bytes=16 * MB),
         name="project",
-    )(info, *own, *other, *ws, residual)
+    )(info, own, other, *ws, residual)
 
 
 def vocab_kernel(
@@ -377,8 +393,8 @@
     (part,) = attend_half(window, info, *args, got=got)
     part = lax.all_to_all(part, ("z", "x"), 0, 0)
     att = combine(part, tokens // (nz * nx), half)
-    own = [att] + [shifted(att, "x", s) for s in range(1, nx)]
-    other = [lax.ppermute(a, "core", swap) for a in own]
+    own = pile([att] + [shifted(att, "x", s) for s in range(1, nx)], ws)
+    other = lax.ppermute(own, "core", swap)
     hid = project(info, own, other, ws, residual, nz * nx).reshape(nz * nx, -1, block)
     hid = lax.all_to_all(hid, ("z", "x"), 0, 0).reshape(nz, nx, -1, block)
     other = lax.ppermute(hid, "core", swap)

time: 93.6 us -> 93.9 us (level)
  waiting for transfers between devices: 12.8 us -> 16.1 us
  starting transfers between devices: 29.4 us -> 26.5 us
    ppermute x6, waiting for transfers between devices: 0.07 us -> 3.09 us  [shifted(): return lax.ppermute(a, axis, [(i, (i + step) % n) for i in range(n)])]
    ppermute x4 -> x1, starting transfers between devices: 6.55 us -> 3.6 us  [local(): other = lax.ppermute(own, 'core', swap)]
  transfers between devices with their start and end apart: 15 -> 12, of which waited for: 5 -> 6; matrix products, arithmetic and copies ran while one was open for 0% -> 0% of each run, Pallas kernels for 9% -> 9%
where the time goes in v7:
time: 93.9 us; the launch traced here: 93.3 us
  blocking collectives  28.5 us (30%)
  starting transfers between devices  26.5 us (28%)
  Pallas kernels  20.7 us (22%)
  waiting for transfers between devices  16.1 us (17%)
    all_to_all x1, blocking collectives, local(): hid = lax.all_to_all(hid, ('z', 'x'), 0, 0).reshape(nz, nx, -1, block)  17.8 us
    all_to_all x1, blocking collectives, local(): stats = jnp.sum(lax.all_to_all(stats, ('z', 'x', 'core'), 0, 0), axis=0)  10.7 us
    pallas_call x2, Pallas kernels, attend_half(): pl.pallas_call(functools.partial(attend_kernel, window, add), out_shape=o...  9.71 us
    all_to_all x1, starting transfers between devices, local(): w = lax.all_to_all(w.reshape((nz * nx,) + w.shape[2:]), ('z', 'x'), 0, 0)  7.68 us
    ppermute x6, starting transfers between devices, shifted(): return lax.ppermute(a, axis, [(i, (i + step) % n) for i in range(n)])  7.51 us
    all_to_all x1, waiting for transfers between devices, local(): part = lax.all_to_all(part, ('z', 'x'), 0, 0)  7.27 us
    pallas_call x1, Pallas kernels, vocab(): pl.pallas_call(vocab_kernel, out_shape=(jax.ShapeDtypeStruct((tokens, wid...  6.16 us
    all_to_all x1, waiting for transfers between devices, local(): w = lax.all_to_all(w.reshape((nz * nx,) + w.shape[2:]), ('z', 'x'), 0, 0)  3.65 us
  transfers between devices with their start and end apart: 12, of which 6 were waited for; matrix products, arithmetic and copies ran while one was open for 0% of the time, Pallas kernels for 9%

profile of v7, /device:TPU:1, one launch (start us, length us, event | category | flops | bytes accessed | tf_op | source)
XLA Modules:
  0.0 93.3 jit_solution(9298537459516806595)
XLA Ops:
  0.6 0.1 stack.41.info_ref
  0.7 4.8 %attend_theirs.1 = (bf16[16,200,128]{2,1,0:T(8,128)(2,1)S(1)}, bf16[4,4,2,16,256]{4,3,2,1,0:T(8,128)(2,1)}) custom-call(s32[8]{0:T(128)S(1)} %stack.41.info_ref, s32[8]{0:T(128)} %len_ref.3, s32[8,48]{1,0:T(8,128)} %par_ref.5, bf16[8,48,2048]{2,1,0:T(8,128)(2,1)} %q_ref.3, bf16[8,128,2048]{2,1,0:T(8,128)(2,1)} %k_ref.3, bf16[8,128,2048]{2,1,0:T(8,128)(2,1)} %v_ref.3, ...), custom_call_target="tpu_custom_call" | custom-call | tf_op jit(solution)/shard_map/attend_theirs/pallas_call | solution.py:144
  5.6 1.4 %collective-permute-start = (bf16[16,200,128]{2,1,0:T(8,128)(2,1)S(1)}, bf16[16,200,128]{2,1,0:T(8,128)(2,1)S(1)}, u32[]{:S(2)}, u32[]{:S(2)}) collective-permute-start(bf16[16,200,128]{2,1,0:T(8,128)(2,1)S(1)} %get-tuple-element.6), channel_id=1, source_target_pairs={{0,1},{1,0},{2,3},{3,2},{4,5},{5,4},{6,7},{7,6},{8,9},{9,8},{10,11... | collective-permute-start | bytes 2457608 | tf_op jit(solution)/shard_map/ppermute | solution.py:389
  7.0 7.7 %all-to-all-start.1 = ((bf16[16,2,16,256]{3,2,1,0:T(8,128)(2,1)}), bf16[16,2,16,256]{3,2,1,0:T(8,128)(2,1)S(1)}, u32[]{:S(2)}, u32[]{:S(2)}) async-start(bf16[16,2,16,256]{3,2,1,0:T(8,128)(2,1)} %bitcast.8), calls=%async_computation.1 | async-start | bytes 524288 | tf_op jit(solution)/shard_map/all_to_all | solution.py:390
  14.7 0.0 collective-permute-done.refs_0_
  14.7 4.9 %attend_mine.1 = bf16[16,200,128]{2,1,0:T(8,128)(2,1)} custom-call(s32[8]{0:T(128)S(1)} %stack.41.info_ref, s32[8]{0:T(128)} %len_ref.3, s32[8,48]{1,0:T(8,128)} %par_ref.5, bf16[8,48,2048]{2,1,0:T(8,128)(2,1)} %q_ref.3, bf16[8,128,2048]{2,1,0:T(8,128)(2,1)} %k_ref.3, bf16[8,128,2048]{2,1,0:T(8,128)(2,1)} %v_ref.3, bf16[8,48,2048]{2,1,0:T(8,128)(2,1)} %nk_ref.3, ...), custom_call_target="tpu_custom_call" | custom-call | tf_op jit(solution)/shard_map/attend_mine/pallas_call | solution.py:144
  19.6 3.6 %all-to-all-done.1 = bf16[16,2,16,256]{3,2,1,0:T(8,128)(2,1)S(1)} async-done(((bf16[16,2,16,256]{3,2,1,0:T(8,128)(2,1)}), bf16[16,2,16,256]{3,2,1,0:T(8,128)(2,1)S(1)}, u32[]{:S(2)}, u32[]{:S(2)}) %all-to-all-start.1) | async-done | bytes 262176 | tf_op jit(solution)/shard_map/all_to_all | solution.py:390
  23.2 3.6 %all-to-all-start = ((bf16[16,200,128]{2,1,0:T(8,128)(2,1)}), bf16[16,200,128]{2,1,0:T(8,128)(2,1)S(1)}, u32[]{:S(2)}, u32[]{:S(2)}) async-start(bf16[16,200,128]{2,1,0:T(8,128)(2,1)} %attend_mine.1), calls=%async_computation | async-start | bytes 1638400 | tf_op jit(solution)/shard_map/all_to_all | solution.py:394
  26.9 1.2 %collective-permute-start.4 = (bf16[256,256]{1,0:T(8,128)(2,1)S(1)}, bf16[256,256]{1,0:T(8,128)(2,1)S(1)}, u32[]{:S(2)}, u32[]{:S(2)}) collective-permute-start(bf16[256,256]{1,0:T(8,128)(2,1)S(1)} %bitcast.24), channel_id=1, source_target_pairs={{0,1},{1,0},{2,3},{3,2},{4,5},{5,4},{6,7},{7,6},{8,9},{9,8},{10,11... | collective-permute-start | bytes 393224 | tf_op jit(solution)/shard_map/ppermute | solution.py:391
  28.0 1.0 %collective-permute-done.4 = bf16[256,256]{1,0:T(8,128)(2,1)S(1)} collective-permute-done((bf16[256,256]{1,0:T(8,128)(2,1)S(1)}, bf16[256,256]{1,0:T(8,128)(2,1)S(1)}, u32[]{:S(2)}, u32[]{:S(2)}) %collective-permute-start.4) | collective-permute-done | bytes 131104 | tf_op jit(solution)/shard_map/ppermute | solution.py:391
  29.1 2.8 %collective-permute-start.7 = (bf16[2,256,256]{2,1,0:T(8,128)(2,1)S(1)}, bf16[2,256,256]{2,1,0:T(8,128)(2,1)S(1)}, u32[]{:S(2)}, u32[]{:S(2)}) collective-permute-start(bf16[2,256,256]{2,1,0:T(8,128)(2,1)S(1)} %pad_maximum_fusion.refs_4_.refs_0_), channel_id=1, source_target_pairs={{0,96},{32,0},{64,32},{96,64},{1,97},{33,1},{65,33},{97,65},{2,98}... | collective-permute-start | bytes 786440 | tf_op jit(solution)/shard_map/ppermute | solution.py:365
  31.9 0.4 collective-permute-start.6
  32.2 0.7 collective-permute-start.5
  32.9 7.3 %all-to-all-done.parts_ref = bf16[16,200,128]{2,1,0:T(8,128)(2,1)S(1)} async-done(((bf16[16,200,128]{2,1,0:T(8,128)(2,1)}), bf16[16,200,128]{2,1,0:T(8,128)(2,1)S(1)}, u32[]{:S(2)}, u32[]{:S(2)}) %all-to-all-start) | async-done | bytes 819232 | tf_op jit(solution)/shard_map/all_to_all | solution.py:394
  40.2 0.3 combine.1.refs_0_
  40.5 1.5 %collective-permute-start.3 = (bf16[24,1024]{1,0:T(8,128)(2,1)S(1)}, bf16[24,1024]{1,0:T(8,128)(2,1)S(1)}, u32[]{:S(2)}, u32[]{:S(2)}) collective-permute-start(bf16[24,1024]{1,0:T(8,128)(2,1)S(1)} %combine.1.refs_0_), channel_id=1, source_target_pairs={{0,6},{2,0},{4,2},{6,4},{1,7},{3,1},{5,3},{7,5},{8,14},{10,8},{12,... | collective-permute-start | bytes 147464 | tf_op jit(solution)/shard_map/ppermute | solution.py:365
  41.9 0.7 collective-permute-start.2
  42.6 0.1 collective-permute-done.7.refs_7_.refs_3_
  42.7 1.5 %collective-permute-start.1 = (bf16[24,1024]{1,0:T(8,128)(2,1)S(1)}, bf16[24,1024]{1,0:T(8,128)(2,1)S(1)}, u32[]{:S(2)}, u32[]{:S(2)}) collective-permute-start(bf16[24,1024]{1,0:T(8,128)(2,1)S(1)} %combine.1.refs_0_), channel_id=1, source_target_pairs={{0,2},{2,4},{4,6},{6,0},{1,3},{3,5},{5,7},{7,1},{8,10},{10,12},{12... | collective-permute-start | bytes 147464 | tf_op jit(solution)/shard_map/ppermute | solution.py:365
  44.2 0.0 collective-permute-done.6.refs_6_.refs_2_
  44.2 3.0 %collective-permute-done.5.refs_5_.refs_1_ = bf16[2,256,256]{2,1,0:T(8,128)(2,1)S(1)} collective-permute-done((bf16[2,256,256]{2,1,0:T(8,128)(2,1)S(1)}, bf16[2,256,256]{2,1,0:T(8,128)(2,1)S(1)}, u32[]{:S(2)}, u32[]{:S(2)}) %collective-permute-start.5) | collective-permute-done | bytes 262176 | tf_op jit(solution)/shard_map/ppermute | solution.py:365
  47.2 0.0 collective-permute-done.2.refs_2_
  47.2 0.0 collective-permute-done.1.refs_1_
  47.3 3.6 %collective-permute-start.8 = (bf16[4,24,1024]{2,1,0:T(8,128)(2,1)S(1)}, bf16[4,24,1024]{2,1,0:T(8,128)(2,1)S(1)}, u32[]{:S(2)}, u32[]{:S(2)}) collective-permute-start(bf16[4,24,1024]{2,1,0:T(8,128)(2,1)S(1)} %pile.1.own), channel_id=1, source_target_pairs={{0,1},{1,0},{2,3},{3,2},{4,5},{5,4},{6,7},{7,6},{8,9},{9,8},{10,11... | collective-permute-start | bytes 589832 | tf_op jit(solution)/shard_map/ppermute | solution.py:397
  50.9 1.1 %collective-permute-done.8.other = bf16[4,24,1024]{2,1,0:T(8,128)(2,1)S(1)} collective-permute-done((bf16[4,24,1024]{2,1,0:T(8,128)(2,1)S(1)}, bf16[4,24,1024]{2,1,0:T(8,128)(2,1)S(1)}, u32[]{:S(2)}, u32[]{:S(2)}) %collective-permute-start.8) | collective-permute-done | bytes 196640 | tf_op jit(solution)/shard_map/ppermute | solution.py:397
  51.9 1.7 %project.1 = bf16[16,4,24,256]{3,2,1,0:T(8,128)(2,1)S(1)} custom-call(s32[8]{0:T(128)S(1)} %stack.41.info_ref, bf16[4,24,1024]{2,1,0:T(8,128)(2,1)S(1)} %pile.1.own, bf16[4,24,1024]{2,1,0:T(8,128)(2,1)S(1)} %collective-permute-done.8.other, bf16[2,256,256]{2,1,0:T(8,128)(2,1)S(1)} %pad_maximum_fusion.refs_4_.refs_0_, ...), custom_call_target="tpu_custom_call" | custom-call | tf_op jit(solution)/shard_map/project/pallas_call | solution.py:229
  53.6 17.8 %all_to_all.20 = bf16[16,96,256]{2,1,0:T(8,128)(2,1)S(1)} all-to-all(bf16[16,96,256]{2,1,0:T(8,128)(2,1)S(1)} %bitcast.20), channel_id=1, replica_groups=mesh['dp'=4,'z'=4,'x'=4,'core'=2] {'z','x'}, dimensions={0} | all-to-all | bytes 1572864 | tf_op jit(solution)/shard_map/all_to_all | solution.py:399
  71.5 1.5 %collective-permute-start.9 = (bf16[4,4,96,256]{3,2,1,0:T(8,128)(2,1)S(1)}, bf16[4,4,96,256]{3,2,1,0:T(8,128)(2,1)S(1)}, u32[]{:S(2)}, u32[]{:S(2)}) collective-permute-start(bf16[4,4,96,256]{3,2,1,0:T(8,128)(2,1)S(1)} %bitcast.17), channel_id=1, source_target_pairs={{0,1},{1,0},{2,3},{3,2},{4,5},{5,4},{6,7},{7,6},{8,9},{9,8},{10,11... | collective-permute-start | bytes 2359304 | tf_op jit(solution)/shard_map/ppermute | solution.py:400
  72.9 2.8 %fetch.1.w_ref = bf16[2048,1536]{1,0:T(8,128)(2,1)S(1)} custom-call(bf16[2048,2432]{1,0:T(8,128)(2,1)} %more_ref.1, bf16[4,4,96,256]{3,2,1,0:T(8,128)(2,1)S(1)} %bitcast.18), custom_call_target="tpu_custom_call" | custom-call | tf_op jit(solution)/shard_map/fetch/pallas_call | solution.py:352
  75.8 6.2 %vocab.1 = (bf16[384,2048]{1,0:T(8,128)(2,1)}, f32[32,8,128]{2,1,0:T(8,128)S(1)}) custom-call(s32[8]{0:T(128)S(1)} %stack.41.info_ref, bf16[4,4,96,256]{3,2,1,0:T(8,128)(2,1)S(1)} %bitcast.19, bf16[4,4,96,256]{3,2,1,0:T(8,128)(2,1)S(1)} %collective-permute-done.9.theirs_ref, f32[1,2048]{1,0:T(1,128)S(1)} %bitcast.21, s32[8,48]{1,0:T(8,128)S(1)} %copy-done.2, ...), custom_call_target="tpu_custom_call" | custom-call | tf_op jit(solution)/shard_map/vocab/pallas_call | solution.py:325
  82.0 10.7 %all_to_all.21 = f32[32,8,128]{2,1,0:T(8,128)S(1)} all-to-all(f32[32,8,128]{2,1,0:T(8,128)S(1)} %get-tuple-element.9), channel_id=1, replica_groups=mesh['dp'=4,'z'=4,'x'=4,'core'=2] {'z','x','core'}, dimensions={0} | all-to-all | bytes 262144 | tf_op jit(solution)/shard_map/all_to_all | solution.py:403
  92.7 0.7 log_subtract_fusion
  (12 shorter events, 0.1 us)
Async XLA Ops:
  5.6 9.1 %collective-permute-start = (bf16[16,200,128]{2,1,0:T(8,128)(2,1)S(1)}, bf16[16,200,128]{2,1,0:T(8,128)(2,1)S(1)}, u32[]{:S(2)}, u32[]{:S(2)}) collective-permute-start(bf16[16,200,128]{2,1,0:T(8,128)(2,1)S(1)} %get-tuple-element.6), channel_id=1, source_target_pairs={{0,1},{1,0},{2,3},{3,2},{4,5},{5,4},{6,7},{7,6},{8,9},{9,8},{10,11... | collective-permute-start | bytes 2457608 | tf_op jit(solution)/shard_map/ppermute | solution.py:389
  7.0 16.2 %all-to-all-start.1 = ((bf16[16,2,16,256]{3,2,1,0:T(8,128)(2,1)}), bf16[16,2,16,256]{3,2,1,0:T(8,128)(2,1)S(1)}, u32[]{:S(2)}, u32[]{:S(2)}) async-start(bf16[16,2,16,256]{3,2,1,0:T(8,128)(2,1)} %bitcast.8), calls=%async_computation.1 | async-start | bytes 524288 | tf_op jit(solution)/shard_map/all_to_all | solution.py:390
  23.2 17.0 %all-to-all-start = ((bf16[16,200,128]{2,1,0:T(8,128)(2,1)}), bf16[16,200,128]{2,1,0:T(8,128)(2,1)S(1)}, u32[]{:S(2)}, u32[]{:S(2)}) async-start(bf16[16,200,128]{2,1,0:T(8,128)(2,1)} %attend_mine.1), calls=%async_computation | async-start | bytes 1638400 | tf_op jit(solution)/shard_map/all_to_all | solution.py:394
  26.9 2.2 %collective-permute-start.4 = (bf16[256,256]{1,0:T(8,128)(2,1)S(1)}, bf16[256,256]{1,0:T(8,128)(2,1)S(1)}, u32[]{:S(2)}, u32[]{:S(2)}) collective-permute-start(bf16[256,256]{1,0:T(8,128)(2,1)S(1)} %bitcast.24), channel_id=1, source_target_pairs={{0,1},{1,0},{2,3},{3,2},{4,5},{5,4},{6,7},{7,6},{8,9},{9,8},{10,11... | collective-permute-start | bytes 393224 | tf_op jit(solution)/shard_map/ppermute | solution.py:391
  29.1 13.6 %collective-permute-start.7 = (bf16[2,256,256]{2,1,0:T(8,128)(2,1)S(1)}, bf16[2,256,256]{2,1,0:T(8,128)(2,1)S(1)}, u32[]{:S(2)}, u32[]{:S(2)}) collective-permute-start(bf16[2,256,256]{2,1,0:T(8,128)(2,1)S(1)} %pad_maximum_fusion.refs_4_.refs_0_), channel_id=1, source_target_pairs={{0,96},{32,0},{64,32},{96,64},{1,97},{33,1},{65,33},{97,65},{2,98}... | collective-permute-start | bytes 786440 | tf_op jit(solution)/shard_map/ppermute | solution.py:365
  31.9 12.3 %collective-permute-start.6 = (bf16[2,256,256]{2,1,0:T(8,128)(2,1)S(1)}, bf16[2,256,256]{2,1,0:T(8,128)(2,1)S(1)}, u32[]{:S(2)}, u32[]{:S(2)}) collective-permute-start(bf16[2,256,256]{2,1,0:T(8,128)(2,1)S(1)} %pad_maximum_fusion.refs_4_.refs_0_), channel_id=1, source_target_pairs={{0,64},{32,96},{64,0},{96,32},{1,65},{33,97},{65,1},{97,33},{2,66}... | collective-permute-start | bytes 786440 | tf_op jit(solution)/shard_map/ppermute | solution.py:365
  32.2 15.0 %collective-permute-start.5 = (bf16[2,256,256]{2,1,0:T(8,128)(2,1)S(1)}, bf16[2,256,256]{2,1,0:T(8,128)(2,1)S(1)}, u32[]{:S(2)}, u32[]{:S(2)}) collective-permute-start(bf16[2,256,256]{2,1,0:T(8,128)(2,1)S(1)} %pad_maximum_fusion.refs_4_.refs_0_), channel_id=1, source_target_pairs={{0,32},{32,64},{64,96},{96,0},{1,33},{33,65},{65,97},{97,1},{2,34}... | collective-permute-start | bytes 786440 | tf_op jit(solution)/shard_map/ppermute | solution.py:365
  40.5 6.8 %collective-permute-start.3 = (bf16[24,1024]{1,0:T(8,128)(2,1)S(1)}, bf16[24,1024]{1,0:T(8,128)(2,1)S(1)}, u32[]{:S(2)}, u32[]{:S(2)}) collective-permute-start(bf16[24,1024]{1,0:T(8,128)(2,1)S(1)} %combine.1.refs_0_), channel_id=1, source_target_pairs={{0,6},{2,0},{4,2},{6,4},{1,7},{3,1},{5,3},{7,5},{8,14},{10,8},{12,... | collective-permute-start | bytes 147464 | tf_op jit(solution)/shard_map/ppermute | solution.py:365
  41.9 5.3 %collective-permute-start.2 = (bf16[24,1024]{1,0:T(8,128)(2,1)S(1)}, bf16[24,1024]{1,0:T(8,128)(2,1)S(1)}, u32[]{:S(2)}, u32[]{:S(2)}) collective-permute-start(bf16[24,1024]{1,0:T(8,128)(2,1)S(1)} %combine.1.refs_0_), channel_id=1, source_target_pairs={{0,4},{2,6},{4,0},{6,2},{1,5},{3,7},{5,1},{7,3},{8,12},{10,14},{12... | collective-permute-start | bytes 147464 | tf_op jit(solution)/shard_map/ppermute | solution.py:365
  42.7 4.6 %collective-permute-start.1 = (bf16[24,1024]{1,0:T(8,128)(2,1)S(1)}, bf16[24,1024]{1,0:T(8,128)(2,1)S(1)}, u32[]{:S(2)}, u32[]{:S(2)}) collective-permute-start(bf16[24,1024]{1,0:T(8,128)(2,1)S(1)} %combine.1.refs_0_), channel_id=1, source_target_pairs={{0,2},{2,4},{4,6},{6,0},{1,3},{3,5},{5,7},{7,1},{8,10},{10,12},{12... | collective-permute-start | bytes 147464 | tf_op jit(solution)/shard_map/ppermute | solution.py:365
  47.3 4.7 %collective-permute-start.8 = (bf16[4,24,1024]{2,1,0:T(8,128)(2,1)S(1)}, bf16[4,24,1024]{2,1,0:T(8,128)(2,1)S(1)}, u32[]{:S(2)}, u32[]{:S(2)}) collective-permute-start(bf16[4,24,1024]{2,1,0:T(8,128)(2,1)S(1)} %pile.1.own), channel_id=1, source_target_pairs={{0,1},{1,0},{2,3},{3,2},{4,5},{5,4},{6,7},{7,6},{8,9},{9,8},{10,11... | collective-permute-start | bytes 589832 | tf_op jit(solution)/shard_map/ppermute | solution.py:397
  71.5 4.3 %copy-start = (s32[8,48]{1,0:T(8,128)S(1)}, s32[8,48]{1,0:T(8,128)}, u32[]{:S(2)}) copy-start(s32[8,48]{1,0:T(8,128)} %par_ref.5) | copy-start | bytes 4612
  71.5 4.3 %copy-start.1 = (f32[2048]{0:T(1024)S(1)}, f32[2048]{0:T(1024)}, u32[]{:S(2)}) copy-start(f32[2048]{0:T(1024)} %param.22) | copy-start | bytes 24580
  71.5 4.3 %copy-start.2 = (s32[8,48]{1,0:T(8,128)S(1)}, s32[8,48]{1,0:T(8,128)}, u32[]{:S(2)}) copy-start(s32[8,48]{1,0:T(8,128)} %tok_ref.1) | copy-start | bytes 4612
  71.5 4.3 %collective-permute-start.9 = (bf16[4,4,96,256]{3,2,1,0:T(8,128)(2,1)S(1)}, bf16[4,4,96,256]{3,2,1,0:T(8,128)(2,1)S(1)}, u32[]{:S(2)}, u32[]{:S(2)}) collective-permute-start(bf16[4,4,96,256]{3,2,1,0:T(8,128)(2,1)S(1)} %bitcast.17), channel_id=1, source_target_pairs={{0,1},{1,0},{2,3},{3,2},{4,5},{5,4},{6,7},{7,6},{8,9},{9,8},{10,11... | collective-permute-start | bytes 2359304 | tf_op jit(solution)/shard_map/ppermute | solution.py:400

commit v8 on v7

--- a/solution.py
+++ b/solution.py
@@ -23,17 +23,15 @@
         got_ref, out_ref, anc_ref = refs
     else:
         w_ref, out_ref, spread_ref, anc_ref = refs
-        nz, nx, _, _, block = spread_ref.shape
+        nz, nx, nc, _, block = spread_ref.shape
 
         @pl.when(step == 0)
         def _():
-            for x in range(nx):
-                a = w_ref[:, x * block:(x + 1) * block]
-                b = w_ref[:, (nx + x) * block:(nx + x + 1) * block]
-                low = info_ref[CORE] == 0
-                for z in range(nz):
-                    spread_ref[z, x, 0] = jnp.where(low, a, b)
-                    spread_ref[z, x, 1] = jnp.where(low, b, a)
+            for c in range(nc):
+                for x in range(nx):
+                    at = (c * nx + x) * block
+                    for z in range(nz):
+                        spread_ref[z, x, c] = w_ref[:, at:at + block]
 
     first = info_ref[FIRST]
     treq = info_ref[TREQ]
@@ -199,9 +197,7 @@
     ws, (res_ref, out_ref) = refs[:-2], refs[-2:]
     core, x, y = info_ref[CORE], info_ref[X], info_ref[DP]
     nx, rows, half = own.shape
-    ny, deep = len(ws), 2 * ws[0].shape[1]
-    run = out_ref.shape[0]
-    run = deep // (2 * run)
+    ny, deep = len(ws), ws[0].shape[0]
     mine = jnp.concatenate([own[s] for s in range(nx)], axis=0)
     theirs = jnp.concatenate([other[s] for s in range(nx)], axis=0)
     acc = None
@@ -209,10 +205,7 @@
         at = lax.rem(y + ny - s, ny)
         a = jnp.where(core == at // 2, mine, theirs)
         a = jnp.where(at % 2 == 0, a[:, :deep], a[:, deep:])
-        even = jnp.where(core == 0, ws[s][0], ws[s][1])
-        odd = jnp.where(core == 0, ws[s][1], ws[s][0])
-        w = [b[i:i + run] for i in range(0, deep // 2, run) for b in (even, odd)]
-        part = jnp.dot(a, jnp.concatenate(w, axis=0), preferred_element_type=F32)
+        part = jnp.dot(a, ws[s][...], preferred_element_type=F32)
         acc = part if acc is None else acc + part
     for s in range(nx):
         at = lax.rem(x + nx - s, nx)
@@ -223,7 +216,7 @@
 
 def project(info, own, other, ws, residual, copies):
     nx, rows, half = own.shape
-    cols = ws[0].shape[2]
+    cols = ws[0].shape[1]
     part = pl.BlockSpec((nx, rows, half), lambda g, i: (0, 0, 0))
     residual = pltpu.with_memory_space_constraint(residual.reshape(-1, rows, residual.shape[2]), pltpu.HBM)
     return pl.pallas_call(
@@ -233,7 +226,7 @@
             num_scalar_prefetch=1,
             grid=(1,),
             in_specs=[part, part]
-            + [pl.BlockSpec(w.shape, lambda g, i: (0, 0, 0)) for w in ws]
+            + [pl.BlockSpec(w.shape, lambda g, i: (0, 0)) for w in ws]
             + [pl.BlockSpec((nx, rows, cols), lambda g, i: (i[Z], 0, i[BLOCK]))],
             out_specs=pl.BlockSpec((copies, nx, rows, cols), lambda g, i: (0, 0, 0, 0)),
         ),
@@ -387,8 +380,7 @@
     spread = (nz, nx, nc, out_weight.shape[0], block)
     send, w = attend_half(window, info, *args, w=out_weight, spread=spread)
     got = lax.ppermute(send, "core", swap)
-    w = lax.all_to_all(w.reshape((nz * nx,) + w.shape[2:]), ("z", "x"), 0, 0)
-    w = jnp.stack([w[:, 0].reshape(-1, block), lax.ppermute(w[:, 1].reshape(-1, block), "core", swap)])
+    w = lax.all_to_all(w.reshape(shards, -1, block), ("z", "x", "core"), 0, 0).reshape(-1, block)
     ws = [w] + [shifted(w, "dp", s) for s in range(1, ny)]
     (part,) = attend_half(window, info, *args, got=got)
     part = lax.all_to_all(part, ("z", "x"), 0, 0)

time: 93.9 us -> 93.3 us (level)
  waiting for transfers between devices: 16.1 us -> 19.9 us
  starting transfers between devices: 26.5 us -> 23.2 us
  blocking collectives: 28.5 us -> 27.4 us
    all_to_all x1, waiting for transfers between devices: 7.27 us -> 10.5 us  [local(): part = lax.all_to_all(part, ('z', 'x'), 0, 0)]
    ppermute x6, starting transfers between devices: 7.51 us -> 6.07 us  [shifted(): return lax.ppermute(a, axis, [(i, (i + step) % n) for i in range(n)])]
    ppermute x6, waiting for transfers between devices: 3.09 us -> 4.35 us  [shifted(): return lax.ppermute(a, axis, [(i, (i + step) % n) for i in range(n)])]
    ppermute x1 -> x0, starting transfers between devices: 1.18 us -> none  [local(): lax.ppermute(w[:, 1].reshape(-1, block), 'core', swap)]
    all_to_all x1, blocking collectives: 17.8 us -> 16.7 us  [local(): hid = lax.all_to_all(hid, ('z', 'x'), 0, 0).reshape(nz, nx, -1, block)]
    ppermute x1 -> x0, waiting for transfers between devices: 0.99 us -> none  [local(): lax.ppermute(w[:, 1].reshape(-1, block), 'core', swap)]
  transfers between devices with their start and end apart: 12 -> 11, of which waited for: 6 -> 6; matrix products, arithmetic and copies ran while one was open for 0% -> 0% of each run, Pallas kernels for 9% -> 9%
where the time goes in v8:
time: 93.3 us; the launch traced here: 92.8 us
  blocking collectives  27.4 us (29%)
  starting transfers between devices  23.2 us (25%)
  Pallas kernels  20.7 us (22%)
  waiting for transfers between devices  19.9 us (21%)
    all_to_all x1, blocking collectives, local(): hid = lax.all_to_all(hid, ('z', 'x'), 0, 0).reshape(nz, nx, -1, block)  16.7 us
    all_to_all x1, blocking collectives, local(): stats = jnp.sum(lax.all_to_all(stats, ('z', 'x', 'core'), 0, 0), axis=0)  10.7 us
    all_to_all x1, waiting for transfers between devices, local(): part = lax.all_to_all(part, ('z', 'x'), 0, 0)  10.5 us
    pallas_call x2, Pallas kernels, attend_half(): pl.pallas_call(functools.partial(attend_kernel, window, add), out_shape=o...  9.71 us
    all_to_all x1, starting transfers between devices, local(): lax.all_to_all(w.reshape(shards, -1, block), ('z', 'x', 'core'), 0, 0)  8.12 us
    pallas_call x1, Pallas kernels, vocab(): pl.pallas_call(vocab_kernel, out_shape=(jax.ShapeDtypeStruct((tokens, wid...  6.16 us
    ppermute x6, starting transfers between devices, shifted(): return lax.ppermute(a, axis, [(i, (i + step) % n) for i in range(n)])  6.07 us
    ppermute x6, waiting for transfers between devices, shifted(): return lax.ppermute(a, axis, [(i, (i + step) % n) for i in range(n)])  4.35 us
  transfers between devices with their start and end apart: 11, of which 6 were waited for; matrix products, arithmetic and copies ran while one was open for 0% of the time, Pallas kernels for 9%

profile of v8, /device:TPU:1, one launch (start us, length us, event | category | flops | bytes accessed | tf_op | source)
XLA Modules:
  0.0 92.8 jit_solution(4709106289284353785)
XLA Ops:
  0.6 0.1 stack.35.info_ref
  0.7 4.8 %attend_theirs.1 = (bf16[16,200,128]{2,1,0:T(8,128)(2,1)S(1)}, bf16[4,4,2,16,256]{4,3,2,1,0:T(8,128)(2,1)}) custom-call(s32[8]{0:T(128)S(1)} %stack.35.info_ref, s32[8]{0:T(128)} %len_ref.3, s32[8,48]{1,0:T(8,128)} %par_ref.5, bf16[8,48,2048]{2,1,0:T(8,128)(2,1)} %q_ref.3, bf16[8,128,2048]{2,1,0:T(8,128)(2,1)} %k_ref.3, bf16[8,128,2048]{2,1,0:T(8,128)(2,1)} %v_ref.3, ...), custom_call_target="tpu_custom_call" | custom-call | tf_op jit(solution)/shard_map/attend_theirs/pallas_call | solution.py:142
  5.6 1.4 %collective-permute-start = (bf16[16,200,128]{2,1,0:T(8,128)(2,1)S(1)}, bf16[16,200,128]{2,1,0:T(8,128)(2,1)S(1)}, u32[]{:S(2)}, u32[]{:S(2)}) collective-permute-start(bf16[16,200,128]{2,1,0:T(8,128)(2,1)S(1)} %get-tuple-element.6), channel_id=1, source_target_pairs={{0,1},{1,0},{2,3},{3,2},{4,5},{5,4},{6,7},{7,6},{8,9},{9,8},{10,11... | collective-permute-start | bytes 2457608 | tf_op jit(solution)/shard_map/ppermute | solution.py:382
  7.0 8.1 %all-to-all-start.1 = ((bf16[32,16,256]{2,1,0:T(8,128)(2,1)}), bf16[32,16,256]{2,1,0:T(8,128)(2,1)S(1)}, u32[]{:S(2)}, u32[]{:S(2)}) async-start(bf16[32,16,256]{2,1,0:T(8,128)(2,1)} %bitcast.8), calls=%async_computation.1 | async-start | bytes 524288 | tf_op jit(solution)/shard_map/all_to_all | solution.py:383
  15.1 0.0 collective-permute-done.refs_0_
  15.1 4.9 %attend_mine.1 = bf16[16,200,128]{2,1,0:T(8,128)(2,1)} custom-call(s32[8]{0:T(128)S(1)} %stack.35.info_ref, s32[8]{0:T(128)} %len_ref.3, s32[8,48]{1,0:T(8,128)} %par_ref.5, bf16[8,48,2048]{2,1,0:T(8,128)(2,1)} %q_ref.3, bf16[8,128,2048]{2,1,0:T(8,128)(2,1)} %k_ref.3, bf16[8,128,2048]{2,1,0:T(8,128)(2,1)} %v_ref.3, bf16[8,48,2048]{2,1,0:T(8,128)(2,1)} %nk_ref.3, ...), custom_call_target="tpu_custom_call" | custom-call | tf_op jit(solution)/shard_map/attend_mine/pallas_call | solution.py:142
  20.0 4.0 %all-to-all-done.1 = bf16[32,16,256]{2,1,0:T(8,128)(2,1)S(1)} async-done(((bf16[32,16,256]{2,1,0:T(8,128)(2,1)}), bf16[32,16,256]{2,1,0:T(8,128)(2,1)S(1)}, u32[]{:S(2)}, u32[]{:S(2)}) %all-to-all-start.1) | async-done | bytes 262176 | tf_op jit(solution)/shard_map/all_to_all | solution.py:383
  24.0 3.6 %all-to-all-start = ((bf16[16,200,128]{2,1,0:T(8,128)(2,1)}), bf16[16,200,128]{2,1,0:T(8,128)(2,1)S(1)}, u32[]{:S(2)}, u32[]{:S(2)}) async-start(bf16[16,200,128]{2,1,0:T(8,128)(2,1)} %attend_mine.1), calls=%async_computation | async-start | bytes 1638400 | tf_op jit(solution)/shard_map/all_to_all | solution.py:386
  27.7 2.8 %collective-permute-start.6 = (bf16[512,256]{1,0:T(8,128)(2,1)S(1)}, bf16[512,256]{1,0:T(8,128)(2,1)S(1)}, u32[]{:S(2)}, u32[]{:S(2)}) collective-permute-start(bf16[512,256]{1,0:T(8,128)(2,1)S(1)} %bitcast.19), channel_id=1, source_target_pairs={{0,96},{32,0},{64,32},{96,64},{1,97},{33,1},{65,33},{97,65},{2,98}... | collective-permute-start | bytes 786440 | tf_op jit(solution)/shard_map/ppermute | solution.py:358
  30.4 0.4 collective-permute-start.5
  30.8 0.7 collective-permute-start.4
  31.5 10.5 %all-to-all-done.parts_ref = bf16[16,200,128]{2,1,0:T(8,128)(2,1)S(1)} async-done(((bf16[16,200,128]{2,1,0:T(8,128)(2,1)}), bf16[16,200,128]{2,1,0:T(8,128)(2,1)S(1)}, u32[]{:S(2)}, u32[]{:S(2)}) %all-to-all-start) | async-done | bytes 819232 | tf_op jit(solution)/shard_map/all_to_all | solution.py:386
  42.0 0.3 combine.1.refs_0_
  42.3 0.1 collective-permute-start.3
  42.4 2.0 %collective-permute-start.2 = (bf16[24,1024]{1,0:T(8,128)(2,1)S(1)}, bf16[24,1024]{1,0:T(8,128)(2,1)S(1)}, u32[]{:S(2)}, u32[]{:S(2)}) collective-permute-start(bf16[24,1024]{1,0:T(8,128)(2,1)S(1)} %combine.1.refs_0_), channel_id=1, source_target_pairs={{0,4},{2,6},{4,0},{6,2},{1,5},{3,7},{5,1},{7,3},{8,12},{10,14},{12... | collective-permute-start | bytes 147464 | tf_op jit(solution)/shard_map/ppermute | solution.py:358
  44.4 0.0 collective-permute-done.6.refs_7_.refs_3_
  44.4 0.1 collective-permute-start.1
  44.5 0.0 collective-permute-done.5.refs_6_.refs_2_
  44.5 1.3 %collective-permute-done.4.refs_5_.refs_1_ = bf16[512,256]{1,0:T(8,128)(2,1)S(1)} collective-permute-done((bf16[512,256]{1,0:T(8,128)(2,1)S(1)}, bf16[512,256]{1,0:T(8,128)(2,1)S(1)}, u32[]{:S(2)}, u32[]{:S(2)}) %collective-permute-start.4) | collective-permute-done | bytes 262176 | tf_op jit(solution)/shard_map/ppermute | solution.py:358
  45.8 0.0 collective-permute-done.3.refs_3_
  45.8 1.1 %collective-permute-done.2.refs_2_ = bf16[24,1024]{1,0:T(8,128)(2,1)S(1)} collective-permute-done((bf16[24,1024]{1,0:T(8,128)(2,1)S(1)}, bf16[24,1024]{1,0:T(8,128)(2,1)S(1)}, u32[]{:S(2)}, u32[]{:S(2)}) %collective-permute-start.2) | collective-permute-done | bytes 49184 | tf_op jit(solution)/shard_map/ppermute | solution.py:358
  46.9 2.0 %collective-permute-done.1.refs_1_ = bf16[24,1024]{1,0:T(8,128)(2,1)S(1)} collective-permute-done((bf16[24,1024]{1,0:T(8,128)(2,1)S(1)}, bf16[24,1024]{1,0:T(8,128)(2,1)S(1)}, u32[]{:S(2)}, u32[]{:S(2)}) %collective-permute-start.1) | collective-permute-done | bytes 49184 | tf_op jit(solution)/shard_map/ppermute | solution.py:358
  48.9 2.8 %collective-permute-start.7 = (bf16[4,24,1024]{2,1,0:T(8,128)(2,1)S(1)}, bf16[4,24,1024]{2,1,0:T(8,128)(2,1)S(1)}, u32[]{:S(2)}, u32[]{:S(2)}) collective-permute-start(bf16[4,24,1024]{2,1,0:T(8,128)(2,1)S(1)} %pile.1.own), channel_id=1, source_target_pairs={{0,1},{1,0},{2,3},{3,2},{4,5},{5,4},{6,7},{7,6},{8,9},{9,8},{10,11... | collective-permute-start | bytes 589832 | tf_op jit(solution)/shard_map/ppermute | solution.py:389
  51.7 1.1 %collective-permute-done.7.other = bf16[4,24,1024]{2,1,0:T(8,128)(2,1)S(1)} collective-permute-done((bf16[4,24,1024]{2,1,0:T(8,128)(2,1)S(1)}, bf16[4,24,1024]{2,1,0:T(8,128)(2,1)S(1)}, u32[]{:S(2)}, u32[]{:S(2)}) %collective-permute-start.7) | collective-permute-done | bytes 196640 | tf_op jit(solution)/shard_map/ppermute | solution.py:389
  52.8 1.7 %project.1 = bf16[16,4,24,256]{3,2,1,0:T(8,128)(2,1)S(1)} custom-call(s32[8]{0:T(128)S(1)} %stack.35.info_ref, bf16[4,24,1024]{2,1,0:T(8,128)(2,1)S(1)} %pile.1.own, bf16[4,24,1024]{2,1,0:T(8,128)(2,1)S(1)} %collective-permute-done.7.other, bf16[512,256]{1,0:T(8,128)(2,1)S(1)} %bitcast.23, bf16[512,256]{1,0:T(8,128)(2,1)S(1)} %collective-permute-done.4.refs_5_.refs_1_, ...), custom_call_target="tpu_custom_call" | custom-call | tf_op jit(solution)/shard_map/project/pallas_call | solution.py:222
  54.5 16.7 %all_to_all.20 = bf16[16,96,256]{2,1,0:T(8,128)(2,1)S(1)} all-to-all(bf16[16,96,256]{2,1,0:T(8,128)(2,1)S(1)} %bitcast.18), channel_id=1, replica_groups=mesh['dp'=4,'z'=4,'x'=4,'core'=2] {'z','x'}, dimensions={0} | all-to-all | bytes 1572864 | tf_op jit(solution)/shard_map/all_to_all | solution.py:391
  71.2 1.2 %collective-permute-start.8 = (bf16[4,4,96,256]{3,2,1,0:T(8,128)(2,1)S(1)}, bf16[4,4,96,256]{3,2,1,0:T(8,128)(2,1)S(1)}, u32[]{:S(2)}, u32[]{:S(2)}) collective-permute-start(bf16[4,4,96,256]{3,2,1,0:T(8,128)(2,1)S(1)} %bitcast.15), channel_id=1, source_target_pairs={{0,1},{1,0},{2,3},{3,2},{4,5},{5,4},{6,7},{7,6},{8,9},{9,8},{10,11... | collective-permute-start | bytes 2359304 | tf_op jit(solution)/shard_map/ppermute | solution.py:392
  72.4 2.8 %fetch.1.w_ref = bf16[2048,1536]{1,0:T(8,128)(2,1)S(1)} custom-call(bf16[2048,2432]{1,0:T(8,128)(2,1)} %more_ref.1, bf16[4,4,96,256]{3,2,1,0:T(8,128)(2,1)S(1)} %bitcast.16), custom_call_target="tpu_custom_call" | custom-call | tf_op jit(solution)/shard_map/fetch/pallas_call | solution.py:345
  75.2 0.0 collective-permute-done.8.theirs_ref
  75.2 6.2 %vocab.1 = (bf16[384,2048]{1,0:T(8,128)(2,1)}, f32[32,8,128]{2,1,0:T(8,128)S(1)}) custom-call(s32[8]{0:T(128)S(1)} %stack.35.info_ref, bf16[4,4,96,256]{3,2,1,0:T(8,128)(2,1)S(1)} %bitcast.17, bf16[4,4,96,256]{3,2,1,0:T(8,128)(2,1)S(1)} %collective-permute-done.8.theirs_ref, f32[1,2048]{1,0:T(1,128)S(1)} %bitcast.24, s32[8,48]{1,0:T(8,128)S(1)} %copy-done.2, ...), custom_call_target="tpu_custom_call" | custom-call | tf_op jit(solution)/shard_map/vocab/pallas_call | solution.py:318
  81.4 10.7 %all_to_all.21 = f32[32,8,128]{2,1,0:T(8,128)S(1)} all-to-all(f32[32,8,128]{2,1,0:T(8,128)S(1)} %get-tuple-element.9), channel_id=1, replica_groups=mesh['dp'=4,'z'=4,'x'=4,'core'=2] {'z','x','core'}, dimensions={0} | all-to-all | bytes 262144 | tf_op jit(solution)/shard_map/all_to_all | solution.py:395
  92.1 0.7 log_subtract_fusion
  (8 shorter events, 0.1 us)
Async XLA Ops:
  5.6 9.6 %collective-permute-start = (bf16[16,200,128]{2,1,0:T(8,128)(2,1)S(1)}, bf16[16,200,128]{2,1,0:T(8,128)(2,1)S(1)}, u32[]{:S(2)}, u32[]{:S(2)}) collective-permute-start(bf16[16,200,128]{2,1,0:T(8,128)(2,1)S(1)} %get-tuple-element.6), channel_id=1, source_target_pairs={{0,1},{1,0},{2,3},{3,2},{4,5},{5,4},{6,7},{7,6},{8,9},{9,8},{10,11... | collective-permute-start | bytes 2457608 | tf_op jit(solution)/shard_map/ppermute | solution.py:382
  7.0 17.0 %all-to-all-start.1 = ((bf16[32,16,256]{2,1,0:T(8,128)(2,1)}), bf16[32,16,256]{2,1,0:T(8,128)(2,1)S(1)}, u32[]{:S(2)}, u32[]{:S(2)}) async-start(bf16[32,16,256]{2,1,0:T(8,128)(2,1)} %bitcast.8), calls=%async_computation.1 | async-start | bytes 524288 | tf_op jit(solution)/shard_map/all_to_all | solution.py:383
  24.0 18.0 %all-to-all-start = ((bf16[16,200,128]{2,1,0:T(8,128)(2,1)}), bf16[16,200,128]{2,1,0:T(8,128)(2,1)S(1)}, u32[]{:S(2)}, u32[]{:S(2)}) async-start(bf16[16,200,128]{2,1,0:T(8,128)(2,1)} %attend_mine.1), calls=%async_computation | async-start | bytes 1638400 | tf_op jit(solution)/shard_map/all_to_all | solution.py:386
  27.7 16.7 %collective-permute-start.6 = (bf16[512,256]{1,0:T(8,128)(2,1)S(1)}, bf16[512,256]{1,0:T(8,128)(2,1)S(1)}, u32[]{:S(2)}, u32[]{:S(2)}) collective-permute-start(bf16[512,256]{1,0:T(8,128)(2,1)S(1)} %bitcast.19), channel_id=1, source_target_pairs={{0,96},{32,0},{64,32},{96,64},{1,97},{33,1},{65,33},{97,65},{2,98}... | collective-permute-start | bytes 786440 | tf_op jit(solution)/shard_map/ppermute | solution.py:358
  30.4 14.1 %collective-permute-start.5 = (bf16[512,256]{1,0:T(8,128)(2,1)S(1)}, bf16[512,256]{1,0:T(8,128)(2,1)S(1)}, u32[]{:S(2)}, u32[]{:S(2)}) collective-permute-start(bf16[512,256]{1,0:T(8,128)(2,1)S(1)} %bitcast.20), channel_id=1, source_target_pairs={{0,64},{32,96},{64,0},{96,32},{1,65},{33,97},{65,1},{97,33},{2,66}... | collective-permute-start | bytes 786440 | tf_op jit(solution)/shard_map/ppermute | solution.py:358
  30.8 15.0 %collective-permute-start.4 = (bf16[512,256]{1,0:T(8,128)(2,1)S(1)}, bf16[512,256]{1,0:T(8,128)(2,1)S(1)}, u32[]{:S(2)}, u32[]{:S(2)}) collective-permute-start(bf16[512,256]{1,0:T(8,128)(2,1)S(1)} %bitcast.21), channel_id=1, source_target_pairs={{0,32},{32,64},{64,96},{96,0},{1,33},{33,65},{65,97},{97,1},{2,34}... | collective-permute-start | bytes 786440 | tf_op jit(solution)/shard_map/ppermute | solution.py:358
  42.3 3.5 %collective-permute-start.3 = (bf16[24,1024]{1,0:T(8,128)(2,1)S(1)}, bf16[24,1024]{1,0:T(8,128)(2,1)S(1)}, u32[]{:S(2)}, u32[]{:S(2)}) collective-permute-start(bf16[24,1024]{1,0:T(8,128)(2,1)S(1)} %combine.1.refs_0_), channel_id=1, source_target_pairs={{0,6},{2,0},{4,2},{6,4},{1,7},{3,1},{5,3},{7,5},{8,14},{10,8},{12,... | collective-permute-start | bytes 147464 | tf_op jit(solution)/shard_map/ppermute | solution.py:358
  42.4 4.5 %collective-permute-start.2 = (bf16[24,1024]{1,0:T(8,128)(2,1)S(1)}, bf16[24,1024]{1,0:T(8,128)(2,1)S(1)}, u32[]{:S(2)}, u32[]{:S(2)}) collective-permute-start(bf16[24,1024]{1,0:T(8,128)(2,1)S(1)} %combine.1.refs_0_), channel_id=1, source_target_pairs={{0,4},{2,6},{4,0},{6,2},{1,5},{3,7},{5,1},{7,3},{8,12},{10,14},{12... | collective-permute-start | bytes 147464 | tf_op jit(solution)/shard_map/ppermute | solution.py:358
  44.4 4.5 %collective-permute-start.1 = (bf16[24,1024]{1,0:T(8,128)(2,1)S(1)}, bf16[24,1024]{1,0:T(8,128)(2,1)S(1)}, u32[]{:S(2)}, u32[]{:S(2)}) collective-permute-start(bf16[24,1024]{1,0:T(8,128)(2,1)S(1)} %combine.1.refs_0_), channel_id=1, source_target_pairs={{0,2},{2,4},{4,6},{6,0},{1,3},{3,5},{5,7},{7,1},{8,10},{10,12},{12... | collective-permute-start | bytes 147464 | tf_op jit(solution)/shard_map/ppermute | solution.py:358
  48.9 3.9 %collective-permute-start.7 = (bf16[4,24,1024]{2,1,0:T(8,128)(2,1)S(1)}, bf16[4,24,1024]{2,1,0:T(8,128)(2,1)S(1)}, u32[]{:S(2)}, u32[]{:S(2)}) collective-permute-start(bf16[4,24,1024]{2,1,0:T(8,128)(2,1)S(1)} %pile.1.own), channel_id=1, source_target_pairs={{0,1},{1,0},{2,3},{3,2},{4,5},{5,4},{6,7},{7,6},{8,9},{9,8},{10,11... | collective-permute-start | bytes 589832 | tf_op jit(solution)/shard_map/ppermute | solution.py:389
  71.2 4.0 %copy-start = (s32[8,48]{1,0:T(8,128)S(1)}, s32[8,48]{1,0:T(8,128)}, u32[]{:S(2)}) copy-start(s32[8,48]{1,0:T(8,128)} %par_ref.5) | copy-start | bytes 4612
  71.2 4.0 %copy-start.1 = (f32[2048]{0:T(1024)S(1)}, f32[2048]{0:T(1024)}, u32[]{:S(2)}) copy-start(f32[2048]{0:T(1024)} %param.22) | copy-start | bytes 24580
  71.2 4.0 %copy-start.2 = (s32[8,48]{1,0:T(8,128)S(1)}, s32[8,48]{1,0:T(8,128)}, u32[]{:S(2)}) copy-start(s32[8,48]{1,0:T(8,128)} %tok_ref.1) | copy-start | bytes 4612
  71.2 4.0 %collective-permute-start.8 = (bf16[4,4,96,256]{3,2,1,0:T(8,128)(2,1)S(1)}, bf16[4,4,96,256]{3,2,1,0:T(8,128)(2,1)S(1)}, u32[]{:S(2)}, u32[]{:S(2)}) collective-permute-start(bf16[4,4,96,256]{3,2,1,0:T(8,128)(2,1)S(1)} %bitcast.15), channel_id=1, source_target_pairs={{0,1},{1,0},{2,3},{3,2},{4,5},{5,4},{6,7},{7,6},{8,9},{9,8},{10,11... | collective-permute-start | bytes 2359304 | tf_op jit(solution)/shard_map/ppermute | solution.py:392

commit v9 on v8

--- a/solution.py
+++ b/solution.py
@@ -20,10 +20,11 @@
 def attend_kernel(window, add, info_ref, len_ref, par_ref, q_ref, k_ref, v_ref, nk_ref, nv_ref, *refs):
     step = pl.program_id(0)
     if add:
-        got_ref, out_ref, anc_ref = refs
+        got_ref, out_ref, anc_ref, new_ref, sem = refs
     else:
-        w_ref, out_ref, spread_ref, anc_ref = refs
+        w_ref, out_ref, spread_hbm, anc_ref, new_ref, sem, spread_ref, spread_sem = refs
         nz, nx, nc, _, block = spread_ref.shape
+        leave = pltpu.make_async_copy(spread_ref, spread_hbm, spread_sem)
 
         @pl.when(step == 0)
         def _():
@@ -32,6 +33,7 @@
                     at = (c * nx + x) * block
                     for z in range(nz):
                         spread_ref[z, x, c] = w_ref[:, at:at + block]
+            leave.start()
 
     first = info_ref[FIRST]
     treq = info_ref[TREQ]
@@ -96,6 +98,14 @@
 
         @pl.when(treq // reqs == step)
         def _():
+            half = info_ref[CORE] if add else 1 - info_ref[CORE]
+            at = pl.ds(pl.multiple_of(half * width, 128), width)
+            copies = [
+                pltpu.make_async_copy(ref.at[treq, :, at], new_ref.at[i], sem.at[i])
+                for i, ref in enumerate((nk_ref, nv_ref))
+            ]
+            for copy in copies:
+                copy.start()
             node = lax.broadcasted_iota(jnp.int32, (1, 128), 1)
             anc_ref[...] = jnp.zeros_like(anc_ref)
             anc_ref[0:1, :] = jnp.where(node == 0, 1.0, 0.0)
@@ -109,8 +119,16 @@
             mask = jnp.transpose(anc_ref[...])[:tree, :tree]
             mask = jnp.concatenate([mask, mask], axis=1) > 0.5
             r = lax.rem(treq, reqs)
-            weights = weigh(score(r, lambda cols: nk_ref[0, :, cols]), mask)
-            finish(r, *weights, lambda cols: nv_ref[0, :, cols])
+            for copy in copies:
+                copy.wait()
+            weights = weigh(score(r, lambda cols: new_ref[0, :, cols]), mask)
+            finish(r, *weights, lambda cols: new_ref[1, :, cols])
+
+    if not add:
+
+        @pl.when(step == pl.num_programs(0) - 1)
+        def _():
+            leave.wait()
 
 
 def attend_half(window, info, lengths, parents, q, k, v, nk, nv, got=None, w=None, spread=None):
@@ -122,7 +140,7 @@
     hidx = (lambda i: i[CORE]) if add else (lambda i: 1 - i[CORE])
     qs = pl.BlockSpec((group, tree, half), lambda r, i, l, p: (r, 0, hidx(i)))
     ks = pl.BlockSpec((group, slots, half), lambda r, i, l, p: (r, 0, hidx(i)))
-    ns = pl.BlockSpec((1, tree, half), lambda r, i, l, p: (jnp.clip(i[TREQ], 0, reqs - 1), 0, hidx(i)))
+    ns = pl.BlockSpec(memory_space=pl.ANY)
     lengths, parents, q, k, v, nk, nv = (
         pltpu.with_memory_space_constraint(a, pltpu.HBM) for a in (lengths, parents, q, k, v, nk, nv)
     )
@@ -131,13 +149,15 @@
     in_specs = [qs, ks, ks, ns, ns]
     out_specs = [sums]
     out_shape = [jax.ShapeDtypeStruct((2 * reqs, rows, 128), BF)]
+    scratch = [pltpu.VMEM((128, 128), F32), pltpu.VMEM((2, tree, half), BF), pltpu.SemaphoreType.DMA((2,))]
     if add:
         extra = (got,)
         in_specs.append(sums)
     else:
         extra = (pltpu.with_memory_space_constraint(w, pltpu.HBM),)
         in_specs.append(pl.BlockSpec(w.shape, lambda r, i, l, p: (0, 0)))
-        out_specs.append(pl.BlockSpec(spread, lambda r, i, l, p: (0, 0, 0, 0, 0)))
+        out_specs.append(pl.BlockSpec(memory_space=pl.ANY))
+        scratch += [pltpu.VMEM(spread, w.dtype), pltpu.SemaphoreType.DMA]
         out_shape.append(jax.ShapeDtypeStruct(spread, w.dtype))
     return pl.pallas_call(
         functools.partial(attend_kernel, window, add),
@@ -147,7 +167,7 @@
             grid=(reqs // group,),
             in_specs=in_specs,
             out_specs=out_specs,
-            scratch_shapes=[pltpu.VMEM((128, 128), F32)],
+            scratch_shapes=scratch,
         ),
         compiler_params=pltpu.CompilerParams(vmem_limit_bytes=24 * MB),
         name="attend_mine" if add else "attend_theirs",

time: 93.3 us -> 92.7 us (level)
  Pallas kernels: 20.7 us -> 19.7 us
    pallas_call x2, Pallas kernels: 9.71 us -> 8.71 us  [attend_half(): pl.pallas_call(functools.partial(attend_kernel, window, add), out_shape=o...]
  transfers between devices with their start and end apart: 11 -> 11, of which waited for: 6 -> 6; matrix products, arithmetic and copies ran while one was open for 0% -> 0% of each run, Pallas kernels for 9% -> 8%
where the time goes in v9:
time: 92.7 us; the launch traced here: 92.1 us
  blocking collectives  27.4 us (30%)
  starting transfers between devices  23.3 us (25%)
  waiting for transfers between devices  20.2 us (22%)
  Pallas kernels  19.7 us (21%)
    all_to_all x1, blocking collectives, local(): hid = lax.all_to_all(hid, ('z', 'x'), 0, 0).reshape(nz, nx, -1, block)  16.7 us
    all_to_all x1, blocking collectives, local(): stats = jnp.sum(lax.all_to_all(stats, ('z', 'x', 'core'), 0, 0), axis=0)  10.7 us
    all_to_all x1, waiting for transfers between devices, local(): part = lax.all_to_all(part, ('z', 'x'), 0, 0)  10.5 us
    pallas_call x2, Pallas kernels, attend_half(): pl.pallas_call(functools.partial(attend_kernel, window, add), out_shape=o...  8.71 us
    all_to_all x1, starting transfers between devices, local(): lax.all_to_all(w.reshape(shards, -1, block), ('z', 'x', 'core'), 0, 0)  8.13 us
    pallas_call x1, Pallas kernels, vocab(): pl.pallas_call(vocab_kernel, out_shape=(jax.ShapeDtypeStruct((tokens, wid...  6.15 us
    ppermute x6, starting transfers between devices, shifted(): return lax.ppermute(a, axis, [(i, (i + step) % n) for i in range(n)])  6.08 us
    ppermute x6, waiting for transfers between devices, shifted(): return lax.ppermute(a, axis, [(i, (i + step) % n) for i in range(n)])  4.35 us
  transfers between devices with their start and end apart: 11, of which 6 were waited for; matrix products, arithmetic and copies ran while one was open for 0% of the time, Pallas kernels for 8%

profile of v9, /device:TPU:1, one launch (start us, length us, event | category | flops | bytes accessed | tf_op | source)
XLA Modules:
  0.0 92.1 jit_solution(3155833393072911830)
XLA Ops:
  0.6 0.1 stack.35.info_ref
  0.7 4.1 %attend_theirs.1 = (bf16[16,200,128]{2,1,0:T(8,128)(2,1)S(1)}, bf16[4,4,2,16,256]{4,3,2,1,0:T(8,128)(2,1)}) custom-call(s32[8]{0:T(128)S(1)} %stack.35.info_ref, s32[8]{0:T(128)} %len_ref.3, s32[8,48]{1,0:T(8,128)} %par_ref.5, bf16[8,48,2048]{2,1,0:T(8,128)(2,1)} %q_ref.3, bf16[8,128,2048]{2,1,0:T(8,128)(2,1)} %k_ref.3, bf16[8,128,2048]{2,1,0:T(8,128)(2,1)} %v_ref.3, ...), custom_call_target="tpu_custom_call" | custom-call | tf_op jit(solution)/shard_map/attend_theirs/pallas_call | solution.py:162
  4.8 1.5 %collective-permute-start = (bf16[16,200,128]{2,1,0:T(8,128)(2,1)S(1)}, bf16[16,200,128]{2,1,0:T(8,128)(2,1)S(1)}, u32[]{:S(2)}, u32[]{:S(2)}) collective-permute-start(bf16[16,200,128]{2,1,0:T(8,128)(2,1)S(1)} %get-tuple-element.6), channel_id=1, source_target_pairs={{0,1},{1,0},{2,3},{3,2},{4,5},{5,4},{6,7},{7,6},{8,9},{9,8},{10,11... | collective-permute-start | bytes 2457608 | tf_op jit(solution)/shard_map/ppermute | solution.py:402
  6.3 8.1 %all-to-all-start.1 = ((bf16[32,16,256]{2,1,0:T(8,128)(2,1)}), bf16[32,16,256]{2,1,0:T(8,128)(2,1)S(1)}, u32[]{:S(2)}, u32[]{:S(2)}) async-start(bf16[32,16,256]{2,1,0:T(8,128)(2,1)} %bitcast.8), calls=%async_computation.1 | async-start | bytes 524288 | tf_op jit(solution)/shard_map/all_to_all | solution.py:403
  14.5 0.0 collective-permute-done.refs_0_
  14.5 4.6 %attend_mine.1 = bf16[16,200,128]{2,1,0:T(8,128)(2,1)} custom-call(s32[8]{0:T(128)S(1)} %stack.35.info_ref, s32[8]{0:T(128)} %len_ref.3, s32[8,48]{1,0:T(8,128)} %par_ref.5, bf16[8,48,2048]{2,1,0:T(8,128)(2,1)} %q_ref.3, bf16[8,128,2048]{2,1,0:T(8,128)(2,1)} %k_ref.3, bf16[8,128,2048]{2,1,0:T(8,128)(2,1)} %v_ref.3, bf16[8,48,2048]{2,1,0:T(8,128)(2,1)} %nk_ref.3, ...), custom_call_target="tpu_custom_call" | custom-call | tf_op jit(solution)/shard_map/attend_mine/pallas_call | solution.py:162
  19.1 4.3 %all-to-all-done.1 = bf16[32,16,256]{2,1,0:T(8,128)(2,1)S(1)} async-done(((bf16[32,16,256]{2,1,0:T(8,128)(2,1)}), bf16[32,16,256]{2,1,0:T(8,128)(2,1)S(1)}, u32[]{:S(2)}, u32[]{:S(2)}) %all-to-all-start.1) | async-done | bytes 262176 | tf_op jit(solution)/shard_map/all_to_all | solution.py:403
  23.4 3.6 %all-to-all-start = ((bf16[16,200,128]{2,1,0:T(8,128)(2,1)}), bf16[16,200,128]{2,1,0:T(8,128)(2,1)S(1)}, u32[]{:S(2)}, u32[]{:S(2)}) async-start(bf16[16,200,128]{2,1,0:T(8,128)(2,1)} %attend_mine.1), calls=%async_computation | async-start | bytes 1638400 | tf_op jit(solution)/shard_map/all_to_all | solution.py:406
  27.0 2.8 %collective-permute-start.6 = (bf16[512,256]{1,0:T(8,128)(2,1)S(1)}, bf16[512,256]{1,0:T(8,128)(2,1)S(1)}, u32[]{:S(2)}, u32[]{:S(2)}) collective-permute-start(bf16[512,256]{1,0:T(8,128)(2,1)S(1)} %bitcast.19), channel_id=1, source_target_pairs={{0,96},{32,0},{64,32},{96,64},{1,97},{33,1},{65,33},{97,65},{2,98}... | collective-permute-start | bytes 786440 | tf_op jit(solution)/shard_map/ppermute | solution.py:378
  29.8 0.4 collective-permute-start.5
  30.1 0.7 collective-permute-start.4
  30.8 10.5 %all-to-all-done.parts_ref = bf16[16,200,128]{2,1,0:T(8,128)(2,1)S(1)} async-done(((bf16[16,200,128]{2,1,0:T(8,128)(2,1)}), bf16[16,200,128]{2,1,0:T(8,128)(2,1)S(1)}, u32[]{:S(2)}, u32[]{:S(2)}) %all-to-all-start) | async-done | bytes 819232 | tf_op jit(solution)/shard_map/all_to_all | solution.py:406
  41.3 0.3 combine.1.refs_0_
  41.6 0.1 collective-permute-start.3
  41.7 2.0 %collective-permute-start.2 = (bf16[24,1024]{1,0:T(8,128)(2,1)S(1)}, bf16[24,1024]{1,0:T(8,128)(2,1)S(1)}, u32[]{:S(2)}, u32[]{:S(2)}) collective-permute-start(bf16[24,1024]{1,0:T(8,128)(2,1)S(1)} %combine.1.refs_0_), channel_id=1, source_target_pairs={{0,4},{2,6},{4,0},{6,2},{1,5},{3,7},{5,1},{7,3},{8,12},{10,14},{12... | collective-permute-start | bytes 147464 | tf_op jit(solution)/shard_map/ppermute | solution.py:378
  43.7 0.0 collective-permute-done.6.refs_7_.refs_3_
  43.7 0.1 collective-permute-start.1
  43.9 0.0 collective-permute-done.5.refs_6_.refs_2_
  43.9 1.3 %collective-permute-done.4.refs_5_.refs_1_ = bf16[512,256]{1,0:T(8,128)(2,1)S(1)} collective-permute-done((bf16[512,256]{1,0:T(8,128)(2,1)S(1)}, bf16[512,256]{1,0:T(8,128)(2,1)S(1)}, u32[]{:S(2)}, u32[]{:S(2)}) %collective-permute-start.4) | collective-permute-done | bytes 262176 | tf_op jit(solution)/shard_map/ppermute | solution.py:378
  45.1 0.0 collective-permute-done.3.refs_3_
  45.1 1.1 %collective-permute-done.2.refs_2_ = bf16[24,1024]{1,0:T(8,128)(2,1)S(1)} collective-permute-done((bf16[24,1024]{1,0:T(8,128)(2,1)S(1)}, bf16[24,1024]{1,0:T(8,128)(2,1)S(1)}, u32[]{:S(2)}, u32[]{:S(2)}) %collective-permute-start.2) | collective-permute-done | bytes 49184 | tf_op jit(solution)/shard_map/ppermute | solution.py:378
  46.2 2.0 %collective-permute-done.1.refs_1_ = bf16[24,1024]{1,0:T(8,128)(2,1)S(1)} collective-permute-done((bf16[24,1024]{1,0:T(8,128)(2,1)S(1)}, bf16[24,1024]{1,0:T(8,128)(2,1)S(1)}, u32[]{:S(2)}, u32[]{:S(2)}) %collective-permute-start.1) | collective-permute-done | bytes 49184 | tf_op jit(solution)/shard_map/ppermute | solution.py:378
  48.2 2.8 %collective-permute-start.7 = (bf16[4,24,1024]{2,1,0:T(8,128)(2,1)S(1)}, bf16[4,24,1024]{2,1,0:T(8,128)(2,1)S(1)}, u32[]{:S(2)}, u32[]{:S(2)}) collective-permute-start(bf16[4,24,1024]{2,1,0:T(8,128)(2,1)S(1)} %pile.1.own), channel_id=1, source_target_pairs={{0,1},{1,0},{2,3},{3,2},{4,5},{5,4},{6,7},{7,6},{8,9},{9,8},{10,11... | collective-permute-start | bytes 589832 | tf_op jit(solution)/shard_map/ppermute | solution.py:409
  51.0 1.1 %collective-permute-done.7.other = bf16[4,24,1024]{2,1,0:T(8,128)(2,1)S(1)} collective-permute-done((bf16[4,24,1024]{2,1,0:T(8,128)(2,1)S(1)}, bf16[4,24,1024]{2,1,0:T(8,128)(2,1)S(1)}, u32[]{:S(2)}, u32[]{:S(2)}) %collective-permute-start.7) | collective-permute-done | bytes 196640 | tf_op jit(solution)/shard_map/ppermute | solution.py:409
  52.1 1.7 %project.1 = bf16[16,4,24,256]{3,2,1,0:T(8,128)(2,1)S(1)} custom-call(s32[8]{0:T(128)S(1)} %stack.35.info_ref, bf16[4,24,1024]{2,1,0:T(8,128)(2,1)S(1)} %pile.1.own, bf16[4,24,1024]{2,1,0:T(8,128)(2,1)S(1)} %collective-permute-done.7.other, bf16[512,256]{1,0:T(8,128)(2,1)S(1)} %bitcast.23, bf16[512,256]{1,0:T(8,128)(2,1)S(1)} %collective-permute-done.4.refs_5_.refs_1_, ...), custom_call_target="tpu_custom_call" | custom-call | tf_op jit(solution)/shard_map/project/pallas_call | solution.py:242
  53.8 16.7 %all_to_all.20 = bf16[16,96,256]{2,1,0:T(8,128)(2,1)S(1)} all-to-all(bf16[16,96,256]{2,1,0:T(8,128)(2,1)S(1)} %bitcast.18), channel_id=1, replica_groups=mesh['dp'=4,'z'=4,'x'=4,'core'=2] {'z','x'}, dimensions={0} | all-to-all | bytes 1572864 | tf_op jit(solution)/shard_map/all_to_all | solution.py:411
  70.5 1.2 %collective-permute-start.8 = (bf16[4,4,96,256]{3,2,1,0:T(8,128)(2,1)S(1)}, bf16[4,4,96,256]{3,2,1,0:T(8,128)(2,1)S(1)}, u32[]{:S(2)}, u32[]{:S(2)}) collective-permute-start(bf16[4,4,96,256]{3,2,1,0:T(8,128)(2,1)S(1)} %bitcast.15), channel_id=1, source_target_pairs={{0,1},{1,0},{2,3},{3,2},{4,5},{5,4},{6,7},{7,6},{8,9},{9,8},{10,11... | collective-permute-start | bytes 2359304 | tf_op jit(solution)/shard_map/ppermute | solution.py:412
  71.7 2.8 %fetch.1.w_ref = bf16[2048,1536]{1,0:T(8,128)(2,1)S(1)} custom-call(bf16[2048,2432]{1,0:T(8,128)(2,1)} %more_ref.1, bf16[4,4,96,256]{3,2,1,0:T(8,128)(2,1)S(1)} %bitcast.16), custom_call_target="tpu_custom_call" | custom-call | tf_op jit(solution)/shard_map/fetch/pallas_call | solution.py:365
  74.5 0.0 collective-permute-done.8.theirs_ref
  74.6 6.2 %vocab.1 = (bf16[384,2048]{1,0:T(8,128)(2,1)}, f32[32,8,128]{2,1,0:T(8,128)S(1)}) custom-call(s32[8]{0:T(128)S(1)} %stack.35.info_ref, bf16[4,4,96,256]{3,2,1,0:T(8,128)(2,1)S(1)} %bitcast.17, bf16[4,4,96,256]{3,2,1,0:T(8,128)(2,1)S(1)} %collective-permute-done.8.theirs_ref, f32[1,2048]{1,0:T(1,128)S(1)} %bitcast.24, s32[8,48]{1,0:T(8,128)S(1)} %copy-done.2, ...), custom_call_target="tpu_custom_call" | custom-call | tf_op jit(solution)/shard_map/vocab/pallas_call | solution.py:338
  80.7 10.7 %all_to_all.21 = f32[32,8,128]{2,1,0:T(8,128)S(1)} all-to-all(f32[32,8,128]{2,1,0:T(8,128)S(1)} %get-tuple-element.9), channel_id=1, replica_groups=mesh['dp'=4,'z'=4,'x'=4,'core'=2] {'z','x','core'}, dimensions={0} | all-to-all | bytes 262144 | tf_op jit(solution)/shard_map/all_to_all | solution.py:415
  91.5 0.7 log_subtract_fusion
  (8 shorter events, 0.1 us)
Async XLA Ops:
  4.8 9.6 %collective-permute-start = (bf16[16,200,128]{2,1,0:T(8,128)(2,1)S(1)}, bf16[16,200,128]{2,1,0:T(8,128)(2,1)S(1)}, u32[]{:S(2)}, u32[]{:S(2)}) collective-permute-start(bf16[16,200,128]{2,1,0:T(8,128)(2,1)S(1)} %get-tuple-element.6), channel_id=1, source_target_pairs={{0,1},{1,0},{2,3},{3,2},{4,5},{5,4},{6,7},{7,6},{8,9},{9,8},{10,11... | collective-permute-start | bytes 2457608 | tf_op jit(solution)/shard_map/ppermute | solution.py:402
  6.3 17.0 %all-to-all-start.1 = ((bf16[32,16,256]{2,1,0:T(8,128)(2,1)}), bf16[32,16,256]{2,1,0:T(8,128)(2,1)S(1)}, u32[]{:S(2)}, u32[]{:S(2)}) async-start(bf16[32,16,256]{2,1,0:T(8,128)(2,1)} %bitcast.8), calls=%async_computation.1 | async-start | bytes 524288 | tf_op jit(solution)/shard_map/all_to_all | solution.py:403
  23.4 18.0 %all-to-all-start = ((bf16[16,200,128]{2,1,0:T(8,128)(2,1)}), bf16[16,200,128]{2,1,0:T(8,128)(2,1)S(1)}, u32[]{:S(2)}, u32[]{:S(2)}) async-start(bf16[16,200,128]{2,1,0:T(8,128)(2,1)} %attend_mine.1), calls=%async_computation | async-start | bytes 1638400 | tf_op jit(solution)/shard_map/all_to_all | solution.py:406
  27.0 16.7 %collective-permute-start.6 = (bf16[512,256]{1,0:T(8,128)(2,1)S(1)}, bf16[512,256]{1,0:T(8,128)(2,1)S(1)}, u32[]{:S(2)}, u32[]{:S(2)}) collective-permute-start(bf16[512,256]{1,0:T(8,128)(2,1)S(1)} %bitcast.19), channel_id=1, source_target_pairs={{0,96},{32,0},{64,32},{96,64},{1,97},{33,1},{65,33},{97,65},{2,98}... | collective-permute-start | bytes 786440 | tf_op jit(solution)/shard_map/ppermute | solution.py:378
  29.8 14.1 %collective-permute-start.5 = (bf16[512,256]{1,0:T(8,128)(2,1)S(1)}, bf16[512,256]{1,0:T(8,128)(2,1)S(1)}, u32[]{:S(2)}, u32[]{:S(2)}) collective-permute-start(bf16[512,256]{1,0:T(8,128)(2,1)S(1)} %bitcast.20), channel_id=1, source_target_pairs={{0,64},{32,96},{64,0},{96,32},{1,65},{33,97},{65,1},{97,33},{2,66}... | collective-permute-start | bytes 786440 | tf_op jit(solution)/shard_map/ppermute | solution.py:378
  30.1 15.0 %collective-permute-start.4 = (bf16[512,256]{1,0:T(8,128)(2,1)S(1)}, bf16[512,256]{1,0:T(8,128)(2,1)S(1)}, u32[]{:S(2)}, u32[]{:S(2)}) collective-permute-start(bf16[512,256]{1,0:T(8,128)(2,1)S(1)} %bitcast.21), channel_id=1, source_target_pairs={{0,32},{32,64},{64,96},{96,0},{1,33},{33,65},{65,97},{97,1},{2,34}... | collective-permute-start | bytes 786440 | tf_op jit(solution)/shard_map/ppermute | solution.py:378
  41.6 3.5 %collective-permute-start.3 = (bf16[24,1024]{1,0:T(8,128)(2,1)S(1)}, bf16[24,1024]{1,0:T(8,128)(2,1)S(1)}, u32[]{:S(2)}, u32[]{:S(2)}) collective-permute-start(bf16[24,1024]{1,0:T(8,128)(2,1)S(1)} %combine.1.refs_0_), channel_id=1, source_target_pairs={{0,6},{2,0},{4,2},{6,4},{1,7},{3,1},{5,3},{7,5},{8,14},{10,8},{12,... | collective-permute-start | bytes 147464 | tf_op jit(solution)/shard_map/ppermute | solution.py:378
  41.7 4.5 %collective-permute-start.2 = (bf16[24,1024]{1,0:T(8,128)(2,1)S(1)}, bf16[24,1024]{1,0:T(8,128)(2,1)S(1)}, u32[]{:S(2)}, u32[]{:S(2)}) collective-permute-start(bf16[24,1024]{1,0:T(8,128)(2,1)S(1)} %combine.1.refs_0_), channel_id=1, source_target_pairs={{0,4},{2,6},{4,0},{6,2},{1,5},{3,7},{5,1},{7,3},{8,12},{10,14},{12... | collective-permute-start | bytes 147464 | tf_op jit(solution)/shard_map/ppermute | solution.py:378
  43.7 4.5 %collective-permute-start.1 = (bf16[24,1024]{1,0:T(8,128)(2,1)S(1)}, bf16[24,1024]{1,0:T(8,128)(2,1)S(1)}, u32[]{:S(2)}, u32[]{:S(2)}) collective-permute-start(bf16[24,1024]{1,0:T(8,128)(2,1)S(1)} %combine.1.refs_0_), channel_id=1, source_target_pairs={{0,2},{2,4},{4,6},{6,0},{1,3},{3,5},{5,7},{7,1},{8,10},{10,12},{12... | collective-permute-start | bytes 147464 | tf_op jit(solution)/shard_map/ppermute | solution.py:378
  48.2 3.9 %collective-permute-start.7 = (bf16[4,24,1024]{2,1,0:T(8,128)(2,1)S(1)}, bf16[4,24,1024]{2,1,0:T(8,128)(2,1)S(1)}, u32[]{:S(2)}, u32[]{:S(2)}) collective-permute-start(bf16[4,24,1024]{2,1,0:T(8,128)(2,1)S(1)} %pile.1.own), channel_id=1, source_target_pairs={{0,1},{1,0},{2,3},{3,2},{4,5},{5,4},{6,7},{7,6},{8,9},{9,8},{10,11... | collective-permute-start | bytes 589832 | tf_op jit(solution)/shard_map/ppermute | solution.py:409
  70.5 4.0 %copy-start = (s32[8,48]{1,0:T(8,128)S(1)}, s32[8,48]{1,0:T(8,128)}, u32[]{:S(2)}) copy-start(s32[8,48]{1,0:T(8,128)} %par_ref.5) | copy-start | bytes 4612
  70.5 4.0 %copy-start.1 = (f32[2048]{0:T(1024)S(1)}, f32[2048]{0:T(1024)}, u32[]{:S(2)}) copy-start(f32[2048]{0:T(1024)} %param.22) | copy-start | bytes 24580
  70.5 4.0 %copy-start.2 = (s32[8,48]{1,0:T(8,128)S(1)}, s32[8,48]{1,0:T(8,128)}, u32[]{:S(2)}) copy-start(s32[8,48]{1,0:T(8,128)} %tok_ref.1) | copy-start | bytes 4612
  70.5 4.0 %collective-permute-start.8 = (bf16[4,4,96,256]{3,2,1,0:T(8,128)(2,1)S(1)}, bf16[4,4,96,256]{3,2,1,0:T(8,128)(2,1)S(1)}, u32[]{:S(2)}, u32[]{:S(2)}) collective-permute-start(bf16[4,4,96,256]{3,2,1,0:T(8,128)(2,1)S(1)} %bitcast.15), channel_id=1, source_target_pairs={{0,1},{1,0},{2,3},{3,2},{4,5},{5,4},{6,7},{7,6},{8,9},{9,8},{10,11... | collective-permute-start | bytes 2359304 | tf_op jit(solution)/shard_map/ppermute | solution.py:412

commit v10 on v9

--- a/solution.py
+++ b/solution.py
@@ -235,22 +235,14 @@
 
 
 def project(info, own, other, ws, residual, copies):
-    nx, rows, half = own.shape
-    cols = ws[0].shape[1]
-    part = pl.BlockSpec((nx, rows, half), lambda g, i: (0, 0, 0))
-    residual = pltpu.with_memory_space_constraint(residual.reshape(-1, rows, residual.shape[2]), pltpu.HBM)
+    nx, rows, _ = own.shape
+    vm = pl.BlockSpec(memory_space=pltpu.VMEM)
     return pl.pallas_call(
         project_kernel,
-        out_shape=jax.ShapeDtypeStruct((copies, nx, rows, cols), BF),
-        grid_spec=pltpu.PrefetchScalarGridSpec(
-            num_scalar_prefetch=1,
-            grid=(1,),
-            in_specs=[part, part]
-            + [pl.BlockSpec(w.shape, lambda g, i: (0, 0)) for w in ws]
-            + [pl.BlockSpec((nx, rows, cols), lambda g, i: (i[Z], 0, i[BLOCK]))],
-            out_specs=pl.BlockSpec((copies, nx, rows, cols), lambda g, i: (0, 0, 0, 0)),
-        ),
-        compiler_params=pltpu.CompilerParams(vmem_limit_bytes=16 * MB),
+        out_shape=jax.ShapeDtypeStruct((copies, nx, rows, ws[0].shape[1]), BF),
+        in_specs=[pl.BlockSpec(memory_space=pltpu.SMEM)] + [vm] * (3 + len(ws)),
+        out_specs=vm,
+        compiler_params=pltpu.CompilerParams(vmem_limit_bytes=8 * MB),
         name="project",
     )(info, own, other, *ws, residual)
 
@@ -407,7 +399,11 @@
     att = combine(part, tokens // (nz * nx), half)
     own = pile([att] + [shifted(att, "x", s) for s in range(1, nx)], ws)
     other = lax.ppermute(own, "core", swap)
-    hid = project(info, own, other, ws, residual, nz * nx).reshape(nz * nx, -1, block)
+    rows = tokens // (nz * nx)
+    mine = lax.dynamic_slice(
+        residual.reshape(nz * nx, rows, width), (z * nx, 0, (core * nx + x) * block), (nx, rows, block)
+    )
+    hid = project(info, own, other, ws, mine, nz * nx).reshape(nz * nx, -1, block)
     hid = lax.all_to_all(hid, ("z", "x"), 0, 0).reshape(nz, nx, -1, block)
     other = lax.ppermute(hid, "core", swap)
     scorer = fetch(vocab_weight, hid, 1536)

time: 92.7 us -> 92.7 us (level)
  no operation moved by 1% of the time
where the time goes in v10:
time: 92.7 us; the launch traced here: 92.2 us
  blocking collectives  27.4 us (30%)
  starting transfers between devices  23.3 us (25%)
  waiting for transfers between devices  20.2 us (22%)
  Pallas kernels  19.7 us (21%)
    all_to_all x1, blocking collectives, local(): hid = lax.all_to_all(hid, ('z', 'x'), 0, 0).reshape(nz, nx, -1, block)  16.7 us
    all_to_all x1, blocking collectives, local(): stats = jnp.sum(lax.all_to_all(stats, ('z', 'x', 'core'), 0, 0), axis=0)  10.7 us
    all_to_all x1, waiting for transfers between devices, local(): part = lax.all_to_all(part, ('z', 'x'), 0, 0)  10.5 us
    pallas_call x2, Pallas kernels, attend_half(): pl.pallas_call(functools.partial(attend_kernel, window, add), out_shape=o...  9.59 us
    all_to_all x1, starting transfers between devices, local(): lax.all_to_all(w.reshape(shards, -1, block), ('z', 'x', 'core'), 0, 0)  8.14 us
    pallas_call x1, Pallas kernels, vocab(): pl.pallas_call(vocab_kernel, out_shape=(jax.ShapeDtypeStruct((tokens, wid...  6.16 us
    ppermute x6, starting transfers between devices, shifted(): return lax.ppermute(a, axis, [(i, (i + step) % n) for i in range(n)])  6.07 us
    ppermute x6, waiting for transfers between devices, shifted(): return lax.ppermute(a, axis, [(i, (i + step) % n) for i in range(n)])  4.35 us
  transfers between devices with their start and end apart: 11, of which 6 were waited for; matrix products, arithmetic and copies ran while one was open for 0% of the time, Pallas kernels for 8%

profile of v10, /device:TPU:1, one launch (start us, length us, event | category | flops | bytes accessed | tf_op | source)
XLA Modules:
  0.0 92.2 jit_solution(10937698094321101972)
XLA Ops:
  0.6 0.0 copy-start
  0.7 0.1 stack.35.info_ref
  0.8 5.0 %attend_theirs.1 = (bf16[16,200,128]{2,1,0:T(8,128)(2,1)}, bf16[4,4,2,16,256]{4,3,2,1,0:T(8,128)(2,1)}) custom-call(s32[8]{0:T(128)S(1)} %stack.35.info_ref, s32[8]{0:T(128)} %len_ref.3, s32[8,48]{1,0:T(8,128)} %par_ref.5, bf16[8,48,2048]{2,1,0:T(8,128)(2,1)} %q_ref.3, bf16[8,128,2048]{2,1,0:T(8,128)(2,1)} %k_ref.3, bf16[8,128,2048]{2,1,0:T(8,128)(2,1)} %v_ref.3, ...), custom_call_target="tpu_custom_call" | custom-call | tf_op jit(solution)/shard_map/attend_theirs/pallas_call | solution.py:162
  5.7 1.5 %collective-permute-start = (bf16[16,200,128]{2,1,0:T(8,128)(2,1)}, bf16[16,200,128]{2,1,0:T(8,128)(2,1)S(1)}, u32[]{:S(2)}, u32[]{:S(2)}) collective-permute-start(bf16[16,200,128]{2,1,0:T(8,128)(2,1)} %get-tuple-element.6), channel_id=1, source_target_pairs={{0,1},{1,0},{2,3},{3,2},{4,5},{5,4},{6,7},{7,6},{8,9},{9,8},{10,11... | collective-permute-start | bytes 2457608 | tf_op jit(solution)/shard_map/ppermute | solution.py:394
  7.2 8.1 %all-to-all-start.1 = ((bf16[32,16,256]{2,1,0:T(8,128)(2,1)}), bf16[32,16,256]{2,1,0:T(8,128)(2,1)S(1)}, u32[]{:S(2)}, u32[]{:S(2)}) async-start(bf16[32,16,256]{2,1,0:T(8,128)(2,1)} %bitcast.8), calls=%async_computation.1 | async-start | bytes 524288 | tf_op jit(solution)/shard_map/all_to_all | solution.py:395
  15.3 0.0 collective-permute-done.refs_0_
  15.4 4.6 %attend_mine.1 = bf16[16,200,128]{2,1,0:T(8,128)(2,1)} custom-call(s32[8]{0:T(128)S(1)} %stack.35.info_ref, s32[8]{0:T(128)} %len_ref.3, s32[8,48]{1,0:T(8,128)} %par_ref.5, bf16[8,48,2048]{2,1,0:T(8,128)(2,1)} %q_ref.3, bf16[8,128,2048]{2,1,0:T(8,128)(2,1)} %k_ref.3, bf16[8,128,2048]{2,1,0:T(8,128)(2,1)} %v_ref.3, bf16[8,48,2048]{2,1,0:T(8,128)(2,1)} %nk_ref.3, ...), custom_call_target="tpu_custom_call" | custom-call | tf_op jit(solution)/shard_map/attend_mine/pallas_call | solution.py:162
  20.0 4.3 %all-to-all-done.1 = bf16[32,16,256]{2,1,0:T(8,128)(2,1)S(1)} async-done(((bf16[32,16,256]{2,1,0:T(8,128)(2,1)}), bf16[32,16,256]{2,1,0:T(8,128)(2,1)S(1)}, u32[]{:S(2)}, u32[]{:S(2)}) %all-to-all-start.1) | async-done | bytes 262176 | tf_op jit(solution)/shard_map/all_to_all | solution.py:395
  24.2 3.6 %all-to-all-start = ((bf16[16,200,128]{2,1,0:T(8,128)(2,1)}), bf16[16,200,128]{2,1,0:T(8,128)(2,1)S(1)}, u32[]{:S(2)}, u32[]{:S(2)}) async-start(bf16[16,200,128]{2,1,0:T(8,128)(2,1)} %attend_mine.1), calls=%async_computation | async-start | bytes 1638400 | tf_op jit(solution)/shard_map/all_to_all | solution.py:398
  27.9 2.8 %collective-permute-start.6 = (bf16[512,256]{1,0:T(8,128)(2,1)S(1)}, bf16[512,256]{1,0:T(8,128)(2,1)S(1)}, u32[]{:S(2)}, u32[]{:S(2)}) collective-permute-start(bf16[512,256]{1,0:T(8,128)(2,1)S(1)} %bitcast.20), channel_id=1, source_target_pairs={{0,96},{32,0},{64,32},{96,64},{1,97},{33,1},{65,33},{97,65},{2,98}... | collective-permute-start | bytes 786440 | tf_op jit(solution)/shard_map/ppermute | solution.py:370
  30.7 0.4 collective-permute-start.5
  31.0 0.7 collective-permute-start.4
  31.7 10.5 %all-to-all-done.parts_ref = bf16[16,200,128]{2,1,0:T(8,128)(2,1)S(1)} async-done(((bf16[16,200,128]{2,1,0:T(8,128)(2,1)}), bf16[16,200,128]{2,1,0:T(8,128)(2,1)S(1)}, u32[]{:S(2)}, u32[]{:S(2)}) %all-to-all-start) | async-done | bytes 819232 | tf_op jit(solution)/shard_map/all_to_all | solution.py:398
  42.2 0.3 combine.1.refs_0_
  42.5 0.1 collective-permute-start.3
  42.6 2.0 %collective-permute-start.2 = (bf16[24,1024]{1,0:T(8,128)(2,1)S(1)}, bf16[24,1024]{1,0:T(8,128)(2,1)S(1)}, u32[]{:S(2)}, u32[]{:S(2)}) collective-permute-start(bf16[24,1024]{1,0:T(8,128)(2,1)S(1)} %combine.1.refs_0_), channel_id=1, source_target_pairs={{0,4},{2,6},{4,0},{6,2},{1,5},{3,7},{5,1},{7,3},{8,12},{10,14},{12... | collective-permute-start | bytes 147464 | tf_op jit(solution)/shard_map/ppermute | solution.py:370
  44.6 0.0 collective-permute-done.6.refs_7_.refs_3_
  44.6 0.1 collective-permute-start.1
  44.7 1.3 %collective-permute-done.4.refs_5_.refs_1_ = bf16[512,256]{1,0:T(8,128)(2,1)S(1)} collective-permute-done((bf16[512,256]{1,0:T(8,128)(2,1)S(1)}, bf16[512,256]{1,0:T(8,128)(2,1)S(1)}, u32[]{:S(2)}, u32[]{:S(2)}) %collective-permute-start.4) | collective-permute-done | bytes 262176 | tf_op jit(solution)/shard_map/ppermute | solution.py:370
  46.0 0.0 collective-permute-done.3.refs_3_
  46.0 1.1 %collective-permute-done.2.refs_2_ = bf16[24,1024]{1,0:T(8,128)(2,1)S(1)} collective-permute-done((bf16[24,1024]{1,0:T(8,128)(2,1)S(1)}, bf16[24,1024]{1,0:T(8,128)(2,1)S(1)}, u32[]{:S(2)}, u32[]{:S(2)}) %collective-permute-start.2) | collective-permute-done | bytes 49184 | tf_op jit(solution)/shard_map/ppermute | solution.py:370
  47.1 2.0 %collective-permute-done.1.refs_1_ = bf16[24,1024]{1,0:T(8,128)(2,1)S(1)} collective-permute-done((bf16[24,1024]{1,0:T(8,128)(2,1)S(1)}, bf16[24,1024]{1,0:T(8,128)(2,1)S(1)}, u32[]{:S(2)}, u32[]{:S(2)}) %collective-permute-start.1) | collective-permute-done | bytes 49184 | tf_op jit(solution)/shard_map/ppermute | solution.py:370
  49.1 2.8 %collective-permute-start.7 = (bf16[4,24,1024]{2,1,0:T(8,128)(2,1)S(1)}, bf16[4,24,1024]{2,1,0:T(8,128)(2,1)S(1)}, u32[]{:S(2)}, u32[]{:S(2)}) collective-permute-start(bf16[4,24,1024]{2,1,0:T(8,128)(2,1)S(1)} %pile.1.own), channel_id=1, source_target_pairs={{0,1},{1,0},{2,3},{3,2},{4,5},{5,4},{6,7},{7,6},{8,9},{9,8},{10,11... | collective-permute-start | bytes 589832 | tf_op jit(solution)/shard_map/ppermute | solution.py:401
  51.9 1.1 %collective-permute-done.7.other = bf16[4,24,1024]{2,1,0:T(8,128)(2,1)S(1)} collective-permute-done((bf16[4,24,1024]{2,1,0:T(8,128)(2,1)S(1)}, bf16[4,24,1024]{2,1,0:T(8,128)(2,1)S(1)}, u32[]{:S(2)}, u32[]{:S(2)}) %collective-permute-start.7) | collective-permute-done | bytes 196640 | tf_op jit(solution)/shard_map/ppermute | solution.py:401
  53.0 0.9 project.1
  53.9 16.7 %all_to_all.20 = bf16[16,96,256]{2,1,0:T(8,128)(2,1)S(1)} all-to-all(bf16[16,96,256]{2,1,0:T(8,128)(2,1)S(1)} %bitcast.19), channel_id=1, replica_groups=mesh['dp'=4,'z'=4,'x'=4,'core'=2] {'z','x'}, dimensions={0} | all-to-all | bytes 1572864 | tf_op jit(solution)/shard_map/all_to_all | solution.py:407
  70.6 1.2 %collective-permute-start.8 = (bf16[4,4,96,256]{3,2,1,0:T(8,128)(2,1)S(1)}, bf16[4,4,96,256]{3,2,1,0:T(8,128)(2,1)S(1)}, u32[]{:S(2)}, u32[]{:S(2)}) collective-permute-start(bf16[4,4,96,256]{3,2,1,0:T(8,128)(2,1)S(1)} %bitcast.16), channel_id=1, source_target_pairs={{0,1},{1,0},{2,3},{3,2},{4,5},{5,4},{6,7},{7,6},{8,9},{9,8},{10,11... | collective-permute-start | bytes 2359304 | tf_op jit(solution)/shard_map/ppermute | solution.py:408
  71.8 2.8 %fetch.1.w_ref = bf16[2048,1536]{1,0:T(8,128)(2,1)S(1)} custom-call(bf16[2048,2432]{1,0:T(8,128)(2,1)} %more_ref.1, bf16[4,4,96,256]{3,2,1,0:T(8,128)(2,1)S(1)} %bitcast.17), custom_call_target="tpu_custom_call" | custom-call | tf_op jit(solution)/shard_map/fetch/pallas_call | solution.py:357
  74.6 0.0 collective-permute-done.8.theirs_ref
  74.6 6.2 %vocab.1 = (bf16[384,2048]{1,0:T(8,128)(2,1)}, f32[32,8,128]{2,1,0:T(8,128)S(1)}) custom-call(s32[8]{0:T(128)S(1)} %stack.35.info_ref, bf16[4,4,96,256]{3,2,1,0:T(8,128)(2,1)S(1)} %bitcast.18, bf16[4,4,96,256]{3,2,1,0:T(8,128)(2,1)S(1)} %collective-permute-done.8.theirs_ref, f32[1,2048]{1,0:T(1,128)S(1)} %bitcast.25, s32[8,48]{1,0:T(8,128)S(1)} %copy-done.3, ...), custom_call_target="tpu_custom_call" | custom-call | tf_op jit(solution)/shard_map/vocab/pallas_call | solution.py:330
  80.8 10.7 %all_to_all.21 = f32[32,8,128]{2,1,0:T(8,128)S(1)} all-to-all(f32[32,8,128]{2,1,0:T(8,128)S(1)} %get-tuple-element.9), channel_id=1, replica_groups=mesh['dp'=4,'z'=4,'x'=4,'core'=2] {'z','x','core'}, dimensions={0} | all-to-all | bytes 262144 | tf_op jit(solution)/shard_map/all_to_all | solution.py:411
  91.5 0.7 log_subtract_fusion
  (11 shorter events, 0.1 us)
Async XLA Ops:
  0.6 51.3 %copy-start = (bf16[8,48,2048]{2,1,0:T(8,128)(2,1)S(1)}, bf16[8,48,2048]{2,1,0:T(8,128)(2,1)}, u32[]{:S(2)}) copy-start(bf16[8,48,2048]{2,1,0:T(8,128)(2,1)} %param.20) | copy-start | bytes 4718596
  5.7 9.6 %collective-permute-start = (bf16[16,200,128]{2,1,0:T(8,128)(2,1)}, bf16[16,200,128]{2,1,0:T(8,128)(2,1)S(1)}, u32[]{:S(2)}, u32[]{:S(2)}) collective-permute-start(bf16[16,200,128]{2,1,0:T(8,128)(2,1)} %get-tuple-element.6), channel_id=1, source_target_pairs={{0,1},{1,0},{2,3},{3,2},{4,5},{5,4},{6,7},{7,6},{8,9},{9,8},{10,11... | collective-permute-start | bytes 2457608 | tf_op jit(solution)/shard_map/ppermute | solution.py:394
  7.2 17.0 %all-to-all-start.1 = ((bf16[32,16,256]{2,1,0:T(8,128)(2,1)}), bf16[32,16,256]{2,1,0:T(8,128)(2,1)S(1)}, u32[]{:S(2)}, u32[]{:S(2)}) async-start(bf16[32,16,256]{2,1,0:T(8,128)(2,1)} %bitcast.8), calls=%async_computation.1 | async-start | bytes 524288 | tf_op jit(solution)/shard_map/all_to_all | solution.py:395
  24.2 18.0 %all-to-all-start = ((bf16[16,200,128]{2,1,0:T(8,128)(2,1)}), bf16[16,200,128]{2,1,0:T(8,128)(2,1)S(1)}, u32[]{:S(2)}, u32[]{:S(2)}) async-start(bf16[16,200,128]{2,1,0:T(8,128)(2,1)} %attend_mine.1), calls=%async_computation | async-start | bytes 1638400 | tf_op jit(solution)/shard_map/all_to_all | solution.py:398
  27.9 16.7 %collective-permute-start.6 = (bf16[512,256]{1,0:T(8,128)(2,1)S(1)}, bf16[512,256]{1,0:T(8,128)(2,1)S(1)}, u32[]{:S(2)}, u32[]{:S(2)}) collective-permute-start(bf16[512,256]{1,0:T(8,128)(2,1)S(1)} %bitcast.20), channel_id=1, source_target_pairs={{0,96},{32,0},{64,32},{96,64},{1,97},{33,1},{65,33},{97,65},{2,98}... | collective-permute-start | bytes 786440 | tf_op jit(solution)/shard_map/ppermute | solution.py:370
  30.7 14.1 %collective-permute-start.5 = (bf16[512,256]{1,0:T(8,128)(2,1)S(1)}, bf16[512,256]{1,0:T(8,128)(2,1)S(1)}, u32[]{:S(2)}, u32[]{:S(2)}) collective-permute-start(bf16[512,256]{1,0:T(8,128)(2,1)S(1)} %bitcast.21), channel_id=1, source_target_pairs={{0,64},{32,96},{64,0},{96,32},{1,65},{33,97},{65,1},{97,33},{2,66}... | collective-permute-start | bytes 786440 | tf_op jit(solution)/shard_map/ppermute | solution.py:370
  31.0 15.0 %collective-permute-start.4 = (bf16[512,256]{1,0:T(8,128)(2,1)S(1)}, bf16[512,256]{1,0:T(8,128)(2,1)S(1)}, u32[]{:S(2)}, u32[]{:S(2)}) collective-permute-start(bf16[512,256]{1,0:T(8,128)(2,1)S(1)} %bitcast.22), channel_id=1, source_target_pairs={{0,32},{32,64},{64,96},{96,0},{1,33},{33,65},{65,97},{97,1},{2,34}... | collective-permute-start | bytes 786440 | tf_op jit(solution)/shard_map/ppermute | solution.py:370
  42.5 3.5 %collective-permute-start.3 = (bf16[24,1024]{1,0:T(8,128)(2,1)S(1)}, bf16[24,1024]{1,0:T(8,128)(2,1)S(1)}, u32[]{:S(2)}, u32[]{:S(2)}) collective-permute-start(bf16[24,1024]{1,0:T(8,128)(2,1)S(1)} %combine.1.refs_0_), channel_id=1, source_target_pairs={{0,6},{2,0},{4,2},{6,4},{1,7},{3,1},{5,3},{7,5},{8,14},{10,8},{12,... | collective-permute-start | bytes 147464 | tf_op jit(solution)/shard_map/ppermute | solution.py:370
  42.6 4.5 %collective-permute-start.2 = (bf16[24,1024]{1,0:T(8,128)(2,1)S(1)}, bf16[24,1024]{1,0:T(8,128)(2,1)S(1)}, u32[]{:S(2)}, u32[]{:S(2)}) collective-permute-start(bf16[24,1024]{1,0:T(8,128)(2,1)S(1)} %combine.1.refs_0_), channel_id=1, source_target_pairs={{0,4},{2,6},{4,0},{6,2},{1,5},{3,7},{5,1},{7,3},{8,12},{10,14},{12... | collective-permute-start | bytes 147464 | tf_op jit(solution)/shard_map/ppermute | solution.py:370
  44.6 4.5 %collective-permute-start.1 = (bf16[24,1024]{1,0:T(8,128)(2,1)S(1)}, bf16[24,1024]{1,0:T(8,128)(2,1)S(1)}, u32[]{:S(2)}, u32[]{:S(2)}) collective-permute-start(bf16[24,1024]{1,0:T(8,128)(2,1)S(1)} %combine.1.refs_0_), channel_id=1, source_target_pairs={{0,2},{2,4},{4,6},{6,0},{1,3},{3,5},{5,7},{7,1},{8,10},{10,12},{12... | collective-permute-start | bytes 147464 | tf_op jit(solution)/shard_map/ppermute | solution.py:370
  49.1 3.9 %collective-permute-start.7 = (bf16[4,24,1024]{2,1,0:T(8,128)(2,1)S(1)}, bf16[4,24,1024]{2,1,0:T(8,128)(2,1)S(1)}, u32[]{:S(2)}, u32[]{:S(2)}) collective-permute-start(bf16[4,24,1024]{2,1,0:T(8,128)(2,1)S(1)} %pile.1.own), channel_id=1, source_target_pairs={{0,1},{1,0},{2,3},{3,2},{4,5},{5,4},{6,7},{7,6},{8,9},{9,8},{10,11... | collective-permute-start | bytes 589832 | tf_op jit(solution)/shard_map/ppermute | solution.py:401
  70.6 4.0 %copy-start.1 = (s32[8,48]{1,0:T(8,128)S(1)}, s32[8,48]{1,0:T(8,128)}, u32[]{:S(2)}) copy-start(s32[8,48]{1,0:T(8,128)} %par_ref.5) | copy-start | bytes 4612
  70.6 4.0 %copy-start.2 = (f32[2048]{0:T(1024)S(1)}, f32[2048]{0:T(1024)}, u32[]{:S(2)}) copy-start(f32[2048]{0:T(1024)} %param.22) | copy-start | bytes 24580
  70.6 4.0 %copy-start.3 = (s32[8,48]{1,0:T(8,128)S(1)}, s32[8,48]{1,0:T(8,128)}, u32[]{:S(2)}) copy-start(s32[8,48]{1,0:T(8,128)} %tok_ref.1) | copy-start | bytes 4612
  70.6 4.0 %collective-permute-start.8 = (bf16[4,4,96,256]{3,2,1,0:T(8,128)(2,1)S(1)}, bf16[4,4,96,256]{3,2,1,0:T(8,128)(2,1)S(1)}, u32[]{:S(2)}, u32[]{:S(2)}) collective-permute-start(bf16[4,4,96,256]{3,2,1,0:T(8,128)(2,1)S(1)} %bitcast.16), channel_id=1, source_target_pairs={{0,1},{1,0},{2,3},{3,2},{4,5},{5,4},{6,7},{7,6},{8,9},{9,8},{10,11... | collective-permute-start | bytes 2359304 | tf_op jit(solution)/shard_map/ppermute | solution.py:408

commit v11 on v10

--- a/solution.py
+++ b/solution.py
@@ -346,6 +346,21 @@
     )(info, mine, theirs, gain, toks, parents, lead, pltpu.with_memory_space_constraint(w, pltpu.HBM))
 
 
+def settle_kernel(stat_ref, out_ref):
+    tree = out_ref.shape[1]
+    stats = jnp.sum(stat_ref[...], axis=0)
+    out_ref[...] = stats[:, 64:64 + tree] - jnp.log(stats[:, :tree])
+
+
+def settle(stats, tree):
+    return pl.pallas_call(
+        settle_kernel,
+        out_shape=jax.ShapeDtypeStruct((stats.shape[1], tree), F32),
+        compiler_params=pltpu.CompilerParams(vmem_limit_bytes=2 * MB),
+        name="settle",
+    )(stats)
+
+
 def fetch_kernel(w_ref, after_ref, out_ref, sem):
     copy = pltpu.make_async_copy(w_ref.at[:, pl.ds(0, out_ref.shape[1])], out_ref, sem)
     copy.start()
@@ -408,8 +423,7 @@
     other = lax.ppermute(hid, "core", swap)
     scorer = fetch(vocab_weight, hid, 1536)
     hidden, stats = vocab(info, hid, other, norm_gain.reshape(1, -1), tree_tokens, parents, scorer, vocab_weight, shards)
-    stats = jnp.sum(lax.all_to_all(stats, ("z", "x", "core"), 0, 0), axis=0)
-    logprob = stats[:, 64:64 + tree] - jnp.log(stats[:, :tree])
+    logprob = settle(lax.all_to_all(stats, ("z", "x", "core"), 0, 0), tree)
     return hidden.reshape(reqs, tree, width), logprob
 
 

time: 92.7 us -> 92.8 us (level)
  no operation moved by 1% of the time
where the time goes in v11:
time: 92.8 us; the launch traced here: 92.3 us
  blocking collectives  27.4 us (30%)
  starting transfers between devices  23.3 us (25%)
  Pallas kernels  20.5 us (22%)
  waiting for transfers between devices  20.2 us (22%)
    all_to_all x1, blocking collectives, local(): hid = lax.all_to_all(hid, ('z', 'x'), 0, 0).reshape(nz, nx, -1, block)  16.7 us
    all_to_all x1, blocking collectives, local(): logprob = settle(lax.all_to_all(stats, ('z', 'x', 'core'), 0, 0), tree)  10.7 us
    all_to_all x1, waiting for transfers between devices, local(): part = lax.all_to_all(part, ('z', 'x'), 0, 0)  10.5 us
    pallas_call x2, Pallas kernels, attend_half(): pl.pallas_call(functools.partial(attend_kernel, window, add), out_shape=o...  9.59 us
    all_to_all x1, starting transfers between devices, local(): lax.all_to_all(w.reshape(shards, -1, block), ('z', 'x', 'core'), 0, 0)  8.14 us
    pallas_call x1, Pallas kernels, vocab(): pl.pallas_call(vocab_kernel, out_shape=(jax.ShapeDtypeStruct((tokens, wid...  6.16 us
    ppermute x6, starting transfers between devices, shifted(): return lax.ppermute(a, axis, [(i, (i + step) % n) for i in range(n)])  6.07 us
    ppermute x6, waiting for transfers between devices, shifted(): return lax.ppermute(a, axis, [(i, (i + step) % n) for i in range(n)])  4.35 us
  transfers between devices with their start and end apart: 11, of which 6 were waited for; matrix products, arithmetic and copies ran while one was open for 0% of the time, Pallas kernels for 8%

profile of v11, /device:TPU:1, one launch (start us, length us, event | category | flops | bytes accessed | tf_op | source)
XLA Modules:
  0.0 92.3 jit_solution(18114452947503264764)
XLA Ops:
  0.6 0.0 copy-start
  0.7 0.1 stack.35.info_ref
  0.8 5.0 %attend_theirs.1 = (bf16[16,200,128]{2,1,0:T(8,128)(2,1)}, bf16[4,4,2,16,256]{4,3,2,1,0:T(8,128)(2,1)}) custom-call(s32[8]{0:T(128)S(1)} %stack.35.info_ref, s32[8]{0:T(128)} %len_ref.3, s32[8,48]{1,0:T(8,128)} %par_ref.5, bf16[8,48,2048]{2,1,0:T(8,128)(2,1)} %q_ref.3, bf16[8,128,2048]{2,1,0:T(8,128)(2,1)} %k_ref.3, bf16[8,128,2048]{2,1,0:T(8,128)(2,1)} %v_ref.3, ...), custom_call_target="tpu_custom_call" | custom-call | tf_op jit(solution)/shard_map/attend_theirs/pallas_call | solution.py:162
  5.7 1.5 %collective-permute-start = (bf16[16,200,128]{2,1,0:T(8,128)(2,1)}, bf16[16,200,128]{2,1,0:T(8,128)(2,1)S(1)}, u32[]{:S(2)}, u32[]{:S(2)}) collective-permute-start(bf16[16,200,128]{2,1,0:T(8,128)(2,1)} %get-tuple-element.6), channel_id=1, source_target_pairs={{0,1},{1,0},{2,3},{3,2},{4,5},{5,4},{6,7},{7,6},{8,9},{9,8},{10,11... | collective-permute-start | bytes 2457608 | tf_op jit(solution)/shard_map/ppermute | solution.py:409
  7.2 8.1 %all-to-all-start.1 = ((bf16[32,16,256]{2,1,0:T(8,128)(2,1)}), bf16[32,16,256]{2,1,0:T(8,128)(2,1)S(1)}, u32[]{:S(2)}, u32[]{:S(2)}) async-start(bf16[32,16,256]{2,1,0:T(8,128)(2,1)} %bitcast.8), calls=%async_computation.1 | async-start | bytes 524288 | tf_op jit(solution)/shard_map/all_to_all | solution.py:410
  15.3 0.0 collective-permute-done.refs_0_
  15.4 4.6 %attend_mine.1 = bf16[16,200,128]{2,1,0:T(8,128)(2,1)} custom-call(s32[8]{0:T(128)S(1)} %stack.35.info_ref, s32[8]{0:T(128)} %len_ref.3, s32[8,48]{1,0:T(8,128)} %par_ref.5, bf16[8,48,2048]{2,1,0:T(8,128)(2,1)} %q_ref.3, bf16[8,128,2048]{2,1,0:T(8,128)(2,1)} %k_ref.3, bf16[8,128,2048]{2,1,0:T(8,128)(2,1)} %v_ref.3, bf16[8,48,2048]{2,1,0:T(8,128)(2,1)} %nk_ref.3, ...), custom_call_target="tpu_custom_call" | custom-call | tf_op jit(solution)/shard_map/attend_mine/pallas_call | solution.py:162
  20.0 4.3 %all-to-all-done.1 = bf16[32,16,256]{2,1,0:T(8,128)(2,1)S(1)} async-done(((bf16[32,16,256]{2,1,0:T(8,128)(2,1)}), bf16[32,16,256]{2,1,0:T(8,128)(2,1)S(1)}, u32[]{:S(2)}, u32[]{:S(2)}) %all-to-all-start.1) | async-done | bytes 262176 | tf_op jit(solution)/shard_map/all_to_all | solution.py:410
  24.2 3.6 %all-to-all-start = ((bf16[16,200,128]{2,1,0:T(8,128)(2,1)}), bf16[16,200,128]{2,1,0:T(8,128)(2,1)S(1)}, u32[]{:S(2)}, u32[]{:S(2)}) async-start(bf16[16,200,128]{2,1,0:T(8,128)(2,1)} %attend_mine.1), calls=%async_computation | async-start | bytes 1638400 | tf_op jit(solution)/shard_map/all_to_all | solution.py:413
  27.9 2.8 %collective-permute-start.6 = (bf16[512,256]{1,0:T(8,128)(2,1)S(1)}, bf16[512,256]{1,0:T(8,128)(2,1)S(1)}, u32[]{:S(2)}, u32[]{:S(2)}) collective-permute-start(bf16[512,256]{1,0:T(8,128)(2,1)S(1)} %bitcast.20), channel_id=1, source_target_pairs={{0,96},{32,0},{64,32},{96,64},{1,97},{33,1},{65,33},{97,65},{2,98}... | collective-permute-start | bytes 786440 | tf_op jit(solution)/shard_map/ppermute | solution.py:385
  30.7 0.4 collective-permute-start.5
  31.0 0.7 collective-permute-start.4
  31.7 10.5 %all-to-all-done.parts_ref = bf16[16,200,128]{2,1,0:T(8,128)(2,1)S(1)} async-done(((bf16[16,200,128]{2,1,0:T(8,128)(2,1)}), bf16[16,200,128]{2,1,0:T(8,128)(2,1)S(1)}, u32[]{:S(2)}, u32[]{:S(2)}) %all-to-all-start) | async-done | bytes 819232 | tf_op jit(solution)/shard_map/all_to_all | solution.py:413
  42.2 0.3 combine.1.refs_0_
  42.5 0.1 collective-permute-start.3
  42.6 2.0 %collective-permute-start.2 = (bf16[24,1024]{1,0:T(8,128)(2,1)S(1)}, bf16[24,1024]{1,0:T(8,128)(2,1)S(1)}, u32[]{:S(2)}, u32[]{:S(2)}) collective-permute-start(bf16[24,1024]{1,0:T(8,128)(2,1)S(1)} %combine.1.refs_0_), channel_id=1, source_target_pairs={{0,4},{2,6},{4,0},{6,2},{1,5},{3,7},{5,1},{7,3},{8,12},{10,14},{12... | collective-permute-start | bytes 147464 | tf_op jit(solution)/shard_map/ppermute | solution.py:385
  44.6 0.0 collective-permute-done.6.refs_7_.refs_3_
  44.6 0.1 collective-permute-start.1
  44.7 1.3 %collective-permute-done.4.refs_5_.refs_1_ = bf16[512,256]{1,0:T(8,128)(2,1)S(1)} collective-permute-done((bf16[512,256]{1,0:T(8,128)(2,1)S(1)}, bf16[512,256]{1,0:T(8,128)(2,1)S(1)}, u32[]{:S(2)}, u32[]{:S(2)}) %collective-permute-start.4) | collective-permute-done | bytes 262176 | tf_op jit(solution)/shard_map/ppermute | solution.py:385
  46.0 0.0 collective-permute-done.3.refs_3_
  46.0 1.1 %collective-permute-done.2.refs_2_ = bf16[24,1024]{1,0:T(8,128)(2,1)S(1)} collective-permute-done((bf16[24,1024]{1,0:T(8,128)(2,1)S(1)}, bf16[24,1024]{1,0:T(8,128)(2,1)S(1)}, u32[]{:S(2)}, u32[]{:S(2)}) %collective-permute-start.2) | collective-permute-done | bytes 49184 | tf_op jit(solution)/shard_map/ppermute | solution.py:385
  47.1 2.0 %collective-permute-done.1.refs_1_ = bf16[24,1024]{1,0:T(8,128)(2,1)S(1)} collective-permute-done((bf16[24,1024]{1,0:T(8,128)(2,1)S(1)}, bf16[24,1024]{1,0:T(8,128)(2,1)S(1)}, u32[]{:S(2)}, u32[]{:S(2)}) %collective-permute-start.1) | collective-permute-done | bytes 49184 | tf_op jit(solution)/shard_map/ppermute | solution.py:385
  49.1 2.8 %collective-permute-start.7 = (bf16[4,24,1024]{2,1,0:T(8,128)(2,1)S(1)}, bf16[4,24,1024]{2,1,0:T(8,128)(2,1)S(1)}, u32[]{:S(2)}, u32[]{:S(2)}) collective-permute-start(bf16[4,24,1024]{2,1,0:T(8,128)(2,1)S(1)} %pile.1.own), channel_id=1, source_target_pairs={{0,1},{1,0},{2,3},{3,2},{4,5},{5,4},{6,7},{7,6},{8,9},{9,8},{10,11... | collective-permute-start | bytes 589832 | tf_op jit(solution)/shard_map/ppermute | solution.py:416
  51.9 1.1 %collective-permute-done.7.other = bf16[4,24,1024]{2,1,0:T(8,128)(2,1)S(1)} collective-permute-done((bf16[4,24,1024]{2,1,0:T(8,128)(2,1)S(1)}, bf16[4,24,1024]{2,1,0:T(8,128)(2,1)S(1)}, u32[]{:S(2)}, u32[]{:S(2)}) %collective-permute-start.7) | collective-permute-done | bytes 196640 | tf_op jit(solution)/shard_map/ppermute | solution.py:416
  53.0 0.9 project.1
  53.9 16.7 %all_to_all.20 = bf16[16,96,256]{2,1,0:T(8,128)(2,1)S(1)} all-to-all(bf16[16,96,256]{2,1,0:T(8,128)(2,1)S(1)} %bitcast.19), channel_id=1, replica_groups=mesh['dp'=4,'z'=4,'x'=4,'core'=2] {'z','x'}, dimensions={0} | all-to-all | bytes 1572864 | tf_op jit(solution)/shard_map/all_to_all | solution.py:422
  70.6 1.2 %collective-permute-start.8 = (bf16[4,4,96,256]{3,2,1,0:T(8,128)(2,1)S(1)}, bf16[4,4,96,256]{3,2,1,0:T(8,128)(2,1)S(1)}, u32[]{:S(2)}, u32[]{:S(2)}) collective-permute-start(bf16[4,4,96,256]{3,2,1,0:T(8,128)(2,1)S(1)} %bitcast.16), channel_id=1, source_target_pairs={{0,1},{1,0},{2,3},{3,2},{4,5},{5,4},{6,7},{7,6},{8,9},{9,8},{10,11... | collective-permute-start | bytes 2359304 | tf_op jit(solution)/shard_map/ppermute | solution.py:423
  71.8 2.8 %fetch.1.w_ref = bf16[2048,1536]{1,0:T(8,128)(2,1)S(1)} custom-call(bf16[2048,2432]{1,0:T(8,128)(2,1)} %more_ref.1, bf16[4,4,96,256]{3,2,1,0:T(8,128)(2,1)S(1)} %bitcast.17), custom_call_target="tpu_custom_call" | custom-call | tf_op jit(solution)/shard_map/fetch/pallas_call | solution.py:372
  74.6 0.0 collective-permute-done.8.theirs_ref
  74.6 6.2 %vocab.1 = (bf16[384,2048]{1,0:T(8,128)(2,1)}, f32[32,8,128]{2,1,0:T(8,128)S(1)}) custom-call(s32[8]{0:T(128)S(1)} %stack.35.info_ref, bf16[4,4,96,256]{3,2,1,0:T(8,128)(2,1)S(1)} %bitcast.18, bf16[4,4,96,256]{3,2,1,0:T(8,128)(2,1)S(1)} %collective-permute-done.8.theirs_ref, f32[1,2048]{1,0:T(1,128)S(1)} %bitcast.25, s32[8,48]{1,0:T(8,128)S(1)} %copy-done.3, ...), custom_call_target="tpu_custom_call" | custom-call | tf_op jit(solution)/shard_map/vocab/pallas_call | solution.py:330
  80.8 10.7 %all_to_all.21.stat_ref = f32[32,8,128]{2,1,0:T(8,128)S(1)} all-to-all(f32[32,8,128]{2,1,0:T(8,128)S(1)} %get-tuple-element.9), channel_id=1, replica_groups=mesh['dp'=4,'z'=4,'x'=4,'core'=2] {'z','x','core'}, dimensions={0} | all-to-all | bytes 262144 | tf_op jit(solution)/shard_map/all_to_all | solution.py:426
  91.5 0.8 settle.1
  (10 shorter events, 0.0 us)
Async XLA Ops:
  0.6 51.3 %copy-start = (bf16[8,48,2048]{2,1,0:T(8,128)(2,1)S(1)}, bf16[8,48,2048]{2,1,0:T(8,128)(2,1)}, u32[]{:S(2)}) copy-start(bf16[8,48,2048]{2,1,0:T(8,128)(2,1)} %param.20) | copy-start | bytes 4718596
  5.7 9.6 %collective-permute-start = (bf16[16,200,128]{2,1,0:T(8,128)(2,1)}, bf16[16,200,128]{2,1,0:T(8,128)(2,1)S(1)}, u32[]{:S(2)}, u32[]{:S(2)}) collective-permute-start(bf16[16,200,128]{2,1,0:T(8,128)(2,1)} %get-tuple-element.6), channel_id=1, source_target_pairs={{0,1},{1,0},{2,3},{3,2},{4,5},{5,4},{6,7},{7,6},{8,9},{9,8},{10,11... | collective-permute-start | bytes 2457608 | tf_op jit(solution)/shard_map/ppermute | solution.py:409
  7.2 17.0 %all-to-all-start.1 = ((bf16[32,16,256]{2,1,0:T(8,128)(2,1)}), bf16[32,16,256]{2,1,0:T(8,128)(2,1)S(1)}, u32[]{:S(2)}, u32[]{:S(2)}) async-start(bf16[32,16,256]{2,1,0:T(8,128)(2,1)} %bitcast.8), calls=%async_computation.1 | async-start | bytes 524288 | tf_op jit(solution)/shard_map/all_to_all | solution.py:410
  24.2 18.0 %all-to-all-start = ((bf16[16,200,128]{2,1,0:T(8,128)(2,1)}), bf16[16,200,128]{2,1,0:T(8,128)(2,1)S(1)}, u32[]{:S(2)}, u32[]{:S(2)}) async-start(bf16[16,200,128]{2,1,0:T(8,128)(2,1)} %attend_mine.1), calls=%async_computation | async-start | bytes 1638400 | tf_op jit(solution)/shard_map/all_to_all | solution.py:413
  27.9 16.7 %collective-permute-start.6 = (bf16[512,256]{1,0:T(8,128)(2,1)S(1)}, bf16[512,256]{1,0:T(8,128)(2,1)S(1)}, u32[]{:S(2)}, u32[]{:S(2)}) collective-permute-start(bf16[512,256]{1,0:T(8,128)(2,1)S(1)} %bitcast.20), channel_id=1, source_target_pairs={{0,96},{32,0},{64,32},{96,64},{1,97},{33,1},{65,33},{97,65},{2,98}... | collective-permute-start | bytes 786440 | tf_op jit(solution)/shard_map/ppermute | solution.py:385
  30.7 14.1 %collective-permute-start.5 = (bf16[512,256]{1,0:T(8,128)(2,1)S(1)}, bf16[512,256]{1,0:T(8,128)(2,1)S(1)}, u32[]{:S(2)}, u32[]{:S(2)}) collective-permute-start(bf16[512,256]{1,0:T(8,128)(2,1)S(1)} %bitcast.21), channel_id=1, source_target_pairs={{0,64},{32,96},{64,0},{96,32},{1,65},{33,97},{65,1},{97,33},{2,66}... | collective-permute-start | bytes 786440 | tf_op jit(solution)/shard_map/ppermute | solution.py:385
  31.0 15.0 %collective-permute-start.4 = (bf16[512,256]{1,0:T(8,128)(2,1)S(1)}, bf16[512,256]{1,0:T(8,128)(2,1)S(1)}, u32[]{:S(2)}, u32[]{:S(2)}) collective-permute-start(bf16[512,256]{1,0:T(8,128)(2,1)S(1)} %bitcast.22), channel_id=1, source_target_pairs={{0,32},{32,64},{64,96},{96,0},{1,33},{33,65},{65,97},{97,1},{2,34}... | collective-permute-start | bytes 786440 | tf_op jit(solution)/shard_map/ppermute | solution.py:385
  42.5 3.5 %collective-permute-start.3 = (bf16[24,1024]{1,0:T(8,128)(2,1)S(1)}, bf16[24,1024]{1,0:T(8,128)(2,1)S(1)}, u32[]{:S(2)}, u32[]{:S(2)}) collective-permute-start(bf16[24,1024]{1,0:T(8,128)(2,1)S(1)} %combine.1.refs_0_), channel_id=1, source_target_pairs={{0,6},{2,0},{4,2},{6,4},{1,7},{3,1},{5,3},{7,5},{8,14},{10,8},{12,... | collective-permute-start | bytes 147464 | tf_op jit(solution)/shard_map/ppermute | solution.py:385
  42.6 4.5 %collective-permute-start.2 = (bf16[24,1024]{1,0:T(8,128)(2,1)S(1)}, bf16[24,1024]{1,0:T(8,128)(2,1)S(1)}, u32[]{:S(2)}, u32[]{:S(2)}) collective-permute-start(bf16[24,1024]{1,0:T(8,128)(2,1)S(1)} %combine.1.refs_0_), channel_id=1, source_target_pairs={{0,4},{2,6},{4,0},{6,2},{1,5},{3,7},{5,1},{7,3},{8,12},{10,14},{12... | collective-permute-start | bytes 147464 | tf_op jit(solution)/shard_map/ppermute | solution.py:385
  44.6 4.5 %collective-permute-start.1 = (bf16[24,1024]{1,0:T(8,128)(2,1)S(1)}, bf16[24,1024]{1,0:T(8,128)(2,1)S(1)}, u32[]{:S(2)}, u32[]{:S(2)}) collective-permute-start(bf16[24,1024]{1,0:T(8,128)(2,1)S(1)} %combine.1.refs_0_), channel_id=1, source_target_pairs={{0,2},{2,4},{4,6},{6,0},{1,3},{3,5},{5,7},{7,1},{8,10},{10,12},{12... | collective-permute-start | bytes 147464 | tf_op jit(solution)/shard_map/ppermute | solution.py:385
  49.1 3.9 %collective-permute-start.7 = (bf16[4,24,1024]{2,1,0:T(8,128)(2,1)S(1)}, bf16[4,24,1024]{2,1,0:T(8,128)(2,1)S(1)}, u32[]{:S(2)}, u32[]{:S(2)}) collective-permute-start(bf16[4,24,1024]{2,1,0:T(8,128)(2,1)S(1)} %pile.1.own), channel_id=1, source_target_pairs={{0,1},{1,0},{2,3},{3,2},{4,5},{5,4},{6,7},{7,6},{8,9},{9,8},{10,11... | collective-permute-start | bytes 589832 | tf_op jit(solution)/shard_map/ppermute | solution.py:416
  70.6 4.0 %copy-start.1 = (s32[8,48]{1,0:T(8,128)S(1)}, s32[8,48]{1,0:T(8,128)}, u32[]{:S(2)}) copy-start(s32[8,48]{1,0:T(8,128)} %par_ref.5) | copy-start | bytes 4612
  70.6 4.0 %copy-start.2 = (f32[2048]{0:T(1024)S(1)}, f32[2048]{0:T(1024)}, u32[]{:S(2)}) copy-start(f32[2048]{0:T(1024)} %param.22) | copy-start | bytes 24580
  70.6 4.0 %copy-start.3 = (s32[8,48]{1,0:T(8,128)S(1)}, s32[8,48]{1,0:T(8,128)}, u32[]{:S(2)}) copy-start(s32[8,48]{1,0:T(8,128)} %tok_ref.1) | copy-start | bytes 4612
  70.6 4.0 %collective-permute-start.8 = (bf16[4,4,96,256]{3,2,1,0:T(8,128)(2,1)S(1)}, bf16[4,4,96,256]{3,2,1,0:T(8,128)(2,1)S(1)}, u32[]{:S(2)}, u32[]{:S(2)}) collective-permute-start(bf16[4,4,96,256]{3,2,1,0:T(8,128)(2,1)S(1)} %bitcast.16), channel_id=1, source_target_pairs={{0,1},{1,0},{2,3},{3,2},{4,5},{5,4},{6,7},{7,6},{8,9},{9,8},{10,11... | collective-permute-start | bytes 2359304 | tf_op jit(solution)/shard_map/ppermute | solution.py:423
